TPU v7x, 32 devices: a whole 2x2x4 slice. The times are simulated.
32 devices in a mesh: member: 8 (over z, x), dp: 4 (over y, core).
Axes of the slice: x: 2, y: 2, z: 4, core: 2. Of those that a mesh axis runs over, the one named last changes fastest.
Arguments:
- feature_pool: bfloat16 [2048, 256], P('dp'), may hold values from -6 to 6
- labels: int32 [2048], P('dp'), may hold values from 0 to 9
- sample_rows: int32 [1024], P('dp'), may hold values from 0 to 511
- noise_variance: float32 [10], replicated, may hold values from 160 to 640
- first_weight: bfloat16 [16, 256, 2048], P('member', None, 'dp'), may hold values from -6 to 6
- middle_weight: bfloat16 [16, 2048, 2048], P('member', 'dp'), may hold values from -6 to 6
- last_weight: bfloat16 [16, 2048, 10], P('member', 'dp'), may hold values from -6 to 6
Outputs:
- new_first: bfloat16 [16, 256, 2048], P('member', None, 'dp')
- new_middle: bfloat16 [16, 2048, 2048], P('member', 'dp')
- new_last: bfloat16 [16, 2048, 10], P('member', 'dp')
Inputs may be any that keep to these rules, and one draw needn't show every extreme that they name: Sample i reads pool row (i // 256) * 512 + sample_rows[i]. `labels`: class index of each pool row.
All inputs are finite; a program needn't handle non-finite values.
Results may differ from a plain program's by a relative error of at most 0.013.
Values may be sent and summed in bfloat16 or wider, within the bound.
No kernel may reach another device: no remote copies, remote signals or barrier semaphores. Data moves between devices by JAX's collectives and lax.ppermute only.
A program may use at most 128 MiB of HBM per device.

v0:
```python
import jax
import jax.numpy as jnp
from jax import lax
from jax.sharding import PartitionSpec as P

F_IN = 256
H = 2048


precise = lax.Precision.HIGHEST


def update_piece(piece, mixing):
    ensemble = piece.shape[0]
    flat = piece.reshape(ensemble, -1)
    upper = mixing.astype(jnp.bfloat16)
    lower = (mixing - upper.astype(jnp.float32)).astype(jnp.bfloat16)
    stacked = jnp.concatenate([upper.T, lower.T], axis=0)
    both = jnp.dot(stacked, flat, preferred_element_type=jnp.float32)
    product = both[:ensemble] + both[ensemble:]
    column_total = jnp.sum(mixing, axis=0)
    average = jnp.sum(flat, axis=0, dtype=jnp.float32) / ensemble
    renewed = flat.astype(jnp.float32) + product - column_total[:, None] * average[None, :]
    return renewed.astype(jnp.bfloat16).reshape(piece.shape)


def on_device(
    feature_pool, labels, sample_rows, noise_variance, first_weight, middle_weight, last_weight
):
    local_count = sample_rows.shape[0]
    members_here = first_weight.shape[0]
    classes_total = noise_variance.shape[0]
    in_scale = F_IN ** (-0.5)
    hid_scale = H ** (-0.5)
    inputs = feature_pool[sample_rows]
    classes = labels[sample_rows]
    target = (classes[:, None] == jnp.arange(classes_total, dtype=jnp.int32)[None, :]).astype(
        jnp.float32
    )
    first_full, middle_full, last_full = (
        lax.all_gather(first_weight, "dp", axis=2, tiled=True),
        lax.all_gather(middle_weight, "dp", axis=1, tiled=True),
        lax.all_gather(last_weight, "dp", axis=1, tiled=True),
    )
    hidden_one = jnp.tanh(
        jnp.einsum("sf,jfh->jsh", inputs, first_full, preferred_element_type=jnp.float32) * in_scale
    ).astype(jnp.bfloat16)
    hidden_two = jnp.tanh(
        jnp.einsum("jsk,jkh->jsh", hidden_one, middle_full, preferred_element_type=jnp.float32)
        * hid_scale
    ).astype(jnp.bfloat16)
    outputs = (
        jnp.einsum("jsh,jhc->jsc", hidden_two, last_full, preferred_element_type=jnp.float32)
        * hid_scale
    )
    whiten = 1.0 / jnp.sqrt(noise_variance)
    scaled = (outputs * whiten).reshape(members_here, local_count * classes_total)
    observed = (target * whiten).reshape(local_count * classes_total)
    every_member = lax.all_gather(scaled, "member", axis=0, tiled=True)
    center = jnp.mean(every_member, axis=0)
    anomaly = every_member - center
    gram_part = jnp.dot(anomaly, anomaly.T, precision=precise)
    drive_part = jnp.dot(anomaly, observed - center, precision=precise)
    gram_matrix, drive = (
        lax.psum(gram_part.astype(jnp.bfloat16), "dp").astype(jnp.float32),
        lax.psum(drive_part.astype(jnp.bfloat16), "dp").astype(jnp.float32),
    )
    ensemble = gram_matrix.shape[0]
    system = gram_matrix + ensemble * jnp.eye(ensemble, dtype=jnp.float32)
    factor = jnp.linalg.cholesky(system)
    mixing = jax.scipy.linalg.cho_solve((factor, True), drive[:, None] - gram_matrix)
    grouped = (
        lax.all_to_all(first_weight, "member", split_axis=1, concat_axis=0, tiled=True),
        lax.all_to_all(middle_weight, "member", split_axis=1, concat_axis=0, tiled=True),
        lax.all_to_all(last_weight, "member", split_axis=1, concat_axis=0, tiled=True),
    )
    updated = (
        update_piece(grouped[0], mixing),
        update_piece(grouped[1], mixing),
        update_piece(grouped[2], mixing),
    )
    new_first, new_middle, new_last = (
        lax.all_to_all(updated[0], "member", split_axis=0, concat_axis=1, tiled=True),
        lax.all_to_all(updated[1], "member", split_axis=0, concat_axis=1, tiled=True),
        lax.all_to_all(updated[2], "member", split_axis=0, concat_axis=1, tiled=True),
    )
    return (new_first, new_middle, new_last)


def solution(mesh):
    in_specs = (
        P("dp", None),
        P("dp"),
        P("dp"),
        P(),
        P("member", None, "dp"),
        P("member", "dp", None),
        P("member", "dp", None),
    )
    out_specs = (P("member", None, "dp"), P("member", "dp", None), P("member", "dp", None))
    return jax.shard_map(
        on_device, mesh=mesh, in_specs=in_specs, out_specs=out_specs, check_vma=False
    )
```

profile of v0, /device:TPU:0, one launch (start us, length us, event | category | flops | bytes accessed | tf_op | source)
XLA Modules:
  0.0 349.3 jit_solution(2352689093779938661)
XLA Ops:
  7.2 0.7 all-gather.4.cloned.1.call-update
  8.0 0.7 all-gather.6.cloned.1.call-update
  8.9 1.0 reshape.116
  9.9 7.3 %all-to-all-start.4 = ((bf16[8,2,640]{2,1,0:T(2,128)(2,1)}), bf16[8,2,640]{2,1,0:T(2,128)(2,1)S(1)}, u32[]{:S(2)}, u32[]{:S(2)}) async-start(bf16[8,2,640]{2,1,0:T(2,128)(2,1)} %reshape.116), calls=%async_computation.4 | async-start | bytes 40960 | tf_op jit(solution)/shard_map/all_to_all | solution.py:75
  17.2 1.3 copy.40
  18.5 5.3 %all-to-all-done.4 = bf16[8,2,640]{2,1,0:T(2,128)(2,1)S(1)} async-done(((bf16[8,2,640]{2,1,0:T(2,128)(2,1)}), bf16[8,2,640]{2,1,0:T(2,128)(2,1)S(1)}, u32[]{:S(2)}, u32[]{:S(2)}) %all-to-all-start.4) | async-done | bytes 20512 | tf_op jit(solution)/shard_map/all_to_all | solution.py:75
  23.8 3.5 %all-to-all-start = ((bf16[2,256,512]{2,0,1:T(2,128)(2,1)}), bf16[2,256,512]{2,0,1:T(2,128)(2,1)S(1)}, u32[]{:S(2)}, u32[]{:S(2)}) async-start(bf16[2,256,512]{2,0,1:T(2,128)(2,1)} %copy.40), calls=%async_computation | async-start | bytes 1048576 | tf_op jit(solution)/shard_map/all_to_all | solution.py:73
  27.3 8.5 %copy.46 = bf16[2,512,2048]{2,0,1:T(2,128)(2,1)} copy(bf16[2,512,2048]{2,1,0:T(8,128)(2,1)} %param.12) | data formatting | bytes 8388608 | tf_op args[5]
  35.8 4.7 %all-to-all-done = bf16[2,256,512]{2,0,1:T(2,128)(2,1)S(1)} async-done(((bf16[2,256,512]{2,0,1:T(2,128)(2,1)}), bf16[2,256,512]{2,0,1:T(2,128)(2,1)S(1)}, u32[]{:S(2)}, u32[]{:S(2)}) %all-to-all-start) | async-done | bytes 524320 | tf_op jit(solution)/shard_map/all_to_all | solution.py:73
  40.5 4.6 %all-to-all-start.2 = ((bf16[2,512,2048]{2,0,1:T(2,128)(2,1)}), bf16[2,512,2048]{2,0,1:T(2,128)(2,1)}, u32[]{:S(2)}, u32[]{:S(2)}) async-start(bf16[2,512,2048]{2,0,1:T(2,128)(2,1)} %copy.46), calls=%async_computation.2 | async-start | bytes 8388608 | tf_op jit(solution)/shard_map/all_to_all | solution.py:74
  45.3 1.8 gather_fusion
  47.1 1.9 gather_fusion.1
  49.0 0.5 fusion.32
  49.8 6.5 %all_gather.14 = bf16[2,2048,10]{1,2,0:T(8,128)(2,1)S(1)} all-gather(bf16[2,512,10]{1,2,0:T(8,128)(2,1)S(1)} %copy.42), channel_id=1, replica_groups=mesh['member'=8,'dp'=4] {'dp'}, dimensions={1}, use_global_device_ids=true | all-gather | bytes 102400 | tf_op jit(solution)/shard_map/all_gather | solution.py:43
  56.2 0.5 reshape.117
  56.8 0.9 reshape.90
  58.4 0.6 copy.54
  59.1 77.7 %all-to-all-done.2 = bf16[2,512,2048]{2,0,1:T(2,128)(2,1)} async-done(((bf16[2,512,2048]{2,0,1:T(2,128)(2,1)}), bf16[2,512,2048]{2,0,1:T(2,128)(2,1)}, u32[]{:S(2)}, u32[]{:S(2)}) %all-to-all-start.2) | async-done | bytes 4194336 | tf_op jit(solution)/shard_map/all_to_all | solution.py:74
  136.8 4.1 %copy.47 = bf16[2,8,64,2048]{3,2,0,1:T(8,128)(2,1)S(1)} copy(bf16[2,8,64,2048]{3,0,2,1:T(2,128)(2,1)} %bitcast.12) | data formatting | bytes 8388608 | tf_op jit(solution)/shard_map/all_to_all | solution.py:74
  140.9 4.3 %copy.56 = bf16[2,8,64,2048]{3,1,2,0:T(8,128)(2,1)} copy(bf16[2,8,64,2048]{3,2,1,0:T(8,128)(2,1)S(1)} %bitcast.93) | data formatting | bytes 8388608
  145.2 4.2 %convert_reduce_fusion = f32[64,2048]{1,0:T(8,128)S(1)} fusion(bf16[2,8,64,2048]{3,0,2,1:T(2,128)(2,1)} %bitcast.12), kind=kLoop, calls=%fused_computation.6 | loop fusion | flops 4063232 | bytes 4718592 | tf_op jit(solution)/shard_map/reduce_sum | solution.py:22
  149.6 9.9 %tanh_convert_fusion = bf16[2,256,2048]{2,1,0:T(8,128)(2,1)S(1)} fusion(bf16[2,2048,2048]{2,1,0:T(8,128)(2,1)} %all-gather.6.cloned.1.call-done, bf16[2,256,2048]{2,1,0:T(8,128)(2,1)} %all-gather.4.cloned.1.call-done, bf16[256,256]{1,0:T(8,128)(2,1)S(1)} %copy-done.5), kind=kOutput, calls=%fused_computation.7 | convolution fusion | flops 4836032512 | bytes 21102592 | tf_op jit(solution)/shard_map/jsk,jkh->jsh/dot_general | solution.py:49
  159.6 1.3 convolution_multiply_fusion
  160.8 0.9 copy.43
  161.9 30.8 %all-gather = f32[8,2,2560]{2,1,0:T(2,128)S(1)} all-gather(f32[1,2,2560]{2,1,0:T(2,128)S(1)} %reshape.110), channel_id=1, replica_groups=mesh['member'=8,'dp'=4] {'member'}, dimensions={0}, use_global_device_ids=true | all-gather | bytes 184320 | tf_op jit(solution)/shard_map/all_gather | solution.py:59
  193.5 5.8 %all-reduce = (bf16[16,16]{1,0:T(8,128)(2,1)S(1)}, bf16[16]{0:T(256)(128)(2,1)S(1)}) all-reduce(bf16[16,16]{1,0:T(8,128)(2,1)S(1)} %convolution_convert_fusion, bf16[16]{0:T(256)(128)(2,1)S(1)} %fusion.4), channel_id=1, replica_groups=mesh['member'=8,'dp'=4] {'dp'}, use_global_device_ids=true, to_apply=%region_1.0 | all-reduce | flops 272 | bytes 1088 | tf_op jit(solution)/shard_map/psum | solution.py:65
  199.4 1.5 cholesky.16
  200.9 0.6 compare_reduce_fusion
  201.6 0.6 fusion.18
  202.2 1.2 custom-call.10
  203.8 1.0 fusion.28
  204.8 0.8 fusion.17
  205.6 0.5 reshape.91
  206.4 0.7 reshape.118
  207.1 3.7 %all-to-all-start.5 = ((bf16[8,2,640]{2,1,0:T(2,128)(2,1)}), bf16[8,2,640]{2,1,0:T(2,128)(2,1)S(1)}, u32[]{:S(2)}, u32[]{:S(2)}) async-start(bf16[8,2,640]{2,1,0:T(2,128)(2,1)} %reshape.118), calls=%async_computation.5 | async-start | bytes 40960 | tf_op jit(solution)/shard_map/all_to_all | solution.py:85
  210.8 0.5 fusion.30
  211.3 1.4 fusion.7
  213.0 7.0 %fusion.29 = f32[32,131072]{1,0:T(8,128)} fusion(bf16[16,131072]{1,0:T(8,128)(2,1)S(1)} %bitcast.91, bf16[16,16]{0,1:T(8,128)(2,1)S(1)} %get-tuple-element.11, bf16[16,16]{0,1:T(8,128)(2,1)S(1)} %get-tuple-element.8), kind=kOutput, calls=%fused_computation.61 | convolution fusion | flops 134219776 | bytes 20972544 | tf_op jit(solution)/shard_map/dot_general | solution.py:19
  220.0 0.9 copy.55
  221.0 6.0 %all-to-all-start.1 = ((bf16[16,32,512]{2,1,0:T(8,128)(2,1)}), bf16[16,32,512]{2,1,0:T(8,128)(2,1)S(1)}, u32[]{:S(2)}, u32[]{:S(2)}) async-start(bf16[16,32,512]{2,1,0:T(8,128)(2,1)} %bitcast.30), calls=%async_computation.1 | async-start | bytes 1048576 | tf_op jit(solution)/shard_map/all_to_all | solution.py:83
  227.0 7.8 %fusion.2 = bf16[16,131072]{1,0:T(8,128)(2,1)S(1)} fusion(f32[32,131072]{1,0:T(8,128)} %fusion.29, bf16[16,131072]{1,0:T(8,128)(2,1)} %bitcast.90, f32[131072]{0:T(1024)S(1)} %bitcast.102, f32[16]{0:T(128)S(1)} %get-tuple-element.7), kind=kLoop, calls=%fused_computation.5 | loop fusion | flops 12582912 | bytes 25690176 | tf_op jit(solution)/shard_map/convert_element_type | solution.py:24
  234.8 4.3 %copy.58 = bf16[2,8,64,2048]{3,2,1,0:T(8,128)(2,1)} copy(bf16[2,8,64,2048]{3,1,2,0:T(8,128)(2,1)S(1)} %bitcast.94) | data formatting | bytes 8388608
  239.1 1.8 all-to-all-done.1
  240.9 4.6 %all-to-all-start.3 = ((bf16[16,64,2048]{2,1,0:T(8,128)(2,1)}), bf16[16,64,2048]{2,1,0:T(8,128)(2,1)}, u32[]{:S(2)}, u32[]{:S(2)}) async-start(bf16[16,64,2048]{2,1,0:T(8,128)(2,1)} %bitcast.92), calls=%async_computation.3 | async-start | bytes 8388608 | tf_op jit(solution)/shard_map/all_to_all | solution.py:84
  245.6 0.7 all_to_all.92
  246.3 0.8 copy.45
  247.2 90.4 %all-to-all-done.3 = bf16[16,64,2048]{2,1,0:T(8,128)(2,1)} async-done(((bf16[16,64,2048]{2,1,0:T(8,128)(2,1)}), bf16[16,64,2048]{2,1,0:T(8,128)(2,1)}, u32[]{:S(2)}, u32[]{:S(2)}) %all-to-all-start.3) | async-done | bytes 4194336 | tf_op jit(solution)/shard_map/all_to_all | solution.py:84
  337.6 4.8 %copy.48 = bf16[8,2,64,2048]{3,2,0,1:T(8,128)(2,1)} copy(bf16[8,2,64,2048]{3,2,1,0:T(8,128)(2,1)} %bitcast.14) | data formatting | bytes 8388608 | tf_op jit(solution)/shard_map/all_to_all | solution.py:84
  (59 shorter events, 3.5 us)
Async XLA Ops:
  7.2 38.1 %copy-start = (bf16[512,256]{1,0:T(8,128)(2,1)S(1)}, bf16[512,256]{1,0:T(8,128)(2,1)}, u32[]{:S(2)}) copy-start(bf16[512,256]{1,0:T(8,128)(2,1)} %param.7) | copy-start | bytes 786436
  7.2 10.0 %copy-start.4 = (bf16[2,256,512]{2,1,0:T(8,128)(2,1)S(1)}, bf16[2,256,512]{2,1,0:T(8,128)(2,1)}, u32[]{:S(2)}) copy-start(bf16[2,256,512]{2,1,0:T(8,128)(2,1)} %param.11) | copy-start | bytes 1572868
  7.2 1.5 copy-start.6
  7.2 142.4 %all-gather.4.cloned.1.call-start = ((), (), s32[]{:S(2)}) async-start(), calls=%async_computation.6 | async-start | bytes 2621440 | tf_op jit(solution)/shard_map/all_gather | solution.py:41
  7.9 141.7 %all-gather.6.cloned.1.call-start = ((), (), s32[]{:S(2)}) async-start(), calls=%async_computation.7 | async-start | bytes 20971520 | tf_op jit(solution)/shard_map/all_gather | solution.py:42
  9.9 13.9 %all-to-all-start.4 = ((bf16[8,2,640]{2,1,0:T(2,128)(2,1)}), bf16[8,2,640]{2,1,0:T(2,128)(2,1)S(1)}, u32[]{:S(2)}, u32[]{:S(2)}) async-start(bf16[8,2,640]{2,1,0:T(2,128)(2,1)} %reshape.116), calls=%async_computation.4 | async-start | bytes 40960 | tf_op jit(solution)/shard_map/all_to_all | solution.py:75
  23.8 16.8 %all-to-all-start = ((bf16[2,256,512]{2,0,1:T(2,128)(2,1)}), bf16[2,256,512]{2,0,1:T(2,128)(2,1)S(1)}, u32[]{:S(2)}, u32[]{:S(2)}) async-start(bf16[2,256,512]{2,0,1:T(2,128)(2,1)} %copy.40), calls=%async_computation | async-start | bytes 1048576 | tf_op jit(solution)/shard_map/all_to_all | solution.py:73
  35.8 9.4 %copy-start.7 = (s32[256]{0:T(256)S(1)}, s32[256]{0:T(256)}, u32[]{:S(2)}) copy-start(s32[256]{0:T(256)} %param.9) | copy-start | bytes 3076
  35.8 11.2 %copy-start.2 = (s32[512]{0:T(512)S(1)}, s32[512]{0:T(512)}, u32[]{:S(2)}) copy-start(s32[512]{0:T(512)} %param.8) | copy-start | bytes 6148
  35.8 13.2 %copy-start.9 = (f32[10]{0:T(128)S(1)}, f32[10]{0:T(128)}, u32[]{:S(2)}) copy-start(f32[10]{0:T(128)} %param.10) | copy-start | bytes 124
  40.5 96.3 %all-to-all-start.2 = ((bf16[2,512,2048]{2,0,1:T(2,128)(2,1)}), bf16[2,512,2048]{2,0,1:T(2,128)(2,1)}, u32[]{:S(2)}, u32[]{:S(2)}) async-start(bf16[2,512,2048]{2,0,1:T(2,128)(2,1)} %copy.46), calls=%async_computation.2 | async-start | bytes 8388608 | tf_op jit(solution)/shard_map/all_to_all | solution.py:74
  145.2 4.4 %copy-start.5 = (bf16[256,256]{1,0:T(8,128)(2,1)S(1)}, bf16[256,256]{1,0:T(8,128)(2,1)}, u32[]{:S(2)}) copy-start(bf16[256,256]{1,0:T(8,128)(2,1)} %gather_fusion) | copy-start | bytes 393220
  149.6 10.0 %copy-start.8 = (f32[10]{0:T(128)S(1)}, f32[10]{0:T(128)}, u32[]{:S(2)}) copy-start(f32[10]{0:T(128)} %get-tuple-element.10) | copy-start | bytes 124
  207.1 13.9 %all-to-all-start.5 = ((bf16[8,2,640]{2,1,0:T(2,128)(2,1)}), bf16[8,2,640]{2,1,0:T(2,128)(2,1)S(1)}, u32[]{:S(2)}, u32[]{:S(2)}) async-start(bf16[8,2,640]{2,1,0:T(2,128)(2,1)} %reshape.118), calls=%async_computation.5 | async-start | bytes 40960 | tf_op jit(solution)/shard_map/all_to_all | solution.py:85
  210.8 2.2 copy-start.3
  221.0 20.0 %all-to-all-start.1 = ((bf16[16,32,512]{2,1,0:T(8,128)(2,1)}), bf16[16,32,512]{2,1,0:T(8,128)(2,1)S(1)}, u32[]{:S(2)}, u32[]{:S(2)}) async-start(bf16[16,32,512]{2,1,0:T(8,128)(2,1)} %bitcast.30), calls=%async_computation.1 | async-start | bytes 1048576 | tf_op jit(solution)/shard_map/all_to_all | solution.py:83
  240.9 96.7 %all-to-all-start.3 = ((bf16[16,64,2048]{2,1,0:T(8,128)(2,1)}), bf16[16,64,2048]{2,1,0:T(8,128)(2,1)}, u32[]{:S(2)}, u32[]{:S(2)}) async-start(bf16[16,64,2048]{2,1,0:T(8,128)(2,1)} %bitcast.92), calls=%async_computation.3 | async-start | bytes 8388608 | tf_op jit(solution)/shard_map/all_to_all | solution.py:84
  337.6 4.8 %copy-start.1 = (bf16[512,256]{1,0:T(8,128)(2,1)S(1)}, bf16[512,256]{1,0:T(8,128)(2,1)}, u32[]{:S(2)}) copy-start(bf16[512,256]{1,0:T(8,128)(2,1)} %param.7) | copy-start | bytes 786436
Sparse Core Ops, SparseCore 0:
  9.6 25.2 all-gather.3
  36.5 106.5 all-gather.5
where the time goes:
time: 350 us; the launch traced here: 349 us
  waiting for transfers between devices  181 us (52%)
  blocking collectives  43.1 us (12%)
  local copies, waits for them, and re-layouts  40.9 us (12%)
  starting transfers between devices  29.8 us (9%)
  matrix products  20.6 us (6%)
  other arithmetic  19.1 us (5%)
  between operations  14.4 us (4%)
    all_to_all x1, waiting for transfers between devices, on_device(): lax.all_to_all(updated[1], 'member', split_axis=0, concat_axis=1, tiled=T...  90.4 us
    all_to_all x1, waiting for transfers between devices, on_device(): lax.all_to_all(middle_weight, 'member', split_axis=1, concat_axis=0, tile...  77.7 us
    all_gather x1, blocking collectives, on_device(): every_member = lax.all_gather(scaled, 'member', axis=0, tiled=True)  30.8 us
    unnamed x36, local copies, waits for them, and re-layouts  23.7 us
    convert_element_type x3, other arithmetic, update_piece(): return renewed.astype(jnp.bfloat16).reshape(piece.shape)  10 us
    dot_general x1, matrix products, on_device(): jnp.einsum('jsk,jkh->jsh', hidden_one, middle_full, preferred_element_typ...  9.89 us
    dot_general x3, matrix products, update_piece(): both = jnp.dot(stacked, flat, preferred_element_type=jnp.float32)  8.53 us
    all_to_all x1, starting transfers between devices, on_device(): lax.all_to_all(last_weight, 'member', split_axis=1, concat_axis=0, tiled=...  7.28 us
  transfers between devices with their start and end apart: 8, of which 5 were waited for; matrix products, arithmetic and copies ran while one was open for 15% of the time, Pallas kernels for 0%

commit v1 on v0

v1 whole, which is shorter than its diff:
```python
import jax
import jax.numpy as jnp
from jax import lax
from jax.experimental import pallas as pl
from jax.experimental.pallas import tpu as pltpu
from jax.sharding import PartitionSpec as P


GROUP = 16
WIDEST = 256
precise = lax.Precision.HIGHEST


def swap(value, axis, size, k):
    return lax.ppermute(value, axis, [(i, i ^ k) for i in range(size)])


def bits_of(size):
    return [1 << b for b in range(size.bit_length() - 1)]


def gather_xor(value, axis, size, bits):
    stack, order = value[None], [0]
    for bit in bits:
        stack = jnp.concatenate([stack, swap(stack, axis, size, bit)], axis=0)
        order = order + [o ^ bit for o in order]
    return stack, order


def gather_members(value, size):
    have = [value]
    bits = bits_of(size)
    groups = [bits[:1]] + [bits[i : i + 2] for i in range(1, len(bits), 2)]
    for group in groups:
        stack = jnp.concatenate(have, axis=0)
        count = len(have)
        fresh = []
        for step in range(1, 1 << len(group)):
            k = step * group[0]
            got = swap(stack, "member", size, k)
            fresh += jnp.split(got, count, axis=0)
        have = have + fresh
    return have


def gather_blocks(place, array, reads, shapes, steps):
    counts = [len(read) for read in reads]

    def kernel(place_ref, *refs):
        ins, outs = refs[: sum(counts)], refs[sum(counts) :]
        at = 0
        for out, count in zip(outs, counts):
            left = 0
            for ref in ins[at : at + count]:
                value = ref[...]
                value = value.reshape([n for i, n in enumerate(value.shape) if i not in drop])
                out[..., left : left + value.shape[-1]] = value
                left += value.shape[-1]
            at += count

    drop, out_specs = shapes[0][2], [
        pl.BlockSpec(block, index) for (_, (block, index), _) in shapes
    ]
    flat = [pl.BlockSpec(block, index) for read in reads for block, index in read]
    return pl.pallas_call(
        kernel,
        grid_spec=pltpu.PrefetchScalarGridSpec(
            num_scalar_prefetch=1, grid=(steps,), in_specs=flat, out_specs=out_specs
        ),
        out_shape=[jax.ShapeDtypeStruct(shape, array.dtype) for (shape, _, _) in shapes],
    )(place, *[array] * len(flat))


def join_blocks(place, shape, pieces, start, into=None):
    members, count = len(pieces), pieces[0].shape[1]
    slots, columns = pieces[0].shape[0], pieces[0].shape[2]
    extra = [] if into is None else [into]

    def kernel(place_ref, *refs):
        out = refs[-1]
        for k in range(members):
            @pl.when(pl.program_id(0) == k)
            def _():
                out[:, 0] = refs[k][...]

    return pl.pallas_call(
        kernel,
        grid_spec=pltpu.PrefetchScalarGridSpec(
            num_scalar_prefetch=1,
            grid=(members,),
            in_specs=[pl.BlockSpec(p.shape, lambda i, place_ref: (0, 0, 0)) for p in pieces]
            + [pl.BlockSpec(memory_space=pl.ANY)] * len(extra),
            out_specs=pl.BlockSpec(
                (slots, 1, count, columns),
                lambda i, place_ref: (0, place_ref[0] ^ i, start // count, 0),
            ),
        ),
        out_shape=jax.ShapeDtypeStruct(shape, pieces[0].dtype),
        input_output_aliases={} if into is None else {1 + members: 0},
    )(place, *pieces, *extra)


def spread(matrix, rows):
    n = matrix.shape[0]
    wide = n * rows
    pick = (
        lax.broadcasted_iota(jnp.int32, (wide, n), 0) // rows
        == lax.broadcasted_iota(jnp.int32, (wide, n), 1)
    ).astype(jnp.bfloat16)
    tall = jnp.dot(pick, matrix, preferred_element_type=jnp.float32).astype(jnp.bfloat16)
    full = lax.dot_general(
        tall, pick, (((1,), (1,)), ((), ())), preferred_element_type=jnp.float32
    )
    same = (
        lax.broadcasted_iota(jnp.int32, (wide, wide), 0) % rows
        == lax.broadcasted_iota(jnp.int32, (wide, wide), 1) % rows
    )
    return jnp.where(same, full, 0.0).astype(jnp.bfloat16)


def update_pieces(weights, pieces, block):
    count = len(pieces)
    slots, rows, columns = pieces[0].shape
    wide = count * slots * GROUP

    def kernel(weights_ref, *refs):
        ins, outs = refs[:count], refs[count : 2 * count]
        upper_ref, lower_ref = refs[2 * count :]

        @pl.when(pl.program_id(0) == 0)
        def _():
            upper = weights_ref[...].astype(jnp.bfloat16)
            lower = (weights_ref[...] - upper.astype(jnp.float32)).astype(jnp.bfloat16)
            upper_ref[...] = spread(upper, GROUP)
            lower_ref[...] = spread(lower, GROUP)

        for first in range(0, rows, GROUP):
            data = jnp.concatenate(
                [ref[s, first : first + GROUP, :] for ref in ins for s in range(slots)], axis=0
            )
            total = jnp.dot(upper_ref[...], data, preferred_element_type=jnp.float32)
            total += jnp.dot(lower_ref[...], data, preferred_element_type=jnp.float32)
            total = total.astype(jnp.bfloat16)
            for i, ref in enumerate(outs):
                for s in range(slots):
                    at = (i * slots + s) * GROUP
                    ref[s, first : first + GROUP, :] = total[at : at + GROUP]

    spec = pl.BlockSpec((slots, rows, block), lambda i: (0, 0, i))
    return pl.pallas_call(
        kernel,
        grid=(columns // block,),
        in_specs=[pl.BlockSpec(weights.shape, lambda i: (0, 0))] + [spec] * count,
        out_specs=[spec] * count,
        out_shape=[jax.ShapeDtypeStruct(pieces[0].shape, pieces[0].dtype)] * count,
        scratch_shapes=[pltpu.VMEM((wide, wide), jnp.bfloat16)] * 2,
    )(weights, *pieces)


def layer_one(inputs, weights, scale):
    count, features, width = weights.shape
    rows = inputs.shape[0]

    def kernel(inputs_ref, weights_ref, out_ref):
        product = jnp.dot(inputs_ref[...], weights_ref[0], preferred_element_type=jnp.float32)
        out_ref[...] = jnp.tanh(product * scale).astype(jnp.bfloat16)

    return pl.pallas_call(
        kernel,
        grid=(count,),
        in_specs=[
            pl.BlockSpec((rows, features), lambda i: (0, 0)),
            pl.BlockSpec((1, features, width), lambda i: (i, 0, 0)),
        ],
        out_specs=pl.BlockSpec((rows, width), lambda i: (0, i)),
        out_shape=jax.ShapeDtypeStruct((rows, count * width), jnp.bfloat16),
        name="layer_one",
    )(inputs, weights)


def layers_after(hidden, pieces, last, scale, block):
    samples = hidden.shape[0]
    width, columns = pieces[0].shape
    classes = last.shape[0]
    count = len(pieces)

    def kernel(hidden_ref, last_ref, *refs):
        out_ref = refs[count]
        total = None
        for i in range(count):
            term = jnp.dot(
                hidden_ref[:, i * width : (i + 1) * width],
                refs[i][...],
                preferred_element_type=jnp.float32,
            )
            total = term if total is None else total + term
        hidden_two = jnp.tanh(total * scale).astype(jnp.bfloat16)
        out = lax.dot_general(
            last_ref[...], hidden_two, (((1,), (1,)), ((), ())),
            preferred_element_type=jnp.float32,
        )
        out_ref[...] = out * scale

    return pl.pallas_call(
        kernel,
        grid=(samples // block,),
        in_specs=[
            pl.BlockSpec((block, count * width), lambda i: (i, 0)),
            pl.BlockSpec((classes, columns), lambda i: (0, 0)),
        ]
        + [pl.BlockSpec((width, columns), lambda i: (0, 0))] * count,
        out_specs=pl.BlockSpec((classes, block), lambda i: (0, i)),
        out_shape=jax.ShapeDtypeStruct((classes, samples), jnp.float32),
        name="layers_after",
    )(hidden, last, *pieces)


def forward(inputs, first_weight, middle_weight, last_weight, size, place):
    slots, features, width = first_weight.shape
    parts = size // slots
    units = middle_weight.shape[2]
    here = lax.axis_index("dp")
    y = here // parts
    samples = inputs.shape[0]

    steps = 4
    tall = width // steps

    def column_block(d, e):
        dy, dc = d // parts, d % parts

        def index(i, place_ref):
            y, c = place_ref[1] // parts, place_ref[1] % parts
            return (y ^ dy, i, (y ^ dy ^ e) * parts + (c ^ dc))

        return (1, tall, width), index

    middle_out = gather_blocks(
        place, middle_weight,
        [[column_block(d, e) for e in range(slots)] for d in range(size)],
        [
            ((width, slots * width), ((tall, slots * width), lambda i, place_ref: (i, 0)), (0,))
            for _ in range(size)
        ],
        steps,
    )
    middle_at = [middle_out[0]] + [swap(middle_out[d], "dp", size, d) for d in range(1, size)]

    def slot_of(array, dy):
        return lax.dynamic_index_in_dim(array, y ^ dy, 0, keepdims=False)

    every_input, order = gather_xor(inputs, "dp", size, bits_of(size)[::-1])
    every_input = every_input.reshape(size * samples, features)
    first_mine = jnp.stack(
        [slot_of(first_weight, 0)]
        + [swap(slot_of(first_weight, dy), "dp", size, dy * parts) for dy in range(1, slots)]
    )
    first_all, first_order = gather_xor(first_mine, "dp", size, bits_of(parts))
    last_flipped = jnp.transpose(last_weight, (0, 2, 1))
    last_mine = jnp.concatenate(
        [slot_of(last_flipped, 0)]
        + [swap(slot_of(last_flipped, dy), "dp", size, dy * parts) for dy in range(1, slots)],
        axis=1,
    )
    hidden_one = layer_one(
        every_input, first_all.reshape(size, features, width), features ** (-0.5)
    )
    middle_order = [dy * parts + dc for dc in first_order for dy in range(slots)]
    outputs = layers_after(
        hidden_one, [middle_at[d] for d in middle_order], last_mine, units ** (-0.5), samples
    )
    received = [None] * size
    for spot, d in enumerate(order):
        block = outputs[:, spot * samples : (spot + 1) * samples]
        received[d] = block if d == 0 else swap(block, "dp", size, d)
    by_slot = jnp.stack(
        [sum(received[dy * parts + dc] for dc in range(parts)) for dy in range(slots)]
    )
    return jnp.stack(
        [lax.dynamic_index_in_dim(by_slot, y ^ s, 0, keepdims=False) for s in range(slots)]
    )


def mixing_of(every, observed, size):
    ensemble = every.shape[0]
    center = jnp.mean(every, axis=0)
    anomaly = (every - center).reshape(ensemble, -1)
    rest = (observed - center).reshape(1, -1)
    both = lax.dot_general(
        anomaly,
        jnp.concatenate([anomaly, rest], axis=0),
        (((1,), (1,)), ((), ())),
        precision=precise,
        preferred_element_type=jnp.float32,
    )
    for bit in bits_of(size):
        both = both + swap(both, "dp", size, bit)
    gram_matrix, drive = both[:, :ensemble], both[:, ensemble:]
    system = gram_matrix + ensemble * jnp.eye(ensemble, dtype=jnp.float32)
    factor = jnp.linalg.cholesky(system)
    return jax.scipy.linalg.cho_solve((factor, True), drive - gram_matrix)


def exchanged(pieces, members):
    out = [pieces[0]] + [None] * (members - 1)
    for k in far_first(members):
        out[k] = swap(pieces[k], "member", members, k)
    return out


def far_first(members):
    return list(range(members - 1, 0, -1))


def on_device(
    members, size,
    feature_pool, labels, sample_rows, noise_variance, first_weight, middle_weight, last_weight,
):
    slots = first_weight.shape[0]
    classes_total = noise_variance.shape[0]
    ensemble = members * slots
    here = lax.axis_index("member")
    place = jnp.stack([here, lax.axis_index("dp")]).astype(jnp.int32)
    whiten = 1.0 / jnp.sqrt(noise_variance)
    inputs = feature_pool[sample_rows]
    classes = labels[sample_rows]
    target = (
        classes[None, :] == jnp.arange(classes_total, dtype=jnp.int32)[:, None]
    ).astype(jnp.float32)
    observed = target * whiten[:, None]

    def blocks(array):
        return array.reshape((slots, members, array.shape[1] // members) + array.shape[2:])

    first_blocks, middle_blocks = blocks(first_weight), blocks(middle_weight)
    rows = middle_blocks.shape[2]
    fits = rows % GROUP == 0 and first_blocks.shape[2] % GROUP == 0 and ensemble * GROUP <= WIDEST
    scaled_of = lambda: (
        forward(inputs, first_weight, middle_weight, last_weight, size, place)
        * whiten[None, :, None]
    )
    if not fits:
        every = jnp.concatenate(gather_members(scaled_of(), members), axis=0)
        return plain_update(
            mixing_of(every, observed, size), members, first_weight, middle_weight, last_weight
        )

    last_flat = jnp.transpose(blocks(last_weight), (1, 0, 3, 2)).reshape(members, slots, -1)
    early = rows * 3 // 4 // GROUP * GROUP

    def cut(array, start, count, steps):
        columns = array.shape[3]
        wide = columns // steps

        def read(k):
            return (
                (slots, 1, count, wide),
                lambda i, place_ref: (0, place_ref[0] ^ k, start // count, i),
            )

        out = ((slots, count, columns), ((slots, count, wide), lambda i, place_ref: (0, 0, i)), (1,))
        return gather_blocks(
            place, array, [[read(k)] for k in range(members)], [out] * members, steps
        )

    middle_early = exchanged(cut(middle_blocks, 0, early, 4), members)
    late_cut = cut(middle_blocks, early, rows - early, 4)
    first_in = exchanged(cut(first_blocks, 0, first_blocks.shape[2], 1), members)
    last_in = exchanged(
        [lax.dynamic_index_in_dim(last_flat, here ^ k, 0, keepdims=False) for k in range(members)],
        members,
    )
    every = jnp.concatenate(gather_members(scaled_of(), members), axis=0)
    middle_late = exchanged(late_cut, members)

    mixing = mixing_of(every, observed, size)
    weights = (
        jnp.eye(ensemble, dtype=jnp.float32)
        + mixing
        - jnp.mean(mixing, axis=0, keepdims=True)
    ).T

    block = middle_weight.shape[2] // 4
    early_back = exchanged(update_pieces(weights, middle_early, block), members)
    first_back = exchanged(update_pieces(weights, first_in, first_weight.shape[2]), members)
    last_stack = jnp.concatenate(last_in, axis=0).astype(jnp.float32)
    last_new = jnp.dot(weights, last_stack, precision=precise).astype(jnp.bfloat16)
    last_back = exchanged(jnp.split(last_new, members, axis=0), members)
    late_back = exchanged(update_pieces(weights, middle_late, block), members)

    new_first = join_blocks(place, first_blocks.shape, first_back, 0)
    new_middle = join_blocks(place, middle_blocks.shape, early_back, 0)
    new_middle = join_blocks(place, middle_blocks.shape, late_back, early, new_middle)
    last_whole = jnp.zeros((members, slots, last_new.shape[1]), jnp.bfloat16)
    for k in range(members):
        last_whole = lax.dynamic_update_slice(last_whole, last_back[k][None], (here ^ k, 0, 0))
    new_last = last_whole.reshape(members, slots, classes_total, -1)
    new_last = jnp.transpose(new_last, (1, 0, 3, 2)).reshape(last_weight.shape)
    return (
        new_first.reshape(first_weight.shape),
        new_middle.reshape(middle_weight.shape),
        new_last,
    )


def plain_update(mixing, members, first_weight, middle_weight, last_weight):
    slots = first_weight.shape[0]
    ensemble = members * slots
    member = jnp.arange(ensemble, dtype=jnp.int32)
    spot = (member // slots ^ lax.axis_index("member")) * slots + member % slots
    mixing = mixing[spot][:, spot]
    weights = (
        jnp.eye(ensemble, dtype=jnp.float32)
        + mixing
        - jnp.mean(mixing, axis=0, keepdims=True)
    ).T
    upper = weights.astype(jnp.bfloat16)
    lower = (weights - upper.astype(jnp.float32)).astype(jnp.bfloat16)

    def renew(array):
        piece = lax.all_to_all(array, "member", split_axis=1, concat_axis=0, tiled=True)
        flat = piece.reshape(ensemble, -1)
        new = jnp.dot(upper, flat, preferred_element_type=jnp.float32)
        new += jnp.dot(lower, flat, preferred_element_type=jnp.float32)
        new = new.astype(jnp.bfloat16).reshape(piece.shape)
        return lax.all_to_all(new, "member", split_axis=0, concat_axis=1, tiled=True)

    return renew(first_weight), renew(middle_weight), renew(last_weight)


def solution(mesh):
    members, size = mesh.shape["member"], mesh.shape["dp"]
    in_specs = (
        P("dp", None),
        P("dp"),
        P("dp"),
        P(),
        P("member", None, "dp"),
        P("member", "dp", None),
        P("member", "dp", None),
    )
    out_specs = (P("member", None, "dp"), P("member", "dp", None), P("member", "dp", None))

    def step(*arrays):
        return on_device(members, size, *arrays)

    def run(*arrays):
        mapped = jax.shard_map(
            step, mesh=mesh, in_specs=in_specs, out_specs=out_specs, check_vma=False
        )
        return mapped(*arrays)

    return run
```

time: 350 us -> 393 us (1.12)
  the two profiles are of different devices: /device:TPU:0 before, /device:TPU:10 now
where the time goes in v1:
time: 393 us; the launch traced here: 392 us
  waiting for transfers between devices  200 us (51%)
  starting transfers between devices  112 us (28%)
  Pallas kernels  58.5 us (15%)
  local copies, waits for them, and re-layouts  10.1 us (3%)
  other arithmetic  8.9 us (2%)
    ppermute x73, waiting for transfers between devices, swap(): return lax.ppermute(value, axis, [(i, i ^ k) for i in range(size)])  200 us
    ppermute x73, starting transfers between devices, swap(): return lax.ppermute(value, axis, [(i, i ^ k) for i in range(size)])  112 us
    pallas_call x4, Pallas kernels, gather_blocks(): pl.pallas_call(kernel, grid_spec=pltpu.PrefetchScalarGridSpec(num_scalar_...  17.5 us
    pallas_call x3, Pallas kernels, join_blocks(): pl.pallas_call(kernel, grid_spec=pltpu.PrefetchScalarGridSpec(num_scalar_...  14.9 us
    pallas_call x3, Pallas kernels, update_pieces(): pl.pallas_call(kernel, grid=(columns // block,), in_specs=[pl.BlockSpec(w...  12.3 us
    pallas_call x1, Pallas kernels, layers_after(): pl.pallas_call(kernel, grid=(samples // block,), in_specs=[pl.BlockSpec((...  8.96 us
  transfers between devices with their start and end apart: 73, of which 31 were waited for; matrix products, arithmetic and copies ran while one was open for 4% of the time, Pallas kernels for 11%

profile of v1, /device:TPU:10, one launch (start us, length us, event | category | flops | bytes accessed | tf_op | source)
XLA Modules:
  0.0 391.7 jit_solution(3947842150392624277)
XLA Ops:
  4.0 5.6 %shard_map.94 = (bf16[512,1024]{1,0:T(8,128)(2,1)}, bf16[512,1024]{1,0:T(8,128)(2,1)}, bf16[512,1024]{1,0:T(8,128)(2,1)}, bf16[512,1024]{1,0:T(8,128)(2,1)}) custom-call(s32[2]{0:T(128)} %pad_add_fusion.place_ref, bf16[2,512,2048]{2,1,0:T(8,128)(2,1)} %refs_7_.1, bf16[2,512,2048]{2,1,0:T(8,128)(2,1)} %refs_7_.1, bf16[2,512,2048]{2,1,0:T(8,128)(2,1)} %refs_7_.1, ...), custom_call_target="tpu_custom_call" | custom-call | tf_op jit(solution)/shard_map/pallas_call | solution.py:65
  13.8 46.0 %collective-permute-done = bf16[1,256,256]{2,1,0:T(8,128)(2,1)S(1)} collective-permute-done((bf16[1,256,256]{2,1,0:T(8,128)(2,1)S(1)}, bf16[1,256,256]{2,1,0:T(8,128)(2,1)S(1)}, u32[]{:S(2)}, u32[]{:S(2)}) %collective-permute-start) | collective-permute-done | bytes 131104 | tf_op jit(solution)/shard_map/ppermute | solution.py:15
  60.3 3.2 collective-permute-done.4
  67.0 4.9 %layer_one.1.hidden_ref = bf16[1024,2048]{1,0:T(8,128)(2,1)} custom-call(bf16[1024,256]{1,0:T(8,128)(2,1)} %bitcast.137, bf16[4,256,512]{2,1,0:T(8,128)(2,1)} %bitcast.136), custom_call_target="tpu_custom_call" | custom-call | tf_op jit(solution)/shard_map/layer_one/pallas_call | solution.py:168
  73.3 9.0 %layers_after.1 = f32[10,1024]{1,0:T(8,128)} custom-call(bf16[1024,2048]{1,0:T(8,128)(2,1)} %layer_one.1.hidden_ref, bf16[10,1024]{1,0:T(8,128)(2,1)} %pad_maximum_fusion.4.last_ref, bf16[512,1024]{1,0:T(8,128)(2,1)} %get-tuple-element.55.refs_0_, bf16[512,1024]{1,0:T(8,128)(2,1)} %copy-done.2, bf16[512,1024]{1,0:T(8,128)(2,1)} %copy-done.3, ...), custom_call_target="tpu_custom_call" | custom-call | tf_op jit(solution)/shard_map/layers_after/pallas_call | solution.py:204
  94.2 2.6 collective-permute-start.13
  97.6 2.6 collective-permute-done.13
  105.4 2.6 collective-permute-start.63
  111.5 5.0 %shard_map.100 = (bf16[2,48,2048]{2,1,0:T(8,128)(2,1)}, bf16[2,48,2048]{2,1,0:T(8,128)(2,1)}, bf16[2,48,2048]{2,1,0:T(8,128)(2,1)}, bf16[2,48,2048]{2,1,0:T(8,12...) custom-call(s32[2]{0:T(128)} %pad_add_fusion.place_ref, ...), custom_call_target="tpu_custom_call" | custom-call | tf_op jit(solution)/shard_map/pallas_call | solution.py:65
  116.5 4.1 %shard_map.98 = (bf16[2,16,2048]{2,1,0:T(8,128)(2,1)}, bf16[2,16,2048]{2,1,0:T(8,128)(2,1)}, bf16[2,16,2048]{2,1,0:T(8,128)(2,1)}, bf16[2,16,2048]{2,1,0:T(8,128...) custom-call(s32[2]{0:T(128)} %pad_add_fusion.place_ref, ...), custom_call_target="tpu_custom_call" | custom-call | tf_op jit(solution)/shard_map/pallas_call | solution.py:65
  120.6 2.8 shard_map.95
  127.6 2.6 collective-permute-start.19
  135.1 2.8 collective-permute-start.47
  139.9 4.7 %collective-permute-done.19.refs_3_ = bf16[2,32,512]{2,1,0:T(8,128)(2,1)S(1)} collective-permute-done((bf16[2,32,512]{2,1,0:T(8,128)(2,1)}, bf16[2,32,512]{2,1,0:T(8,128)(2,1)S(1)}, u32[]{:S(2)}, u32[]{:S(2)}) %collective-permute-start.19) | collective-permute-done | bytes 65568 | tf_op jit(solution)/shard_map/ppermute | solution.py:15
  144.6 3.6 collective-permute-start.49
  151.4 2.7 collective-permute-done.47.refs_3_
  154.9 29.2 %collective-permute-done.48.refs_4_ = bf16[2,48,2048]{2,1,0:T(8,128)(2,1)S(1)} collective-permute-done((bf16[2,48,2048]{2,1,0:T(8,128)(2,1)}, bf16[2,48,2048]{2,1,0:T(8,128)(2,1)S(1)}, u32[]{:S(2)}, u32[]{:S(2)}) %collective-permute-start.48) | collective-permute-done | bytes 393248 | tf_op jit(solution)/shard_map/ppermute | solution.py:15
  184.1 3.3 collective-permute-start.20
  187.4 8.0 %collective-permute-done.49.refs_5_ = bf16[2,48,2048]{2,1,0:T(8,128)(2,1)S(1)} collective-permute-done((bf16[2,48,2048]{2,1,0:T(8,128)(2,1)}, bf16[2,48,2048]{2,1,0:T(8,128)(2,1)S(1)}, u32[]{:S(2)}, u32[]{:S(2)}) %collective-permute-start.49) | collective-permute-done | bytes 393248 | tf_op jit(solution)/shard_map/ppermute | solution.py:15
  195.3 4.2 %collective-permute-start.21 = (bf16[2,32,512]{2,1,0:T(8,128)(2,1)}, bf16[2,32,512]{2,1,0:T(8,128)(2,1)S(1)}, u32[]{:S(2)}, u32[]{:S(2)}) collective-permute-start(bf16[2,32,512]{2,1,0:T(8,128)(2,1)} %get-tuple-element.64), channel_id=1, source_target_pairs={{0,20},{4,16},{8,28},{12,24},{16,4},{20,0},{24,12},{28,8},{1,21},{... | collective-permute-start | bytes 196616 | tf_op jit(solution)/shard_map/ppermute | solution.py:15
  199.5 6.7 %collective-permute-done.50.refs_6_ = bf16[2,48,2048]{2,1,0:T(8,128)(2,1)S(1)} collective-permute-done((bf16[2,48,2048]{2,1,0:T(8,128)(2,1)}, bf16[2,48,2048]{2,1,0:T(8,128)(2,1)S(1)}, u32[]{:S(2)}, u32[]{:S(2)}) %collective-permute-start.50) | collective-permute-done | bytes 393248 | tf_op jit(solution)/shard_map/ppermute | solution.py:15
  208.2 5.8 %collective-permute-done.51.refs_7_ = bf16[2,48,2048]{2,1,0:T(8,128)(2,1)S(1)} collective-permute-done((bf16[2,48,2048]{2,1,0:T(8,128)(2,1)}, bf16[2,48,2048]{2,1,0:T(8,128)(2,1)S(1)}, u32[]{:S(2)}, u32[]{:S(2)}) %collective-permute-start.51) | collective-permute-done | bytes 393248 | tf_op jit(solution)/shard_map/ppermute | solution.py:15
  216.8 5.7 %shard_map.101 = (bf16[2,48,2048]{2,1,0:T(8,128)(2,1)}, bf16[2,48,2048]{2,1,0:T(8,128)(2,1)}, bf16[2,48,2048]{2,1,0:T(8,128)(2,1)}, bf16[2,48,2048]{2,1,0:T(8,12...) custom-call(f32[16,16]{1,0:T(8,128)} %fusion.8.weights_ref, ...), custom_call_target="tpu_custom_call" | custom-call | tf_op jit(solution)/shard_map/pallas_call | solution.py:150
  225.0 3.4 collective-permute-start.35
  228.5 2.5 shard_map.96
  234.8 2.8 collective-permute-start.53
  244.1 2.4 collective-permute-done.66
  247.7 2.4 collective-permute-done.67
  251.7 2.9 collective-permute-done.68
  256.4 2.7 collective-permute-done.69
  261.5 3.0 collective-permute-done.70
  265.6 2.5 collective-permute-done.71
  269.0 3.6 collective-permute-done.72
  272.6 5.3 %collective-permute-start.26 = (bf16[2,32,512]{2,1,0:T(8,128)(2,1)}, bf16[2,32,512]{2,1,0:T(8,128)(2,1)S(1)}, u32[]{:S(2)}, u32[]{:S(2)}) collective-permute-start(bf16[2,32,512]{2,1,0:T(8,128)(2,1)} %get-tuple-element.70), channel_id=1, source_target_pairs={{0,12},{4,8},{8,4},{12,0},{16,28},{20,24},{24,20},{28,16},{1,13},{... | collective-permute-start | bytes 196616 | tf_op jit(solution)/shard_map/ppermute | solution.py:15
  278.1 3.3 collective-permute-start.28
  282.5 4.1 %shard_map.99 = (bf16[2,16,2048]{2,1,0:T(8,128)(2,1)}, bf16[2,16,2048]{2,1,0:T(8,128)(2,1)}, bf16[2,16,2048]{2,1,0:T(8,128)(2,1)}, bf16[2,16,2048]{2,1,0:T(8,128...) custom-call(f32[16,16]{1,0:T(8,128)} %fusion.8.weights_ref, ...), custom_call_target="tpu_custom_call" | custom-call | tf_op jit(solution)/shard_map/pallas_call | solution.py:150
  287.9 3.1 collective-permute-start.39
  292.2 18.0 %collective-permute-done.30.refs_7_ = bf16[2,32,512]{2,1,0:T(8,128)(2,1)S(1)} collective-permute-done((bf16[2,32,512]{2,1,0:T(8,128)(2,1)}, bf16[2,32,512]{2,1,0:T(8,128)(2,1)S(1)}, u32[]{:S(2)}, u32[]{:S(2)}) %collective-permute-start.30) | collective-permute-done | bytes 65568 | tf_op jit(solution)/shard_map/ppermute | solution.py:15
  316.9 4.7 %collective-permute-done.54.refs_3_ = bf16[2,48,2048]{2,1,0:T(8,128)(2,1)S(1)} collective-permute-done((bf16[2,48,2048]{2,1,0:T(8,128)(2,1)}, bf16[2,48,2048]{2,1,0:T(8,128)(2,1)S(1)}, u32[]{:S(2)}, u32[]{:S(2)}) %collective-permute-start.54) | collective-permute-done | bytes 393248 | tf_op jit(solution)/shard_map/ppermute | solution.py:15
  321.6 22.5 %collective-permute-done.55.refs_4_ = bf16[2,48,2048]{2,1,0:T(8,128)(2,1)S(1)} collective-permute-done((bf16[2,48,2048]{2,1,0:T(8,128)(2,1)}, bf16[2,48,2048]{2,1,0:T(8,128)(2,1)S(1)}, u32[]{:S(2)}, u32[]{:S(2)}) %collective-permute-start.55) | collective-permute-done | bytes 393248 | tf_op jit(solution)/shard_map/ppermute | solution.py:15
  344.1 3.3 collective-permute-start.41
  347.4 6.6 %collective-permute-done.56.refs_5_ = bf16[2,48,2048]{2,1,0:T(8,128)(2,1)S(1)} collective-permute-done((bf16[2,48,2048]{2,1,0:T(8,128)(2,1)}, bf16[2,48,2048]{2,1,0:T(8,128)(2,1)S(1)}, u32[]{:S(2)}, u32[]{:S(2)}) %collective-permute-start.56) | collective-permute-done | bytes 393248 | tf_op jit(solution)/shard_map/ppermute | solution.py:15
  353.9 4.2 %collective-permute-start.42 = (bf16[2,16,2048]{2,1,0:T(8,128)(2,1)}, bf16[2,16,2048]{2,1,0:T(8,128)(2,1)}, u32[]{:S(2)}, u32[]{:S(2)}) collective-permute-start(bf16[2,16,2048]{2,1,0:T(8,128)(2,1)} %get-tuple-element.88), channel_id=1, source_target_pairs={{0,20},{4,16},{8,28},{12,24},{16,4},{20,0},{24,12},{28,8},{1,21},{... | collective-permute-start | bytes 393224 | tf_op jit(solution)/shard_map/ppermute | solution.py:15
  358.1 9.7 %collective-permute-done.57.refs_6_ = bf16[2,48,2048]{2,1,0:T(8,128)(2,1)S(1)} collective-permute-done((bf16[2,48,2048]{2,1,0:T(8,128)(2,1)}, bf16[2,48,2048]{2,1,0:T(8,128)(2,1)S(1)}, u32[]{:S(2)}, u32[]{:S(2)}) %collective-permute-start.57) | collective-permute-done | bytes 393248 | tf_op jit(solution)/shard_map/ppermute | solution.py:15
  369.0 3.6 collective-permute-done.58.refs_7_
  376.1 4.3 %shard_map.97 = bf16[2,8,32,512]{3,2,1,0:T(8,128)(2,1)} custom-call(s32[2]{0:T(128)} %pad_add_fusion.place_ref, bf16[2,32,512]{2,1,0:T(8,128)(2,1)} %get-tuple-element.67.refs_0_, bf16[2,32,512]{2,1,0:T(8,128)(2,1)} %copy-done.34, bf16[2,32,512]{2,1,0:T(8,128)(2,1)} %copy-done.35, bf16[2,32,512]{2,1,0:T(8,128)(2,1)} %copy-done.36, ...), custom_call_target="tpu_custom_call" | custom-call | tf_op jit(solution)/shard_map/pallas_call | solution.py:86
  380.5 5.8 %shard_map.102.refs_8_ = bf16[2,8,64,2048]{3,2,1,0:T(8,128)(2,1)} custom-call(s32[2]{0:T(128)} %pad_add_fusion.place_ref, bf16[2,48,2048]{2,1,0:T(8,128)(2,1)} %get-tuple-element.99.refs_0_, bf16[2,48,2048]{2,1,0:T(8,128)(2,1)} %copy-done.11, bf16[2,48,2048]{2,1,0:T(8,128)(2,1)} %copy-done.12, bf16[2,48,2048]{2,1,0:T(8,128)(2,1)} %copy-done.13, ...), custom_call_target="tpu_custom_call" | custom-call | tf_op jit(solution)/shard_map/pallas_call | solution.py:86
  386.9 4.8 %shard_map.103 = bf16[2,8,64,2048]{3,2,1,0:T(8,128)(2,1)} custom-call(s32[2]{0:T(128)} %pad_add_fusion.place_ref, bf16[2,16,2048]{2,1,0:T(8,128)(2,1)} %get-tuple-element.83.refs_0_, bf16[2,16,2048]{2,1,0:T(8,128)(2,1)} %copy-done.19, bf16[2,16,2048]{2,1,0:T(8,128)(2,1)} %copy-done.20, ...), custom_call_target="tpu_custom_call", output_to_operand_aliasing={{}: (9, {})} | custom-call | tf_op jit(solution)/shard_map/pallas_call | solution.py:86
  (291 shorter events, 91.3 us)
Async XLA Ops:
  1.8 11.8 %collective-permute-start.2 = (bf16[256,512]{1,0:T(8,128)(2,1)S(1)}, bf16[256,512]{1,0:T(8,128)(2,1)S(1)}, u32[]{:S(2)}, u32[]{:S(2)}) collective-permute-start(bf16[256,512]{1,0:T(8,128)(2,1)S(1)} %get-tuple-element.112), channel_id=1, source_target_pairs={{0,2},{1,3},{2,0},{3,1},{4,6},{5,7},{6,4},{7,5},{8,10},{9,11},{10,... | collective-permute-start | bytes 786440 | tf_op jit(solution)/shard_map/ppermute | solution.py:15
  9.6 62.3 %collective-permute-start.5 = (bf16[512,1024]{1,0:T(8,128)(2,1)}, bf16[512,1024]{1,0:T(8,128)(2,1)S(1)}, u32[]{:S(2)}, u32[]{:S(2)}) collective-permute-start(bf16[512,1024]{1,0:T(8,128)(2,1)} %get-tuple-element.56), channel_id=1, source_target_pairs={{0,2},{1,3},{2,0},{3,1},{4,6},{5,7},{6,4},{7,5},{8,10},{9,11},{10,... | collective-permute-start | bytes 3145736 | tf_op jit(solution)/shard_map/ppermute | solution.py:15
  10.2 61.7 %collective-permute-start.6 = (bf16[512,1024]{1,0:T(8,128)(2,1)}, bf16[512,1024]{1,0:T(8,128)(2,1)S(1)}, u32[]{:S(2)}, u32[]{:S(2)}) collective-permute-start(bf16[512,1024]{1,0:T(8,128)(2,1)} %get-tuple-element.57), channel_id=1, source_target_pairs={{0,1},{1,0},{2,3},{3,2},{4,5},{5,4},{6,7},{7,6},{8,9},{9,8},{10,11... | collective-permute-start | bytes 3145736 | tf_op jit(solution)/shard_map/ppermute | solution.py:15
  10.2 61.7 %collective-permute-start.7 = (bf16[512,1024]{1,0:T(8,128)(2,1)}, bf16[512,1024]{1,0:T(8,128)(2,1)}, u32[]{:S(2)}, u32[]{:S(2)}) collective-permute-start(bf16[512,1024]{1,0:T(8,128)(2,1)} %get-tuple-element.58), channel_id=1, source_target_pairs={{0,3},{1,2},{2,1},{3,0},{4,7},{5,6},{6,5},{7,4},{8,11},{9,10},{10,... | collective-permute-start | bytes 3145736 | tf_op jit(solution)/shard_map/ppermute | solution.py:15
  13.0 46.8 %collective-permute-start = (bf16[1,256,256]{2,1,0:T(8,128)(2,1)S(1)}, bf16[1,256,256]{2,1,0:T(8,128)(2,1)S(1)}, u32[]{:S(2)}, u32[]{:S(2)}) collective-permute-start(bf16[1,256,256]{2,1,0:T(8,128)(2,1)S(1)} %bitcast.138), channel_id=1, source_target_pairs={{0,2},{1,3},{2,0},{3,1},{4,6},{5,7},{6,4},{7,5},{8,10},{9,11},{10,... | collective-permute-start | bytes 393224 | tf_op jit(solution)/shard_map/ppermute | solution.py:15
  13.6 52.3 %collective-permute-start.3 = (bf16[1,2,256,512]{3,2,1,0:T(8,128)(2,1)S(1)}, bf16[1,2,256,512]{3,2,1,0:T(8,128)(2,1)S(1)}, u32[]{:S(2)}, u32[]{:S(2)}) collective-permute-start(bf16[1,2,256,512]{3,2,1,0:T(8,128)(2,1)S(1)} %maximum_bitcast_fusion), channel_id=1, source_target_pairs={{0,1},{1,0},{2,3},{3,2},{4,5},{5,4},{6,7},{7,6},{8,9},{9,8},{10,11... | collective-permute-start | bytes 1572872 | tf_op jit(solution)/shard_map/ppermute | solution.py:15
  88.4 17.0 %collective-permute-start.59 = (bf16[2,640]{1,0:T(2,128)(2,1)S(1)}, bf16[2,640]{1,0:T(2,128)(2,1)S(1)}, u32[]{:S(2)}, u32[]{:S(2)}) collective-permute-start(bf16[2,640]{1,0:T(2,128)(2,1)S(1)} %bitcast.169), channel_id=1, source_target_pairs={{0,4},{4,0},{8,12},{12,8},{16,20},{20,16},{24,28},{28,24},{1,5},{5... | collective-permute-start | bytes 7688 | tf_op jit(solution)/shard_map/ppermute | solution.py:15
  90.0 18.0 %collective-permute-start.60 = (bf16[2,640]{1,0:T(2,128)(2,1)S(1)}, bf16[2,640]{1,0:T(2,128)(2,1)S(1)}, u32[]{:S(2)}, u32[]{:S(2)}) collective-permute-start(bf16[2,640]{1,0:T(2,128)(2,1)S(1)} %bitcast.168), channel_id=1, source_target_pairs={{0,8},{4,12},{8,0},{12,4},{16,24},{20,28},{24,16},{28,20},{1,9},{5... | collective-permute-start | bytes 7688 | tf_op jit(solution)/shard_map/ppermute | solution.py:15
  104.1 19.3 %collective-permute-start.62 = (bf16[2,640]{1,0:T(2,128)(2,1)S(1)}, bf16[2,640]{1,0:T(2,128)(2,1)S(1)}, u32[]{:S(2)}, u32[]{:S(2)}) collective-permute-start(bf16[2,640]{1,0:T(2,128)(2,1)S(1)} %bitcast.173), channel_id=1, source_target_pairs={{0,16},{4,20},{8,24},{12,28},{16,0},{20,4},{24,8},{28,12},{1,17},{... | collective-permute-start | bytes 7688 | tf_op jit(solution)/shard_map/ppermute | solution.py:15
  105.4 19.6 %collective-permute-start.63 = (bf16[2,640]{1,0:T(2,128)(2,1)S(1)}, bf16[2,640]{1,0:T(2,128)(2,1)S(1)}, u32[]{:S(2)}, u32[]{:S(2)}) collective-permute-start(bf16[2,640]{1,0:T(2,128)(2,1)S(1)} %bitcast.172), channel_id=1, source_target_pairs={{0,20},{4,16},{8,28},{12,24},{16,4},{20,0},{24,12},{28,8},{1,21},{... | collective-permute-start | bytes 7688 | tf_op jit(solution)/shard_map/ppermute | solution.py:15
  108.0 18.5 %collective-permute-start.64 = (bf16[2,640]{1,0:T(2,128)(2,1)S(1)}, bf16[2,640]{1,0:T(2,128)(2,1)S(1)}, u32[]{:S(2)}, u32[]{:S(2)}) collective-permute-start(bf16[2,640]{1,0:T(2,128)(2,1)S(1)} %bitcast.171), channel_id=1, source_target_pairs={{0,24},{4,28},{8,16},{12,20},{16,8},{20,12},{24,0},{28,4},{1,25},{... | collective-permute-start | bytes 7688 | tf_op jit(solution)/shard_map/ppermute | solution.py:15
  108.6 18.8 %collective-permute-start.65 = (bf16[2,640]{1,0:T(2,128)(2,1)S(1)}, bf16[2,640]{1,0:T(2,128)(2,1)S(1)}, u32[]{:S(2)}, u32[]{:S(2)}) collective-permute-start(bf16[2,640]{1,0:T(2,128)(2,1)S(1)} %bitcast.170), channel_id=1, source_target_pairs={{0,28},{4,24},{8,20},{12,16},{16,12},{20,8},{24,4},{28,0},{1,29},{... | collective-permute-start | bytes 7688 | tf_op jit(solution)/shard_map/ppermute | solution.py:15
  110.0 17.6 %collective-permute-start.16 = (f32[16,17]{1,0:T(8,128)S(1)}, f32[16,17]{1,0:T(8,128)S(1)}, u32[]{:S(2)}, u32[]{:S(2)}) collective-permute-start(f32[16,17]{1,0:T(8,128)S(1)} %add.92), channel_id=1, source_target_pairs={{0,2},{1,3},{2,0},{3,1},{4,6},{5,7},{6,4},{7,5},{8,10},{9,11},{10,... | collective-permute-start | bytes 3272 | tf_op jit(solution)/shard_map/ppermute | solution.py:15
  123.4 24.8 %collective-permute-start.45 = (bf16[2,48,2048]{2,1,0:T(8,128)(2,1)S(1)}, bf16[2,48,2048]{2,1,0:T(8,128)(2,1)S(1)}, u32[]{:S(2)}, u32[]{:S(2)}) collective-permute-start(bf16[2,48,2048]{2,1,0:T(8,128)(2,1)S(1)} %copy-done.43), channel_id=1, source_target_pairs={{0,4},{4,0},{8,12},{12,8},{16,20},{20,16},{24,28},{28,24},{1,5},{5... | collective-permute-start | bytes 1179656 | tf_op jit(solution)/shard_map/ppermute | solution.py:15
  125.0 24.9 %collective-permute-start.46 = (bf16[2,48,2048]{2,1,0:T(8,128)(2,1)S(1)}, bf16[2,48,2048]{2,1,0:T(8,128)(2,1)S(1)}, u32[]{:S(2)}, u32[]{:S(2)}) collective-permute-start(bf16[2,48,2048]{2,1,0:T(8,128)(2,1)S(1)} %copy-done.42), channel_id=1, source_target_pairs={{0,8},{4,12},{8,0},{12,4},{16,24},{20,28},{24,16},{28,20},{1,9},{5... | collective-permute-start | bytes 1179656 | tf_op jit(solution)/shard_map/ppermute | solution.py:15
  127.4 10.4 %collective-permute-start.18 = (bf16[2,32,512]{2,1,0:T(8,128)(2,1)}, bf16[2,32,512]{2,1,0:T(8,128)(2,1)S(1)}, u32[]{:S(2)}, u32[]{:S(2)}) collective-permute-start(bf16[2,32,512]{2,1,0:T(8,128)(2,1)} %get-tuple-element.61), channel_id=1, source_target_pairs={{0,8},{4,12},{8,0},{12,4},{16,24},{20,28},{24,16},{28,20},{1,9},{5... | collective-permute-start | bytes 196616 | tf_op jit(solution)/shard_map/ppermute | solution.py:15
  127.6 17.0 %collective-permute-start.19 = (bf16[2,32,512]{2,1,0:T(8,128)(2,1)}, bf16[2,32,512]{2,1,0:T(8,128)(2,1)S(1)}, u32[]{:S(2)}, u32[]{:S(2)}) collective-permute-start(bf16[2,32,512]{2,1,0:T(8,128)(2,1)} %get-tuple-element.62), channel_id=1, source_target_pairs={{0,12},{4,8},{8,4},{12,0},{16,28},{20,24},{24,20},{28,16},{1,13},{... | collective-permute-start | bytes 196616 | tf_op jit(solution)/shard_map/ppermute | solution.py:15
  135.1 19.0 %collective-permute-start.47 = (bf16[2,48,2048]{2,1,0:T(8,128)(2,1)}, bf16[2,48,2048]{2,1,0:T(8,128)(2,1)S(1)}, u32[]{:S(2)}, u32[]{:S(2)}) collective-permute-start(bf16[2,48,2048]{2,1,0:T(8,128)(2,1)} %get-tuple-element.94), channel_id=1, source_target_pairs={{0,12},{4,8},{8,4},{12,0},{16,28},{20,24},{24,20},{28,16},{1,13},{... | collective-permute-start | bytes 1179656 | tf_op jit(solution)/shard_map/ppermute | solution.py:15
  137.9 46.2 %collective-permute-start.48 = (bf16[2,48,2048]{2,1,0:T(8,128)(2,1)}, bf16[2,48,2048]{2,1,0:T(8,128)(2,1)S(1)}, u32[]{:S(2)}, u32[]{:S(2)}) collective-permute-start(bf16[2,48,2048]{2,1,0:T(8,128)(2,1)} %get-tuple-element.95), channel_id=1, source_target_pairs={{0,16},{4,20},{8,24},{12,28},{16,0},{20,4},{24,8},{28,12},{1,17},{... | collective-permute-start | bytes 1179656 | tf_op jit(solution)/shard_map/ppermute | solution.py:15
  144.6 50.7 %collective-permute-start.49 = (bf16[2,48,2048]{2,1,0:T(8,128)(2,1)}, bf16[2,48,2048]{2,1,0:T(8,128)(2,1)S(1)}, u32[]{:S(2)}, u32[]{:S(2)}) collective-permute-start(bf16[2,48,2048]{2,1,0:T(8,128)(2,1)} %get-tuple-element.96), channel_id=1, source_target_pairs={{0,20},{4,16},{8,28},{12,24},{16,4},{20,0},{24,12},{28,8},{1,21},{... | collective-permute-start | bytes 1179656 | tf_op jit(solution)/shard_map/ppermute | solution.py:15
  148.2 58.0 %collective-permute-start.50 = (bf16[2,48,2048]{2,1,0:T(8,128)(2,1)}, bf16[2,48,2048]{2,1,0:T(8,128)(2,1)S(1)}, u32[]{:S(2)}, u32[]{:S(2)}) collective-permute-start(bf16[2,48,2048]{2,1,0:T(8,128)(2,1)} %get-tuple-element.97), channel_id=1, source_target_pairs={{0,24},{4,28},{8,16},{12,20},{16,8},{20,12},{24,0},{28,4},{1,25},{... | collective-permute-start | bytes 1179656 | tf_op jit(solution)/shard_map/ppermute | solution.py:15
  149.8 64.2 %collective-permute-start.51 = (bf16[2,48,2048]{2,1,0:T(8,128)(2,1)}, bf16[2,48,2048]{2,1,0:T(8,128)(2,1)S(1)}, u32[]{:S(2)}, u32[]{:S(2)}) collective-permute-start(bf16[2,48,2048]{2,1,0:T(8,128)(2,1)} %get-tuple-element.98), channel_id=1, source_target_pairs={{0,28},{4,24},{8,20},{12,16},{16,12},{20,8},{24,4},{28,0},{1,29},{... | collective-permute-start | bytes 1179656 | tf_op jit(solution)/shard_map/ppermute | solution.py:15
  154.1 76.9 %collective-permute-start.31 = (bf16[2,16,2048]{2,1,0:T(8,128)(2,1)}, bf16[2,16,2048]{2,1,0:T(8,128)(2,1)S(1)}, u32[]{:S(2)}, u32[]{:S(2)}) collective-permute-start(bf16[2,16,2048]{2,1,0:T(8,128)(2,1)} %get-tuple-element.76), channel_id=1, source_target_pairs={{0,4},{4,0},{8,12},{12,8},{16,20},{20,16},{24,28},{28,24},{1,5},{5... | collective-permute-start | bytes 393224 | tf_op jit(solution)/shard_map/ppermute | solution.py:15
  184.1 38.4 %collective-permute-start.20 = (bf16[2,32,512]{2,1,0:T(8,128)(2,1)}, bf16[2,32,512]{2,1,0:T(8,128)(2,1)S(1)}, u32[]{:S(2)}, u32[]{:S(2)}) collective-permute-start(bf16[2,32,512]{2,1,0:T(8,128)(2,1)} %get-tuple-element.63), channel_id=1, source_target_pairs={{0,16},{4,20},{8,24},{12,28},{16,0},{20,4},{24,8},{28,12},{1,17},{... | collective-permute-start | bytes 196616 | tf_op jit(solution)/shard_map/ppermute | solution.py:15
  195.3 27.3 %collective-permute-start.21 = (bf16[2,32,512]{2,1,0:T(8,128)(2,1)}, bf16[2,32,512]{2,1,0:T(8,128)(2,1)S(1)}, u32[]{:S(2)}, u32[]{:S(2)}) collective-permute-start(bf16[2,32,512]{2,1,0:T(8,128)(2,1)} %get-tuple-element.64), channel_id=1, source_target_pairs={{0,20},{4,16},{8,28},{12,24},{16,4},{20,0},{24,12},{28,8},{1,21},{... | collective-permute-start | bytes 196616 | tf_op jit(solution)/shard_map/ppermute | solution.py:15
  206.2 18.4 %collective-permute-start.22 = (bf16[2,32,512]{2,1,0:T(8,128)(2,1)}, bf16[2,32,512]{2,1,0:T(8,128)(2,1)}, u32[]{:S(2)}, u32[]{:S(2)}) collective-permute-start(bf16[2,32,512]{2,1,0:T(8,128)(2,1)} %get-tuple-element.65), channel_id=1, source_target_pairs={{0,24},{4,28},{8,16},{12,20},{16,8},{20,12},{24,0},{28,4},{1,25},{... | collective-permute-start | bytes 196616 | tf_op jit(solution)/shard_map/ppermute | solution.py:15
  214.0 11.0 %collective-permute-start.23 = (bf16[2,32,512]{2,1,0:T(8,128)(2,1)}, bf16[2,32,512]{2,1,0:T(8,128)(2,1)}, u32[]{:S(2)}, u32[]{:S(2)}) collective-permute-start(bf16[2,32,512]{2,1,0:T(8,128)(2,1)} %get-tuple-element.66), channel_id=1, source_target_pairs={{0,28},{4,24},{8,20},{12,16},{16,12},{20,8},{24,4},{28,0},{1,29},{... | collective-permute-start | bytes 196616 | tf_op jit(solution)/shard_map/ppermute | solution.py:15
  222.6 10.8 %collective-permute-start.33 = (bf16[2,16,2048]{2,1,0:T(8,128)(2,1)}, bf16[2,16,2048]{2,1,0:T(8,128)(2,1)S(1)}, u32[]{:S(2)}, u32[]{:S(2)}) collective-permute-start(bf16[2,16,2048]{2,1,0:T(8,128)(2,1)} %get-tuple-element.78), channel_id=1, source_target_pairs={{0,12},{4,8},{8,4},{12,0},{16,28},{20,24},{24,20},{28,16},{1,13},{... | collective-permute-start | bytes 393224 | tf_op jit(solution)/shard_map/ppermute | solution.py:15
  224.7 10.2 %collective-permute-start.34 = (bf16[2,16,2048]{2,1,0:T(8,128)(2,1)}, bf16[2,16,2048]{2,1,0:T(8,128)(2,1)S(1)}, u32[]{:S(2)}, u32[]{:S(2)}) collective-permute-start(bf16[2,16,2048]{2,1,0:T(8,128)(2,1)} %get-tuple-element.79), channel_id=1, source_target_pairs={{0,16},{4,20},{8,24},{12,28},{16,0},{20,4},{24,8},{28,12},{1,17},{... | collective-permute-start | bytes 393224 | tf_op jit(solution)/shard_map/ppermute | solution.py:15
  225.0 12.7 %collective-permute-start.35 = (bf16[2,16,2048]{2,1,0:T(8,128)(2,1)}, bf16[2,16,2048]{2,1,0:T(8,128)(2,1)S(1)}, u32[]{:S(2)}, u32[]{:S(2)}) collective-permute-start(bf16[2,16,2048]{2,1,0:T(8,128)(2,1)} %get-tuple-element.80), channel_id=1, source_target_pairs={{0,20},{4,16},{8,28},{12,24},{16,4},{20,0},{24,12},{28,8},{1,21},{... | collective-permute-start | bytes 393224 | tf_op jit(solution)/shard_map/ppermute | solution.py:15
  231.8 11.1 %collective-permute-start.37 = (bf16[2,16,2048]{2,1,0:T(8,128)(2,1)}, bf16[2,16,2048]{2,1,0:T(8,128)(2,1)S(1)}, u32[]{:S(2)}, u32[]{:S(2)}) collective-permute-start(bf16[2,16,2048]{2,1,0:T(8,128)(2,1)} %get-tuple-element.82), channel_id=1, source_target_pairs={{0,28},{4,24},{8,20},{12,16},{16,12},{20,8},{24,4},{28,0},{1,29},{... | collective-permute-start | bytes 393224 | tf_op jit(solution)/shard_map/ppermute | solution.py:15
  233.4 81.8 %collective-permute-start.52 = (bf16[2,48,2048]{2,1,0:T(8,128)(2,1)}, bf16[2,48,2048]{2,1,0:T(8,128)(2,1)S(1)}, u32[]{:S(2)}, u32[]{:S(2)}) collective-permute-start(bf16[2,48,2048]{2,1,0:T(8,128)(2,1)} %get-tuple-element.100), channel_id=1, source_target_pairs={{0,4},{4,0},{8,12},{12,8},{16,20},{20,16},{24,28},{28,24},{1,5},{5... | collective-permute-start | bytes 1179656 | tf_op jit(solution)/shard_map/ppermute | solution.py:15
  234.8 81.0 %collective-permute-start.53 = (bf16[2,48,2048]{2,1,0:T(8,128)(2,1)}, bf16[2,48,2048]{2,1,0:T(8,128)(2,1)S(1)}, u32[]{:S(2)}, u32[]{:S(2)}) collective-permute-start(bf16[2,48,2048]{2,1,0:T(8,128)(2,1)} %get-tuple-element.101), channel_id=1, source_target_pairs={{0,8},{4,12},{8,0},{12,4},{16,24},{20,28},{24,16},{28,20},{1,9},{5... | collective-permute-start | bytes 1179656 | tf_op jit(solution)/shard_map/ppermute | solution.py:15
  237.7 40.2 %collective-permute-start.24 = (bf16[2,32,512]{2,1,0:T(8,128)(2,1)}, bf16[2,32,512]{2,1,0:T(8,128)(2,1)S(1)}, u32[]{:S(2)}, u32[]{:S(2)}) collective-permute-start(bf16[2,32,512]{2,1,0:T(8,128)(2,1)} %get-tuple-element.68), channel_id=1, source_target_pairs={{0,4},{4,0},{8,12},{12,8},{16,20},{20,16},{24,28},{28,24},{1,5},{5... | collective-permute-start | bytes 196616 | tf_op jit(solution)/shard_map/ppermute | solution.py:15
  239.3 38.8 %collective-permute-start.25 = (bf16[2,32,512]{2,1,0:T(8,128)(2,1)}, bf16[2,32,512]{2,1,0:T(8,128)(2,1)S(1)}, u32[]{:S(2)}, u32[]{:S(2)}) collective-permute-start(bf16[2,32,512]{2,1,0:T(8,128)(2,1)} %get-tuple-element.69), channel_id=1, source_target_pairs={{0,8},{4,12},{8,0},{12,4},{16,24},{20,28},{24,16},{28,20},{1,9},{5... | collective-permute-start | bytes 196616 | tf_op jit(solution)/shard_map/ppermute | solution.py:15
  286.6 24.2 %collective-permute-start.38 = (bf16[2,16,2048]{2,1,0:T(8,128)(2,1)}, bf16[2,16,2048]{2,1,0:T(8,128)(2,1)S(1)}, u32[]{:S(2)}, u32[]{:S(2)}) collective-permute-start(bf16[2,16,2048]{2,1,0:T(8,128)(2,1)} %get-tuple-element.84), channel_id=1, source_target_pairs={{0,4},{4,0},{8,12},{12,8},{16,20},{20,16},{24,28},{28,24},{1,5},{5... | collective-permute-start | bytes 393224 | tf_op jit(solution)/shard_map/ppermute | solution.py:15
  287.9 25.4 %collective-permute-start.39 = (bf16[2,16,2048]{2,1,0:T(8,128)(2,1)}, bf16[2,16,2048]{2,1,0:T(8,128)(2,1)S(1)}, u32[]{:S(2)}, u32[]{:S(2)}) collective-permute-start(bf16[2,16,2048]{2,1,0:T(8,128)(2,1)} %get-tuple-element.85), channel_id=1, source_target_pairs={{0,8},{4,12},{8,0},{12,4},{16,24},{20,28},{24,16},{28,20},{1,9},{5... | collective-permute-start | bytes 393224 | tf_op jit(solution)/shard_map/ppermute | solution.py:15
  291.0 19.2 %collective-permute-start.30 = (bf16[2,32,512]{2,1,0:T(8,128)(2,1)}, bf16[2,32,512]{2,1,0:T(8,128)(2,1)S(1)}, u32[]{:S(2)}, u32[]{:S(2)}) collective-permute-start(bf16[2,32,512]{2,1,0:T(8,128)(2,1)} %get-tuple-element.74), channel_id=1, source_target_pairs={{0,28},{4,24},{8,20},{12,16},{16,12},{20,8},{24,4},{28,0},{1,29},{... | collective-permute-start | bytes 196616 | tf_op jit(solution)/shard_map/ppermute | solution.py:15
  310.8 10.8 %collective-permute-start.54 = (bf16[2,48,2048]{2,1,0:T(8,128)(2,1)}, bf16[2,48,2048]{2,1,0:T(8,128)(2,1)S(1)}, u32[]{:S(2)}, u32[]{:S(2)}) collective-permute-start(bf16[2,48,2048]{2,1,0:T(8,128)(2,1)} %get-tuple-element.102), channel_id=1, source_target_pairs={{0,12},{4,8},{8,4},{12,0},{16,28},{20,24},{24,20},{28,16},{1,13},{... | collective-permute-start | bytes 1179656 | tf_op jit(solution)/shard_map/ppermute | solution.py:15
  310.8 33.3 %collective-permute-start.55 = (bf16[2,48,2048]{2,1,0:T(8,128)(2,1)}, bf16[2,48,2048]{2,1,0:T(8,128)(2,1)S(1)}, u32[]{:S(2)}, u32[]{:S(2)}) collective-permute-start(bf16[2,48,2048]{2,1,0:T(8,128)(2,1)} %get-tuple-element.103), channel_id=1, source_target_pairs={{0,16},{4,20},{8,24},{12,28},{16,0},{20,4},{24,8},{28,12},{1,17},{... | collective-permute-start | bytes 1179656 | tf_op jit(solution)/shard_map/ppermute | solution.py:15
  313.3 40.7 %collective-permute-start.56 = (bf16[2,48,2048]{2,1,0:T(8,128)(2,1)}, bf16[2,48,2048]{2,1,0:T(8,128)(2,1)S(1)}, u32[]{:S(2)}, u32[]{:S(2)}) collective-permute-start(bf16[2,48,2048]{2,1,0:T(8,128)(2,1)} %get-tuple-element.104), channel_id=1, source_target_pairs={{0,20},{4,16},{8,28},{12,24},{16,4},{20,0},{24,12},{28,8},{1,21},{... | collective-permute-start | bytes 1179656 | tf_op jit(solution)/shard_map/ppermute | solution.py:15
  315.2 52.5 %collective-permute-start.57 = (bf16[2,48,2048]{2,1,0:T(8,128)(2,1)}, bf16[2,48,2048]{2,1,0:T(8,128)(2,1)S(1)}, u32[]{:S(2)}, u32[]{:S(2)}) collective-permute-start(bf16[2,48,2048]{2,1,0:T(8,128)(2,1)} %get-tuple-element.105), channel_id=1, source_target_pairs={{0,24},{4,28},{8,16},{12,20},{16,8},{20,12},{24,0},{28,4},{1,25},{... | collective-permute-start | bytes 1179656 | tf_op jit(solution)/shard_map/ppermute | solution.py:15
  315.8 56.7 %collective-permute-start.58 = (bf16[2,48,2048]{2,1,0:T(8,128)(2,1)}, bf16[2,48,2048]{2,1,0:T(8,128)(2,1)S(1)}, u32[]{:S(2)}, u32[]{:S(2)}) collective-permute-start(bf16[2,48,2048]{2,1,0:T(8,128)(2,1)} %get-tuple-element.106), channel_id=1, source_target_pairs={{0,28},{4,24},{8,20},{12,16},{16,12},{20,8},{24,4},{28,0},{1,29},{... | collective-permute-start | bytes 1179656 | tf_op jit(solution)/shard_map/ppermute | solution.py:15
  321.6 64.7 %collective-permute-start.40 = (bf16[2,16,2048]{2,1,0:T(8,128)(2,1)}, bf16[2,16,2048]{2,1,0:T(8,128)(2,1)S(1)}, u32[]{:S(2)}, u32[]{:S(2)}) collective-permute-start(bf16[2,16,2048]{2,1,0:T(8,128)(2,1)} %get-tuple-element.86), channel_id=1, source_target_pairs={{0,12},{4,8},{8,4},{12,0},{16,28},{20,24},{24,20},{28,16},{1,13},{... | collective-permute-start | bytes 393224 | tf_op jit(solution)/shard_map/ppermute | solution.py:15
  344.1 42.2 %collective-permute-start.41 = (bf16[2,16,2048]{2,1,0:T(8,128)(2,1)}, bf16[2,16,2048]{2,1,0:T(8,128)(2,1)}, u32[]{:S(2)}, u32[]{:S(2)}) collective-permute-start(bf16[2,16,2048]{2,1,0:T(8,128)(2,1)} %get-tuple-element.87), channel_id=1, source_target_pairs={{0,16},{4,20},{8,24},{12,28},{16,0},{20,4},{24,8},{28,12},{1,17},{... | collective-permute-start | bytes 393224 | tf_op jit(solution)/shard_map/ppermute | solution.py:15
  353.9 32.4 %collective-permute-start.42 = (bf16[2,16,2048]{2,1,0:T(8,128)(2,1)}, bf16[2,16,2048]{2,1,0:T(8,128)(2,1)}, u32[]{:S(2)}, u32[]{:S(2)}) collective-permute-start(bf16[2,16,2048]{2,1,0:T(8,128)(2,1)} %get-tuple-element.88), channel_id=1, source_target_pairs={{0,20},{4,16},{8,28},{12,24},{16,4},{20,0},{24,12},{28,8},{1,21},{... | collective-permute-start | bytes 393224 | tf_op jit(solution)/shard_map/ppermute | solution.py:15
  367.8 18.6 %collective-permute-start.43 = (bf16[2,16,2048]{2,1,0:T(8,128)(2,1)}, bf16[2,16,2048]{2,1,0:T(8,128)(2,1)}, u32[]{:S(2)}, u32[]{:S(2)}) collective-permute-start(bf16[2,16,2048]{2,1,0:T(8,128)(2,1)} %get-tuple-element.89), channel_id=1, source_target_pairs={{0,24},{4,28},{8,16},{12,20},{16,8},{20,12},{24,0},{28,4},{1,25},{... | collective-permute-start | bytes 393224 | tf_op jit(solution)/shard_map/ppermute | solution.py:15
  372.6 13.7 %collective-permute-start.44 = (bf16[2,16,2048]{2,1,0:T(8,128)(2,1)}, bf16[2,16,2048]{2,1,0:T(8,128)(2,1)}, u32[]{:S(2)}, u32[]{:S(2)}) collective-permute-start(bf16[2,16,2048]{2,1,0:T(8,128)(2,1)} %get-tuple-element.90), channel_id=1, source_target_pairs={{0,28},{4,24},{8,20},{12,16},{16,12},{20,8},{24,4},{28,0},{1,29},{... | collective-permute-start | bytes 393224 | tf_op jit(solution)/shard_map/ppermute | solution.py:15
  (70 other events, 1677.7 us)

commit v2 on v0

v2 whole, which is shorter than its diff:
```python
import jax
import jax.numpy as jnp
from jax import lax
from jax.experimental import pallas as pl
from jax.experimental.pallas import tpu as pltpu
from jax.sharding import PartitionSpec as P


GROUP = 16
WIDEST = 256
precise = lax.Precision.HIGHEST
MEMBER, DP = "member", "dp"


def swap(value, axis, size, k):
    return lax.ppermute(value, axis, [(i, i ^ k) for i in range(size)])


def launch(kernel, **settings):
    return pl.pallas_call(kernel, **settings)


def bits_of(size):
    return [1 << b for b in range(size.bit_length() - 1)]


def gather_members(value, size):
    have = [value]
    bits = bits_of(size)
    groups = [bits[:1]] + [bits[i : i + 2] for i in range(1, len(bits), 2)]
    for group in groups:
        stack = jnp.concatenate(have, axis=0) if len(have) > 1 else have[0]
        ks = [step * group[0] for step in range(1, 1 << len(group))]
        have = have + [swap(stack, MEMBER, size, k) for k in ks]
    return have


def copies(place, sources, plan, out_shapes, into=()):
    count, kept, results = len(sources), len(into), len(out_shapes)
    shapes = plan(None, None, None)
    total = len(shapes)

    def kernel(place_ref, *refs):
        ins, outs = refs[:count], refs[count + kept : count + kept + results]
        stage, sems = refs[-total - 1 : -1], refs[-1]
        items = [
            (
                [
                    pltpu.make_async_copy(a, stage[i].at[at], sems.at[0, i, j])
                    for j, (a, at) in enumerate(inward)
                ],
                [
                    pltpu.make_async_copy(stage[i].at[at], b, sems.at[1, i, j])
                    for j, (at, b) in enumerate(outward)
                ],
            )
            for i, (inward, outward) in enumerate(plan(place_ref, ins, outs))
        ]
        for inward, _ in items:
            for copy in inward:
                copy.start()
        for inward, outward in items:
            for copy in inward:
                copy.wait()
            for copy in outward:
                copy.start()
        for _, outward in items:
            for copy in outward:
                copy.wait()

    anywhere = pl.BlockSpec(memory_space=pl.ANY)
    return launch(
        kernel,
        in_specs=[pl.BlockSpec(memory_space=pltpu.SMEM)] + [anywhere] * (count + kept),
        out_specs=[anywhere] * results,
        out_shape=out_shapes,
        scratch_shapes=[pltpu.VMEM(shape, jnp.bfloat16) for shape in shapes]
        + [pltpu.SemaphoreType.DMA((2, total, 8))],
        input_output_aliases={1 + count + i: i for i in range(kept)},
    )(place, *sources, *into)


def views(middle, first, k, place_ref, early, late):
    slots, _, rows, _ = middle.shape
    _, _, tall, wide = first.shape
    block, half, found, at = place_ref[0] ^ k, rows // 2, [], 0
    for wanted, start in ((late, half), (early, 0)):
        for s in range(slots if wanted else 0):
            found.append((pl.ds(at, half), middle.at[s, block, start : start + half]))
            at += half
    for s in range(slots if early else 0):
        for h in range(tall // GROUP):
            left = (s * (tall // GROUP) + h) * wide
            found.append(
                (
                    (pl.ds(at, GROUP), pl.ds(left, wide)),
                    first.at[s, block, h * GROUP : (h + 1) * GROUP],
                )
            )
    return found


def piece_shape(middle, early, late):
    slots, _, rows, columns = middle.shape
    return (slots * (rows // 2) * (early + late) + GROUP * early, columns)


def cut_pieces(place, middle, first, wanted):
    shapes = [piece_shape(middle, early, late) for _, early, late in wanted]

    def plan(place_ref, ins, outs):
        if place_ref is None:
            return shapes
        return [
            (
                [(b, at) for at, b in views(*ins, k, place_ref, early, late)],
                [(slice(None), out)],
            )
            for (k, early, late), out in zip(wanted, outs)
        ]

    return list(
        copies(
            place, [middle, first], plan,
            [jax.ShapeDtypeStruct(shape, middle.dtype) for shape in shapes],
        )
    )


def join_early(place, middle_shape, first_shape, pieces):
    def plan(place_ref, ins, outs):
        if place_ref is None:
            return [piece.shape for piece in pieces.values()]
        return [
            ([(ref, slice(None))], views(*outs, k, place_ref, 1, 0)) for k, ref in zip(pieces, ins)
        ]

    shapes = [jax.ShapeDtypeStruct(shape, jnp.bfloat16) for shape in (middle_shape, first_shape)]
    return copies(place, list(pieces.values()), plan, shapes)


def join_late(place, middle, first, pieces):
    def plan(place_ref, ins, outs):
        if place_ref is None:
            return [piece.shape for piece in pieces.values()]
        return [
            ([(ref, slice(None))], views(outs[0], first, k, place_ref, 0, 1))
            for k, ref in zip(pieces, ins)
        ]

    shape = jax.ShapeDtypeStruct(middle.shape, middle.dtype)
    return copies(place, list(pieces.values()), plan, [shape], [middle])[0]


def spread(matrix, rows):
    n = matrix.shape[0]
    wide = n * rows
    pick = (
        lax.broadcasted_iota(jnp.int32, (wide, n), 0) // rows
        == lax.broadcasted_iota(jnp.int32, (wide, n), 1)
    ).astype(jnp.bfloat16)
    tall = lax.dot_general(
        pick, matrix, (((1,), (1,)), ((), ())), preferred_element_type=jnp.float32
    ).astype(jnp.bfloat16)
    full = lax.dot_general(
        tall, pick, (((1,), (1,)), ((), ())), preferred_element_type=jnp.float32
    )
    same = (
        lax.broadcasted_iota(jnp.int32, (wide, wide), 0) % rows
        == lax.broadcasted_iota(jnp.int32, (wide, wide), 1) % rows
    )
    return jnp.where(same, full, 0.0).astype(jnp.bfloat16)


def update_pieces(weights, pieces, slots, rows, block, strips=()):
    count, extra = len(pieces), len(strips)
    columns = pieces[0][0].shape[1]
    wide = count * slots * GROUP
    tall = slots * rows + (GROUP if strips else 0)
    halves = columns // block // slots

    def kernel(weights_ref, *refs):
        ins, refs = refs[:count], refs[count:]
        strip_refs, refs = refs[:extra], refs[extra:]
        outs, (upper_ref, lower_ref) = refs[:count], refs[count:]
        step = pl.program_id(0)

        @pl.when(step == 0)
        def _():
            upper = weights_ref[...].astype(jnp.bfloat16)
            lower = (weights_ref[...] - upper.astype(jnp.float32)).astype(jnp.bfloat16)
            upper_ref[...] = spread(upper, GROUP)
            lower_ref[...] = spread(lower, GROUP)

        def renewed(data):
            data = jnp.concatenate(data, axis=0)
            total = jnp.dot(upper_ref[...], data, preferred_element_type=jnp.float32)
            total += jnp.dot(lower_ref[...], data, preferred_element_type=jnp.float32)
            return total.reshape(count, slots, GROUP, block)

        for first in range(0, rows, GROUP):
            total = renewed(
                [
                    ref[s * rows + first : s * rows + first + GROUP, :]
                    for ref in ins
                    for s in range(slots)
                ]
            ).astype(jnp.bfloat16)
            for i, ref in enumerate(outs):
                for s in range(slots):
                    ref[s * rows + first : s * rows + first + GROUP, :] = total[i, s]
        if strips:
            half = step % halves
            total = renewed(
                [
                    ref[:, pl.ds(pl.multiple_of((s * halves + half) * block, block), block)]
                    for ref in strip_refs
                    for s in range(slots)
                ]
            )
            for i, ref in enumerate(outs):
                mine = total[i, 0]
                for s in range(1, slots):
                    mine = jnp.where(step // halves == s, total[i, s], mine)
                ref[slots * rows : tall, :] = mine.astype(jnp.bfloat16)

    return launch(
        kernel,
        grid=(columns // block,),
        in_specs=[pl.BlockSpec(weights.shape, lambda i: (0, 0))]
        + [pl.BlockSpec((slots * rows, block), lambda i, at=at: (at, i)) for _, at in pieces]
        + [pl.BlockSpec((GROUP, columns), lambda i, at=at: (at, 0)) for _, at in strips],
        out_specs=[pl.BlockSpec((tall, block), lambda i: (0, i))] * count,
        out_shape=[jax.ShapeDtypeStruct((tall, columns), jnp.bfloat16)] * count,
        scratch_shapes=[pltpu.VMEM((wide, wide), jnp.bfloat16)] * 2,
    )(weights, *[array for array, _ in pieces], *[array for array, _ in strips])


def layer_one(inputs, weights, scale, steps):
    rows, features = inputs[0].shape
    width = weights[0].shape[1]
    count, blocks = len(inputs), len(weights)
    tall = rows // steps

    def kernel(*refs):
        out_ref = refs[-1]
        data = jnp.concatenate([ref[...] for ref in refs[:count]], axis=0)
        for j in range(blocks):
            product = jnp.dot(data, refs[count + j][...], preferred_element_type=jnp.float32)
            hidden = jnp.tanh(product * scale).astype(jnp.bfloat16)
            for i in range(count):
                out_ref[i, :, j * width : (j + 1) * width] = hidden[i * tall : (i + 1) * tall]

    return launch(
        kernel,
        grid=(steps,),
        in_specs=[pl.BlockSpec((tall, features), lambda i: (i, 0))] * count
        + [pl.BlockSpec((features, width), lambda i: (0, 0))] * blocks,
        out_specs=pl.BlockSpec((count, tall, blocks * width), lambda i: (0, i, 0)),
        out_shape=jax.ShapeDtypeStruct((count, rows, blocks * width), jnp.bfloat16),
    )(*inputs, *weights)


def layer_two(place, hidden, own, pieces):
    groups, rows, _ = hidden.shape
    width, columns = pieces[0][1].shape
    array, maps = own
    count, own_count = len(pieces), len(maps)

    def kernel(place_ref, *refs):
        hidden_refs, refs = refs[: count + 1], refs[count + 1 :]
        own_refs, piece_refs, out_ref = refs[:own_count], refs[own_count:-1], refs[-1]
        value = jnp.concatenate(
            [
                jnp.dot(hidden_refs[0][0], ref[0], preferred_element_type=jnp.float32)
                for ref in own_refs
            ],
            axis=1,
        )
        for hidden_ref, ref in zip(hidden_refs[1:], piece_refs):
            value += jnp.dot(hidden_ref[0], ref[...], preferred_element_type=jnp.float32)
        out_ref[0] = value

    def column(at):
        return pl.BlockSpec((1, rows, width), lambda i, place_ref: (i, 0, at))

    return launch(
        kernel,
        grid_spec=pltpu.PrefetchScalarGridSpec(
            num_scalar_prefetch=1,
            grid=(groups,),
            in_specs=[column(0)] + [column(at) for at, _ in pieces]
            + [pl.BlockSpec((1, width, columns // own_count), index) for index in maps]
            + [pl.BlockSpec((width, columns), lambda i, place_ref: (0, 0))] * count,
            out_specs=pl.BlockSpec((1, rows, columns), lambda i, place_ref: (i, 0, 0)),
        ),
        out_shape=jax.ShapeDtypeStruct((groups, rows, columns), jnp.float32),
    )(place, *[hidden] * (count + 1), *[array] * own_count, *[value for _, value in pieces])


def layers_after(hidden, piece, total, last, scales, scale):
    groups, rows, _ = hidden.shape
    at, array = piece
    width, columns = array.shape
    classes = scales.shape[0]
    last_count = len(last)

    def kernel(hidden_ref, total_ref, array_ref, scales_ref, *refs):
        last_refs, out_refs = refs[:last_count], refs[last_count:]
        value = total_ref[0] + jnp.dot(
            hidden_ref[0], array_ref[...], preferred_element_type=jnp.float32
        )
        hidden_two = jnp.tanh(value * scale).astype(jnp.bfloat16)
        out = lax.dot_general(
            jnp.concatenate([ref[...] for ref in last_refs], axis=1), hidden_two,
            (((1,), (1,)), ((), ())), preferred_element_type=jnp.float32,
        )
        out = out * scale * scales_ref[...]
        for i in range(groups):
            @pl.when(pl.program_id(0) == i)
            def _():
                out_refs[i][...] = out

    def whole(shape):
        return pl.BlockSpec(shape, lambda i: (0, 0))

    return launch(
        kernel,
        grid=(groups,),
        in_specs=[
            pl.BlockSpec((1, rows, width), lambda i: (i, 0, at)),
            pl.BlockSpec((1, rows, columns), lambda i: (i, 0, 0)),
            whole((width, columns)),
            whole(scales.shape),
        ]
        + [whole(part.shape) for part in last],
        out_specs=[whole((classes, rows))] * groups,
        out_shape=[jax.ShapeDtypeStruct((classes, rows), jnp.float32)] * groups,
    )(hidden, total, array, scales, *last)


def forward(inputs, first_weight, middle_weight, last_weight, whiten, size, place):
    slots, features, width = first_weight.shape
    parts = size // slots
    units = middle_weight.shape[2]
    y = lax.axis_index(DP) // parts

    def column_block(place_ref, d, e):
        dy, dc = d // parts, d % parts
        at_y, at_c = place_ref[1] // parts, place_ref[1] % parts
        return at_y ^ dy, (at_y ^ dy ^ e) * parts + (at_c ^ dc)

    ds = list(range(size - 1, 0, -1))

    def cut_middle(place_ref, ins, outs):
        if place_ref is None:
            return [(width, slots * width)] * len(ds)
        items = []
        for d, out in zip(ds, outs):
            inward = []
            for e in range(slots):
                slot, at = column_block(place_ref, d, e)
                at = pl.multiple_of(at * width, width)
                inward.append(
                    (ins[0].at[slot, :, pl.ds(at, width)], (slice(None), pl.ds(e * width, width)))
                )
            items.append((inward, [(slice(None), out)]))
        return items

    shape = jax.ShapeDtypeStruct((width, slots * width), middle_weight.dtype)
    cuts = copies(place, [middle_weight], cut_middle, [shape] * len(ds))
    middle_at = {d: swap(cut, DP, size, d) for d, cut in zip(ds, cuts)}

    def own_map(e):
        def index(i, place_ref):
            slot, at = column_block(place_ref, 0, e)
            return slot, 0, at

        return index

    def slot_of(array, dy):
        return lax.dynamic_index_in_dim(array, y ^ dy, 0, keepdims=False)

    def everyone(mine):
        have = dict(zip(range(0, size, parts), mine))
        for bit in bits_of(parts):
            for d, value in list(have.items()):
                have[d ^ bit] = swap(value, DP, size, bit)
        return [have[d] for d in range(size)]

    def far(value_of):
        return [value_of(0)] + [swap(value_of(dy), DP, size, dy * parts) for dy in range(1, slots)]

    every_input = everyone(far(lambda dy: inputs))
    first_all = everyone(far(lambda dy: slot_of(first_weight, dy)))
    last_flipped = jnp.transpose(last_weight, (0, 2, 1))
    last_mine = far(lambda dy: slot_of(last_flipped, dy))
    hidden_one = layer_one(every_input, first_all, features ** (-0.5), size)
    final = parts
    total = layer_two(
        place, hidden_one, (middle_weight, [own_map(e) for e in range(slots)]),
        [(d, middle_at[d]) for d in range(1, size) if d != final],
    )
    blocks = layers_after(
        hidden_one, (final, middle_at[final]), total, last_mine, whiten[:, None], units ** (-0.5)
    )
    received = [block if d == 0 else swap(block, DP, size, d) for d, block in enumerate(blocks)]
    by_slot = [sum(received[dy * parts + dc] for dc in range(parts)) for dy in range(slots)]
    return jnp.concatenate(
        [
            sum(jnp.where(y ^ s == dy, value, 0.0) for dy, value in enumerate(by_slot))
            for s in range(slots)
        ],
        axis=0,
    )


def gram_of(every, observed):
    classes = observed.shape[0]
    counts = [part.shape[0] // classes for part in every]
    ensemble = sum(counts)
    side = -(-(ensemble + 1) // 8) * 8
    count = len(every)

    def kernel(*refs):
        observed_ref, out_ref = refs[count:]
        parts = [(ref[...], n) for ref, n in zip(refs, counts)]
        values = jnp.concatenate(
            [
                jnp.concatenate(
                    [part[j * classes + i][None] for part, n in parts for j in range(n)], axis=0
                )
                for i in range(classes)
            ],
            axis=1,
        )
        seen = jnp.concatenate([observed_ref[i : i + 1, :] for i in range(classes)], axis=1)
        center = jnp.sum(values, axis=0, keepdims=True) / ensemble
        stacked = jnp.concatenate(
            [values - center, jnp.broadcast_to(seen - center, (side - ensemble, seen.shape[1]))],
            axis=0,
        )
        out_ref[...] = lax.dot_general(
            stacked, stacked, (((1,), (1,)), ((), ())),
            precision=precise, preferred_element_type=jnp.float32,
        )

    return launch(
        kernel, out_shape=jax.ShapeDtypeStruct((side, side), jnp.float32)
    )(*every, observed)


def weights_of(every, observed, size):
    ensemble = sum(part.shape[0] for part in every) // observed.shape[0]
    both = gram_of(every, observed)
    bits = bits_of(size)
    for bit in bits[:-1]:
        both = both + swap(both, DP, size, bit)
    other = swap(both, DP, size, bits[-1])

    def kernel(first_ref, second_ref, out_ref):
        total = first_ref[...] + second_ref[...]
        gram_matrix, drive = total[:ensemble, :ensemble], total[:ensemble, ensemble : ensemble + 1]
        row = lax.broadcasted_iota(jnp.int32, (ensemble, ensemble), 0)
        column = lax.broadcasted_iota(jnp.int32, (ensemble, ensemble), 1)
        same = (row == column).astype(jnp.float32)
        system = gram_matrix + ensemble * same
        right = drive - gram_matrix
        at = lax.broadcasted_iota(jnp.int32, (ensemble, 1), 0)
        for j in range(ensemble):
            factor = system[:, j : j + 1] / system[j : j + 1, j : j + 1]
            factor = jnp.where(at == j, 0.0, factor)
            system = system - factor * system[j : j + 1, :]
            right = right - factor * right[j : j + 1, :]
        pivots = jnp.sum(system * same, axis=1, keepdims=True)
        mixing = right / pivots
        out_ref[...] = same + mixing - jnp.sum(mixing, axis=0, keepdims=True) / ensemble

    return launch(
        kernel, out_shape=jax.ShapeDtypeStruct((ensemble, ensemble), jnp.float32)
    )(both, other)


def combine(weights, values, classes):
    slots = weights.shape[1]
    count = len(values)
    width = values[0].shape[1]

    def kernel(weights_ref, *refs):
        out_ref = refs[-1]
        totals, k = [0.0] * slots, 0
        for ref in refs[:count]:
            rows = ref[...].astype(jnp.float32)
            for i in range(0, rows.shape[0], classes):
                for s in range(slots):
                    totals[s] += weights_ref[k, s] * rows[i : i + classes]
                k += 1
        for s in range(slots):
            out_ref[s] = totals[s].astype(out_ref.dtype)

    return launch(
        kernel,
        in_specs=[pl.BlockSpec(memory_space=pltpu.SMEM)]
        + [pl.BlockSpec(memory_space=pltpu.VMEM)] * count,
        out_shape=jax.ShapeDtypeStruct((slots, classes, width), values[0].dtype),
    )(weights, *values)


def relayed(pieces, members):
    out = dict(pieces)
    for k in evens(members):
        if k in pieces:
            out[k] = swap(pieces[k], MEMBER, members, k)
        if k + 1 in pieces:
            near = swap(pieces[k + 1], MEMBER, members, 1)
            out[k + 1] = swap(near, MEMBER, members, k)
    if 1 in pieces:
        out[1] = swap(pieces[1], MEMBER, members, 1)
    return out


def evens(members):
    half = members // 2
    return [half] + [k for k in range(2, members, 2) if k != half]


def held(members):
    return evens(members)[:1] + evens(members)[-1:]


def on_device(
    members, size,
    feature_pool, labels, sample_rows, noise_variance, first_weight, middle_weight, last_weight,
):
    slots = first_weight.shape[0]
    classes_total = noise_variance.shape[0]
    ensemble = members * slots
    here = lax.axis_index(MEMBER)
    place = jnp.stack([here, lax.axis_index(DP)]).astype(jnp.int32)
    whiten = 1.0 / jnp.sqrt(noise_variance)
    inputs = feature_pool[sample_rows]
    classes = labels[sample_rows]
    target = (
        classes[None, :] == jnp.arange(classes_total, dtype=jnp.int32)[:, None]
    ).astype(jnp.float32)
    observed = target * whiten[:, None]

    def blocks(array):
        return array.reshape((slots, members, array.shape[1] // members) + array.shape[2:])

    first_blocks, middle_blocks = blocks(first_weight), blocks(middle_weight)
    rows, columns = middle_blocks.shape[2:]
    tall, wide = first_blocks.shape[2:]
    fits = (
        members >= 8
        and ensemble * GROUP <= WIDEST
        and rows % (2 * GROUP) == 0
        and tall % GROUP == 0
        and tall // GROUP * wide * slots == columns
    )
    scaled = forward(inputs, first_weight, middle_weight, last_weight, whiten, size, place)
    every = gather_members(scaled, members)
    if not fits:
        return plain_update(
            weights_of(every, observed, size), members, first_weight, middle_weight, last_weight
        )

    each = range(members)
    wait = [k + 1 for k in held(members)]
    head = evens(members)[0]
    others = [k for k in each if k != head]
    cut = cut_pieces(place, middle_blocks, first_blocks, [(head, 1, 1)])
    cut += cut_pieces(
        place, middle_blocks, first_blocks,
        [(k, 1, k not in wait) for k in others] + [(k, 0, 1) for k in wait],
    )
    pieces_in = relayed(dict(zip([head] + others, cut)), members)
    late_in = relayed(dict(zip(wait, cut[members:])), members)
    weights = weights_of(every, observed, size)

    half = rows // 2
    strip = slots * half // GROUP
    early_back = relayed(
        dict(
            enumerate(
                update_pieces(
                    weights,
                    [(pieces_in[k], int(k not in wait)) for k in each], slots, half, wide,
                    [(pieces_in[k], strip * (1 + (k not in wait))) for k in each],
                )
            )
        ),
        members,
    )
    late_back = relayed(
        dict(
            enumerate(
                update_pieces(
                    weights,
                    [((late_in if k in wait else pieces_in)[k], 0) for k in each], slots, half, wide,
                )
            )
        ),
        members,
    )
    last_flipped = jnp.transpose(last_weight, (0, 2, 1)).reshape(-1, last_weight.shape[1])
    last_all = gather_members(last_flipped, members)
    new_last = jnp.transpose(combine(weights[:, :slots], last_all, classes_total), (0, 2, 1))

    new_middle, new_first = join_early(
        place, middle_blocks.shape, first_blocks.shape, early_back
    )
    last = evens(members)[-1:] + [k + 1 for k in evens(members)]
    kept = {k: late_back[k] for k in each if k not in last}
    new_middle = join_late(place, new_middle, first_blocks, kept)
    for k in last:
        piece = late_back[k].reshape(slots, 1, half, columns)
        new_middle = lax.dynamic_update_slice(new_middle, piece, (0, here ^ k, half, 0))
    return (
        new_first.reshape(first_weight.shape),
        new_middle.reshape(middle_weight.shape),
        new_last,
    )


def plain_update(weights, members, first_weight, middle_weight, last_weight):
    slots = first_weight.shape[0]
    ensemble = members * slots
    member = jnp.arange(ensemble, dtype=jnp.int32)
    spot = (member // slots ^ lax.axis_index(MEMBER)) * slots + member % slots
    weights = weights[spot][:, spot].T
    upper = weights.astype(jnp.bfloat16)
    lower = (weights - upper.astype(jnp.float32)).astype(jnp.bfloat16)

    def renew(array):
        piece = lax.all_to_all(array, MEMBER, split_axis=1, concat_axis=0, tiled=True)
        flat = piece.reshape(ensemble, -1)
        new = jnp.dot(upper, flat, preferred_element_type=jnp.float32)
        new += jnp.dot(lower, flat, preferred_element_type=jnp.float32)
        new = new.astype(jnp.bfloat16).reshape(piece.shape)
        return lax.all_to_all(new, MEMBER, split_axis=0, concat_axis=1, tiled=True)

    return renew(first_weight), renew(middle_weight), renew(last_weight)


def solution(mesh):
    members, size = mesh.shape[MEMBER], mesh.shape[DP]
    in_specs = (
        P(DP, None),
        P(DP),
        P(DP),
        P(),
        P(MEMBER, None, DP),
        P(MEMBER, DP, None),
        P(MEMBER, DP, None),
    )
    out_specs = (P(MEMBER, None, DP), P(MEMBER, DP, None), P(MEMBER, DP, None))

    def step(*arrays):
        return on_device(members, size, *arrays)

    def run(*arrays):
        mapped = jax.shard_map(
            step, mesh=mesh, in_specs=in_specs, out_specs=out_specs, check_vma=False
        )
        return mapped(*arrays)

    return run
```

time: 350 us -> 346 us (0.989)
  starting transfers between devices: 29.8 us -> 96.6 us
  Pallas kernels: 0 us -> 55.4 us
  blocking collectives: 43.1 us -> 0 us
  local copies, waits for them, and re-layouts: 40.9 us -> 20 us
  matrix products: 20.6 us -> 0 us
  other arithmetic: 19.1 us -> 2.72 us
  between operations: 14.4 us -> 1.13 us
  waiting for transfers between devices: 181 us -> 168 us
    all_to_all x6 -> x0, waiting for transfers between devices: 180 us -> none  [the longest x1 90.4 us: on_device(): lax.all_to_all(updated[1], 'member', split_axis=0, concat_axis=1, tiled=T...]
    ppermute x0 -> x57, waiting for transfers between devices: none -> 168 us  [swap(): return lax.ppermute(value, axis, [(i, i ^ k) for i in range(size)])]
    ppermute x0 -> x57, starting transfers between devices: none -> 96.6 us  [swap(): return lax.ppermute(value, axis, [(i, i ^ k) for i in range(size)])]
    pallas_call x0 -> x13, Pallas kernels: none -> 55.4 us  [the longest x5 19.6 us: copies(): launch(kernel, in_specs=[pl.BlockSpec(memory_space=pltpu.SMEM)] + [anywhe...]
    all_gather x2 -> x0, blocking collectives: 37.2 us -> none  [the longest x1 30.8 us: on_device(): every_member = lax.all_gather(scaled, 'member', axis=0, tiled=True)]
    all_to_all x6 -> x0, starting transfers between devices: 29.7 us -> none  [the longest x1 7.28 us: on_device(): lax.all_to_all(last_weight, 'member', split_axis=1, concat_axis=0, tiled=...]
    dot_general x7 -> x0, matrix products: 20.3 us -> none  [the longest x1 9.89 us: on_device(): jnp.einsum('jsk,jkh->jsh', hidden_one, middle_full, preferred_element_typ...]
    unnamed x36 -> x101, local copies, waits for them, and re-layouts: 23.7 us -> 7.74 us
  transfers between devices with their start and end apart: 8 -> 57, of which waited for: 5 -> 20; matrix products, arithmetic and copies ran while one was open for 15% -> 5% of each run, Pallas kernels for 0% -> 15%
where the time goes in v2:
time: 346 us; the launch traced here: 344 us
  waiting for transfers between devices  168 us (49%)
  starting transfers between devices  96.6 us (28%)
  Pallas kernels  55.4 us (16%)
  local copies, waits for them, and re-layouts  20 us (6%)
    ppermute x57, waiting for transfers between devices, swap(): return lax.ppermute(value, axis, [(i, i ^ k) for i in range(size)])  168 us
    ppermute x57, starting transfers between devices, swap(): return lax.ppermute(value, axis, [(i, i ^ k) for i in range(size)])  96.6 us
    pallas_call x5, Pallas kernels, copies(): launch(kernel, in_specs=[pl.BlockSpec(memory_space=pltpu.SMEM)] + [anywhe...  19.6 us
    pallas_call x2, Pallas kernels, update_pieces(): launch(kernel, grid=(columns // block,), in_specs=[pl.BlockSpec(weights.s...  10.5 us
    pallas_call x1, Pallas kernels, layer_two(): launch(kernel, grid_spec=pltpu.PrefetchScalarGridSpec(num_scalar_prefetch...  8.47 us
    unnamed x101, local copies, waits for them, and re-layouts  7.74 us
  transfers between devices with their start and end apart: 57, of which 20 were waited for; matrix products, arithmetic and copies ran while one was open for 5% of the time, Pallas kernels for 15%

profile of v2, /device:TPU:0, one launch (start us, length us, event | category | flops | bytes accessed | tf_op | source)
XLA Modules:
  0.0 344.3 jit_solution(14892716159876329992)
XLA Ops:
  1.2 4.0 %shard_map.95 = (bf16[512,1024]{1,0:T(8,128)(2,1)}, bf16[512,1024]{1,0:T(8,128)(2,1)}, bf16[512,1024]{1,0:T(8,128)(2,1)}) custom-call(s32[2]{0:T(128)} %pad_add_fusion.place_ref, bf16[2,512,2048]{2,1,0:T(8,128)(2,1)} %refs_4_.1), custom_call_target="tpu_custom_call" | custom-call | tf_op jit(solution)/shard_map/pallas_call | solution.py:72
  5.8 2.6 collective-permute-start.7
  9.6 2.0 collective-permute-start.1
  11.8 45.8 %collective-permute-done.1.refs_2_ = bf16[256,256]{1,0:T(8,128)(2,1)S(1)} collective-permute-done((bf16[256,256]{1,0:T(8,128)(2,1)S(1)}, bf16[256,256]{1,0:T(8,128)(2,1)S(1)}, u32[]{:S(2)}, u32[]{:S(2)}) %collective-permute-start.1) | collective-permute-done | bytes 131104 | tf_op jit(solution)/shard_map/ppermute | solution.py:16
  57.6 1.7 collective-permute-start.4
  60.0 5.7 %collective-permute-done.4.refs_6_ = bf16[256,512]{1,0:T(8,128)(2,1)S(1)} collective-permute-done((bf16[256,512]{1,0:T(8,128)(2,1)S(1)}, bf16[256,512]{1,0:T(8,128)(2,1)S(1)}, u32[]{:S(2)}, u32[]{:S(2)}) %collective-permute-start.4) | collective-permute-done | bytes 262176 | tf_op jit(solution)/shard_map/ppermute | solution.py:16
  66.2 5.5 %shard_map.100 = (bf16[144,2048]{1,0:T(8,128)(2,1)}, bf16[144,2048]{1,0:T(8,128)(2,1)}, bf16[144,2048]{1,0:T(8,128)(2,1)}, bf16[144,2048]{1,0:T(8,128)(2,1)}, bf...) custom-call(s32[2]{0:T(128)} %pad_add_fusion.place_ref, ...), custom_call_target="tpu_custom_call" | custom-call | tf_op jit(solution)/shard_map/pallas_call | solution.py:72
  81.4 4.9 %shard_map.94.refs_0_.refs_1_.refs_2_.hidden_ref = bf16[4,256,2048]{2,1,0:T(8,128)(2,1)} custom-call(bf16[256,256]{1,0:T(8,128)(2,1)} %copy-done.12, bf16[256,256]{1,0:T(8,128)(2,1)} %copy-done.28, bf16[256,256]{1,0:T(8,128)(2,1)} %copy-done.27, bf16[256,256]{1,0:T(8,128)(2,1)} %collective-permute-done.2.refs_3_, bf16[256,512]{1,0:T(8,128)(2,1)} %copy-done.11, ...), custom_call_target="tpu_custom_call" | custom-call | tf_op jit(solution)/shard_map/pallas_call | solution.py:254
  86.3 8.5 %shard_map.96.total_ref = f32[4,256,1024]{2,1,0:T(8,128)} custom-call(s32[2]{0:T(128)} %pad_add_fusion.place_ref, bf16[4,256,2048]{2,1,0:T(8,128)(2,1)} %shard_map.94.refs_0_.refs_1_.refs_2_.hidden_ref, bf16[4,256,2048]{2,1,0:T(8,128)(2,1)} %shard_map.94.refs_0_.refs_1_.refs_2_.hidden_ref, ...), custom_call_target="tpu_custom_call" | custom-call | tf_op jit(solution)/shard_map/pallas_call | solution.py:287
  95.4 5.7 %shard_map.97 = (f32[10,256]{1,0:T(8,128)}, f32[10,256]{1,0:T(8,128)}, f32[10,256]{1,0:T(8,128)}, f32[10,256]{1,0:T(8,128)}) custom-call(bf16[4,256,2048]{2,1,0:T(8,128)(2,1)} %shard_map.94.refs_0_.refs_1_.refs_2_.hidden_ref, f32[4,256,1024]{2,1,0:T(8,128)} %shard_map.96.total_ref, bf16[512,1024]{1,0:T(8,128)(2,1)} %collective-permute-done.8.array_ref, ...), custom_call_target="tpu_custom_call" | custom-call | tf_op jit(solution)/shard_map/pallas_call | solution.py:327
  105.3 2.6 collective-permute-start.40
  110.0 3.6 %collective-permute-done.24 = bf16[80,2048]{1,0:T(8,128)(2,1)S(1)} collective-permute-done((bf16[80,2048]{1,0:T(8,128)(2,1)S(1)}, bf16[80,2048]{1,0:T(8,128)(2,1)S(1)}, u32[]{:S(2)}, u32[]{:S(2)}) %collective-permute-start.24) | collective-permute-done | bytes 327712 | tf_op jit(solution)/shard_map/ppermute | solution.py:16
  114.2 6.1 %collective-permute-done.27 = bf16[80,2048]{1,0:T(8,128)(2,1)S(1)} collective-permute-done((bf16[80,2048]{1,0:T(8,128)(2,1)S(1)}, bf16[80,2048]{1,0:T(8,128)(2,1)S(1)}, u32[]{:S(2)}, u32[]{:S(2)}) %collective-permute-start.27) | collective-permute-done | bytes 327712 | tf_op jit(solution)/shard_map/ppermute | solution.py:16
  121.6 1.6 collective-permute-start.20
  123.2 3.5 %collective-permute-done.40.refs_5_ = bf16[64,2048]{1,0:T(8,128)(2,1)} collective-permute-done((bf16[64,2048]{1,0:T(8,128)(2,1)}, bf16[64,2048]{1,0:T(8,128)(2,1)}, u32[]{:S(2)}, u32[]{:S(2)}) %collective-permute-start.40) | collective-permute-done | bytes 262176 | tf_op jit(solution)/shard_map/ppermute | solution.py:16
  126.7 7.1 %collective-permute-start.15 = (f32[40,256]{1,0:T(8,128)S(1)}, f32[40,256]{1,0:T(8,128)S(1)}, u32[]{:S(2)}, u32[]{:S(2)}) collective-permute-start(f32[40,256]{1,0:T(8,128)S(1)} %pad_maximum_fusion), channel_id=1, source_target_pairs={{0,16},{4,20},{8,24},{12,28},{16,0},{20,4},{24,8},{28,12},{1,17},{... | collective-permute-start | bytes 122888 | tf_op jit(solution)/shard_map/ppermute | solution.py:16
  134.2 2.7 shard_map.101
  137.0 3.3 collective-permute-done.14.refs_2_
  140.3 3.9 %collective-permute-start.26 = (bf16[144,2048]{1,0:T(8,128)(2,1)}, bf16[144,2048]{1,0:T(8,128)(2,1)S(1)}, u32[]{:S(2)}, u32[]{:S(2)}) collective-permute-start(bf16[144,2048]{1,0:T(8,128)(2,1)} %get-tuple-element.49), channel_id=1, source_target_pairs={{0,24},{4,28},{8,16},{12,20},{16,8},{20,12},{24,0},{28,4},{1,25},{... | collective-permute-start | bytes 1769480 | tf_op jit(solution)/shard_map/ppermute | solution.py:16
  144.9 2.1 gather_fusion.1
  147.7 1.8 shard_map.98
  150.9 2.3 collective-permute-start.25
  154.5 3.2 collective-permute-done.18.second_ref
  159.8 2.7 shard_map.99.weights_ref
  162.5 46.1 %collective-permute-done.23.refs_4_.refs_12_ = bf16[144,2048]{1,0:T(8,128)(2,1)S(1)} collective-permute-done((bf16[144,2048]{1,0:T(8,128)(2,1)}, bf16[144,2048]{1,0:T(8,128)(2,1)S(1)}, u32[]{:S(2)}, u32[]{:S(2)}) %collective-permute-start.23) | collective-permute-done | bytes 589856 | tf_op jit(solution)/shard_map/ppermute | solution.py:16
  209.7 4.9 %shard_map.104 = (bf16[64,2048]{1,0:T(8,128)(2,1)}, bf16[64,2048]{1,0:T(8,128)(2,1)}, bf16[64,2048]{1,0:T(8,128)(2,1)}, bf16[64,2048]{1,0:T(8,128)(2,1)}, bf16[6...) custom-call(f32[16,16]{1,0:T(8,128)} %shard_map.99.weights_ref, ...), custom_call_target="tpu_custom_call" | custom-call | tf_op jit(solution)/shard_map/pallas_call | solution.py:227
  217.7 4.7 %collective-permute-done.53.refs_1_ = bf16[20,512]{1,0:T(8,128)(2,1)S(1)} collective-permute-done((bf16[20,512]{1,0:T(8,128)(2,1)S(1)}, bf16[20,512]{1,0:T(8,128)(2,1)S(1)}, u32[]{:S(2)}, u32[]{:S(2)}) %collective-permute-start.53) | collective-permute-done | bytes 20512 | tf_op jit(solution)/shard_map/ppermute | solution.py:16
  222.4 4.0 %collective-permute-done.54.refs_2_ = bf16[40,512]{1,0:T(8,128)(2,1)S(1)} collective-permute-done((bf16[40,512]{1,0:T(8,128)(2,1)S(1)}, bf16[40,512]{1,0:T(8,128)(2,1)S(1)}, u32[]{:S(2)}, u32[]{:S(2)}) %collective-permute-start.54) | collective-permute-done | bytes 40992 | tf_op jit(solution)/shard_map/ppermute | solution.py:16
  229.8 5.6 %shard_map.102 = (bf16[80,2048]{1,0:T(8,128)(2,1)}, bf16[80,2048]{1,0:T(8,128)(2,1)}, bf16[80,2048]{1,0:T(8,128)(2,1)}, bf16[80,2048]{1,0:T(8,128)(2,1)}, bf16[8...) custom-call(f32[16,16]{1,0:T(8,128)} %shard_map.99.weights_ref, ...), custom_call_target="tpu_custom_call" | custom-call | tf_op jit(solution)/shard_map/pallas_call | solution.py:227
  240.7 5.6 %collective-permute-done.31 = bf16[80,2048]{1,0:T(8,128)(2,1)S(1)} collective-permute-done((bf16[80,2048]{1,0:T(8,128)(2,1)}, bf16[80,2048]{1,0:T(8,128)(2,1)S(1)}, u32[]{:S(2)}, u32[]{:S(2)}) %collective-permute-start.31) | collective-permute-done | bytes 327712 | tf_op jit(solution)/shard_map/ppermute | solution.py:16
  247.6 5.7 %collective-permute-done.34 = bf16[80,2048]{1,0:T(8,128)(2,1)S(1)} collective-permute-done((bf16[80,2048]{1,0:T(8,128)(2,1)}, bf16[80,2048]{1,0:T(8,128)(2,1)S(1)}, u32[]{:S(2)}, u32[]{:S(2)}) %collective-permute-start.34) | collective-permute-done | bytes 327712 | tf_op jit(solution)/shard_map/ppermute | solution.py:16
  253.3 2.9 collective-permute-start.36
  256.2 3.9 %collective-permute-done.37 = bf16[80,2048]{1,0:T(8,128)(2,1)S(1)} collective-permute-done((bf16[80,2048]{1,0:T(8,128)(2,1)}, bf16[80,2048]{1,0:T(8,128)(2,1)S(1)}, u32[]{:S(2)}, u32[]{:S(2)}) %collective-permute-start.37) | collective-permute-done | bytes 327712 | tf_op jit(solution)/shard_map/ppermute | solution.py:16
  260.7 2.8 collective-permute-done.29.refs_1_
  263.6 1.9 collective-permute-start.35
  267.0 5.1 %collective-permute-done.33.refs_4_ = bf16[80,2048]{1,0:T(8,128)(2,1)S(1)} collective-permute-done((bf16[80,2048]{1,0:T(8,128)(2,1)}, bf16[80,2048]{1,0:T(8,128)(2,1)S(1)}, u32[]{:S(2)}, u32[]{:S(2)}) %collective-permute-start.33) | collective-permute-done | bytes 327712 | tf_op jit(solution)/shard_map/ppermute | solution.py:16
  272.0 13.6 %collective-permute-start.49 = (bf16[64,2048]{1,0:T(8,128)(2,1)}, bf16[64,2048]{1,0:T(8,128)(2,1)}, u32[]{:S(2)}, u32[]{:S(2)}) collective-permute-start(bf16[64,2048]{1,0:T(8,128)(2,1)} %get-tuple-element.69), channel_id=1, source_target_pairs={{0,4},{4,0},{8,12},{12,8},{16,20},{20,16},{24,28},{28,24},{1,5},{5... | collective-permute-start | bytes 786440 | tf_op jit(solution)/shard_map/ppermute | solution.py:16
  285.7 9.2 %collective-permute-start.45 = (bf16[64,2048]{1,0:T(8,128)(2,1)}, bf16[64,2048]{1,0:T(8,128)(2,1)S(1)}, u32[]{:S(2)}, u32[]{:S(2)}) collective-permute-start(bf16[64,2048]{1,0:T(8,128)(2,1)} %get-tuple-element.65), channel_id=1, source_target_pairs={{0,16},{4,20},{8,24},{12,28},{16,0},{20,4},{24,8},{28,12},{1,17},{... | collective-permute-start | bytes 786440 | tf_op jit(solution)/shard_map/ppermute | solution.py:16
  294.9 9.9 %collective-permute-done.35.refs_5_ = bf16[80,2048]{1,0:T(8,128)(2,1)S(1)} collective-permute-done((bf16[80,2048]{1,0:T(8,128)(2,1)S(1)}, bf16[80,2048]{1,0:T(8,128)(2,1)S(1)}, u32[]{:S(2)}, u32[]{:S(2)}) %collective-permute-start.35) | collective-permute-done | bytes 327712 | tf_op jit(solution)/shard_map/ppermute | solution.py:16
  304.8 2.3 collective-permute-start.46
  307.1 11.7 %collective-permute-start.48 = (bf16[64,2048]{1,0:T(8,128)(2,1)}, bf16[64,2048]{1,0:T(8,128)(2,1)}, u32[]{:S(2)}, u32[]{:S(2)}) collective-permute-start(bf16[64,2048]{1,0:T(8,128)(2,1)} %copy-done.48), channel_id=1, source_target_pairs={{0,16},{4,20},{8,24},{12,28},{16,0},{20,4},{24,8},{28,12},{1,17},{... | collective-permute-start | bytes 786440 | tf_op jit(solution)/shard_map/ppermute | solution.py:16
  318.9 1.7 shard_map.106
  322.0 4.2 %shard_map.103 = (bf16[2,8,64,2048]{3,2,1,0:T(8,128)(2,1)}, bf16[2,8,32,512]{3,2,1,0:T(8,128)(2,1)}) custom-call(s32[2]{0:T(128)} %pad_add_fusion.place_ref, bf16[80,2048]{1,0:T(8,128)(2,1)} %get-tuple-element.51.refs_0_, bf16[80,2048]{1,0:T(8,128)(2,1)} %copy-done.13, bf16[80,2048]{1,0:T(8,128)(2,1)} %copy-done.14, bf16[80,2048]{1,0:T(8,128)(2,1)} %copy-done.17, ...), custom_call_target="tpu_custom_call" | custom-call | tf_op jit(solution)/shard_map/pallas_call | solution.py:72
  326.3 1.6 collective-permute-start.52
  329.4 3.1 shard_map.105
  332.5 1.7 constant_dynamic-update-slice_fusion.3
  334.2 6.9 %collective-permute-done.48 = bf16[64,2048]{1,0:T(8,128)(2,1)} collective-permute-done((bf16[64,2048]{1,0:T(8,128)(2,1)}, bf16[64,2048]{1,0:T(8,128)(2,1)}, u32[]{:S(2)}, u32[]{:S(2)}) %collective-permute-start.48) | collective-permute-done | bytes 262176 | tf_op jit(solution)/shard_map/ppermute | solution.py:16
  341.1 1.7 constant_dynamic-update-slice_fusion.2
  (201 shorter events, 49.3 us)
Async XLA Ops:
  5.2 70.1 %collective-permute-start.6 = (bf16[512,1024]{1,0:T(8,128)(2,1)}, bf16[512,1024]{1,0:T(8,128)(2,1)S(1)}, u32[]{:S(2)}, u32[]{:S(2)}) collective-permute-start(bf16[512,1024]{1,0:T(8,128)(2,1)} %get-tuple-element.37), channel_id=1, source_target_pairs={{0,1},{1,0},{2,3},{3,2},{4,5},{5,4},{6,7},{7,6},{8,9},{9,8},{10,11... | collective-permute-start | bytes 3145736 | tf_op jit(solution)/shard_map/ppermute | solution.py:16
  5.8 70.9 %collective-permute-start.7 = (bf16[512,1024]{1,0:T(8,128)(2,1)}, bf16[512,1024]{1,0:T(8,128)(2,1)S(1)}, u32[]{:S(2)}, u32[]{:S(2)}) collective-permute-start(bf16[512,1024]{1,0:T(8,128)(2,1)} %get-tuple-element.38), channel_id=1, source_target_pairs={{0,3},{1,2},{2,1},{3,0},{4,7},{5,6},{6,5},{7,4},{8,11},{9,10},{10,... | collective-permute-start | bytes 3145736 | tf_op jit(solution)/shard_map/ppermute | solution.py:16
  8.4 86.4 %collective-permute-start.8 = (bf16[512,1024]{1,0:T(8,128)(2,1)}, bf16[512,1024]{1,0:T(8,128)(2,1)}, u32[]{:S(2)}, u32[]{:S(2)}) collective-permute-start(bf16[512,1024]{1,0:T(8,128)(2,1)} %get-tuple-element.39), channel_id=1, source_target_pairs={{0,2},{1,3},{2,0},{3,1},{4,6},{5,7},{6,4},{7,5},{8,10},{9,11},{10,... | collective-permute-start | bytes 3145736 | tf_op jit(solution)/shard_map/ppermute | solution.py:16
  9.6 48.0 %collective-permute-start.1 = (bf16[256,256]{1,0:T(8,128)(2,1)S(1)}, bf16[256,256]{1,0:T(8,128)(2,1)S(1)}, u32[]{:S(2)}, u32[]{:S(2)}) collective-permute-start(bf16[256,256]{1,0:T(8,128)(2,1)S(1)} %gather_fusion), channel_id=1, source_target_pairs={{0,2},{1,3},{2,0},{3,1},{4,6},{5,7},{6,4},{7,5},{8,10},{9,11},{10,... | collective-permute-start | bytes 393224 | tf_op jit(solution)/shard_map/ppermute | solution.py:16
  11.7 47.6 %collective-permute-start = (bf16[256,256]{1,0:T(8,128)(2,1)S(1)}, bf16[256,256]{1,0:T(8,128)(2,1)S(1)}, u32[]{:S(2)}, u32[]{:S(2)}) collective-permute-start(bf16[256,256]{1,0:T(8,128)(2,1)S(1)} %gather_fusion), channel_id=1, source_target_pairs={{0,1},{1,0},{2,3},{3,2},{4,5},{5,4},{6,7},{7,6},{8,9},{9,8},{10,11... | collective-permute-start | bytes 393224 | tf_op jit(solution)/shard_map/ppermute | solution.py:16
  57.6 8.1 %collective-permute-start.4 = (bf16[256,512]{1,0:T(8,128)(2,1)S(1)}, bf16[256,512]{1,0:T(8,128)(2,1)S(1)}, u32[]{:S(2)}, u32[]{:S(2)}) collective-permute-start(bf16[256,512]{1,0:T(8,128)(2,1)S(1)} %get-tuple-element.77), channel_id=1, source_target_pairs={{0,2},{1,3},{2,0},{3,1},{4,6},{5,7},{6,4},{7,5},{8,10},{9,11},{10,... | collective-permute-start | bytes 786440 | tf_op jit(solution)/shard_map/ppermute | solution.py:16
  65.7 7.5 %collective-permute-start.5 = (bf16[256,512]{1,0:T(8,128)(2,1)S(1)}, bf16[256,512]{1,0:T(8,128)(2,1)S(1)}, u32[]{:S(2)}, u32[]{:S(2)}) collective-permute-start(bf16[256,512]{1,0:T(8,128)(2,1)S(1)} %collective-permute-done.4.refs_6_), channel_id=1, source_target_pairs={{0,1},{1,0},{2,3},{3,2},{4,5},{5,4},{6,7},{7,6},{8,9},{9,8},{10,11... | collective-permute-start | bytes 786440 | tf_op jit(solution)/shard_map/ppermute | solution.py:16
  71.7 30.0 %collective-permute-start.39 = (bf16[64,2048]{1,0:T(8,128)(2,1)}, bf16[64,2048]{1,0:T(8,128)(2,1)}, u32[]{:S(2)}, u32[]{:S(2)}) collective-permute-start(bf16[64,2048]{1,0:T(8,128)(2,1)} %get-tuple-element.60), channel_id=1, source_target_pairs={{0,4},{4,0},{8,12},{12,8},{16,20},{20,16},{24,28},{28,24},{1,5},{5... | collective-permute-start | bytes 786440 | tf_op jit(solution)/shard_map/ppermute | solution.py:16
  73.1 29.9 %collective-permute-start.41 = (bf16[64,2048]{1,0:T(8,128)(2,1)}, bf16[64,2048]{1,0:T(8,128)(2,1)}, u32[]{:S(2)}, u32[]{:S(2)}) collective-permute-start(bf16[64,2048]{1,0:T(8,128)(2,1)} %get-tuple-element.61), channel_id=1, source_target_pairs={{0,4},{4,0},{8,12},{12,8},{16,20},{20,16},{24,28},{28,24},{1,5},{5... | collective-permute-start | bytes 786440 | tf_op jit(solution)/shard_map/ppermute | solution.py:16
  75.3 19.5 %collective-permute-start.9 = (bf16[10,512]{1,0:T(8,128)(2,1)}, bf16[10,512]{1,0:T(8,128)(2,1)S(1)}, u32[]{:S(2)}, u32[]{:S(2)}) collective-permute-start(bf16[10,512]{1,0:T(8,128)(2,1)} %bitcast.26), channel_id=1, source_target_pairs={{0,2},{1,3},{2,0},{3,1},{4,6},{5,7},{6,4},{7,5},{8,10},{9,11},{10,... | collective-permute-start | bytes 30728 | tf_op jit(solution)/shard_map/ppermute | solution.py:16
  76.7 57.1 %collective-permute-start.21 = (bf16[144,2048]{1,0:T(8,128)(2,1)}, bf16[144,2048]{1,0:T(8,128)(2,1)}, u32[]{:S(2)}, u32[]{:S(2)}) collective-permute-start(bf16[144,2048]{1,0:T(8,128)(2,1)} %get-tuple-element.47), channel_id=1, source_target_pairs={{0,4},{4,0},{8,12},{12,8},{16,20},{20,16},{24,28},{28,24},{1,5},{5... | collective-permute-start | bytes 1769480 | tf_op jit(solution)/shard_map/ppermute | solution.py:16
  103.0 10.6 %collective-permute-start.24 = (bf16[80,2048]{1,0:T(8,128)(2,1)S(1)}, bf16[80,2048]{1,0:T(8,128)(2,1)S(1)}, u32[]{:S(2)}, u32[]{:S(2)}) collective-permute-start(bf16[80,2048]{1,0:T(8,128)(2,1)S(1)} %copy-done.47), channel_id=1, source_target_pairs={{0,4},{4,0},{8,12},{12,8},{16,20},{20,16},{24,28},{28,24},{1,5},{5... | collective-permute-start | bytes 983048 | tf_op jit(solution)/shard_map/ppermute | solution.py:16
  103.6 16.7 %collective-permute-start.27 = (bf16[80,2048]{1,0:T(8,128)(2,1)S(1)}, bf16[80,2048]{1,0:T(8,128)(2,1)S(1)}, u32[]{:S(2)}, u32[]{:S(2)}) collective-permute-start(bf16[80,2048]{1,0:T(8,128)(2,1)S(1)} %copy-done.46), channel_id=1, source_target_pairs={{0,4},{4,0},{8,12},{12,8},{16,20},{20,16},{24,28},{28,24},{1,5},{5... | collective-permute-start | bytes 983048 | tf_op jit(solution)/shard_map/ppermute | solution.py:16
  105.3 21.3 %collective-permute-start.40 = (bf16[64,2048]{1,0:T(8,128)(2,1)}, bf16[64,2048]{1,0:T(8,128)(2,1)}, u32[]{:S(2)}, u32[]{:S(2)}) collective-permute-start(bf16[64,2048]{1,0:T(8,128)(2,1)} %collective-permute-done.39), channel_id=1, source_target_pairs={{0,16},{4,20},{8,24},{12,28},{16,0},{20,4},{24,8},{28,12},{1,17},{... | collective-permute-start | bytes 786440 | tf_op jit(solution)/shard_map/ppermute | solution.py:16
  107.9 18.7 %collective-permute-start.42 = (bf16[64,2048]{1,0:T(8,128)(2,1)}, bf16[64,2048]{1,0:T(8,128)(2,1)}, u32[]{:S(2)}, u32[]{:S(2)}) collective-permute-start(bf16[64,2048]{1,0:T(8,128)(2,1)} %collective-permute-done.41), channel_id=1, source_target_pairs={{0,24},{4,28},{8,16},{12,20},{16,8},{20,12},{24,0},{28,4},{1,25},{... | collective-permute-start | bytes 786440 | tf_op jit(solution)/shard_map/ppermute | solution.py:16
  113.6 8.0 %collective-permute-start.13 = (f32[20,256]{1,0:T(8,128)S(1)}, f32[20,256]{1,0:T(8,128)S(1)}, u32[]{:S(2)}, u32[]{:S(2)}) collective-permute-start(f32[20,256]{1,0:T(8,128)S(1)} %pad_maximum_fusion.2.refs_0_), channel_id=1, source_target_pairs={{0,4},{4,0},{8,12},{12,8},{16,20},{20,16},{24,28},{28,24},{1,5},{5... | collective-permute-start | bytes 61448 | tf_op jit(solution)/shard_map/ppermute | solution.py:16
  121.1 28.4 %collective-permute-start.19 = (bf16[144,2048]{1,0:T(8,128)(2,1)}, bf16[144,2048]{1,0:T(8,128)(2,1)S(1)}, u32[]{:S(2)}, u32[]{:S(2)}) collective-permute-start(bf16[144,2048]{1,0:T(8,128)(2,1)} %get-tuple-element.45), channel_id=1, source_target_pairs={{0,4},{4,0},{8,12},{12,8},{16,20},{20,16},{24,28},{28,24},{1,5},{5... | collective-permute-start | bytes 1769480 | tf_op jit(solution)/shard_map/ppermute | solution.py:16
  121.6 32.3 %collective-permute-start.20 = (bf16[144,2048]{1,0:T(8,128)(2,1)}, bf16[144,2048]{1,0:T(8,128)(2,1)S(1)}, u32[]{:S(2)}, u32[]{:S(2)}) collective-permute-start(bf16[144,2048]{1,0:T(8,128)(2,1)} %get-tuple-element.46), channel_id=1, source_target_pairs={{0,8},{4,12},{8,0},{12,4},{16,24},{20,28},{24,16},{28,20},{1,9},{5... | collective-permute-start | bytes 1769480 | tf_op jit(solution)/shard_map/ppermute | solution.py:16
  126.7 13.6 %collective-permute-start.14 = (f32[40,256]{1,0:T(8,128)S(1)}, f32[40,256]{1,0:T(8,128)S(1)}, u32[]{:S(2)}, u32[]{:S(2)}) collective-permute-start(f32[40,256]{1,0:T(8,128)S(1)} %pad_maximum_fusion), channel_id=1, source_target_pairs={{0,8},{4,12},{8,0},{12,4},{16,24},{20,28},{24,16},{28,20},{1,9},{5... | collective-permute-start | bytes 122888 | tf_op jit(solution)/shard_map/ppermute | solution.py:16
  126.7 17.5 %collective-permute-start.15 = (f32[40,256]{1,0:T(8,128)S(1)}, f32[40,256]{1,0:T(8,128)S(1)}, u32[]{:S(2)}, u32[]{:S(2)}) collective-permute-start(f32[40,256]{1,0:T(8,128)S(1)} %pad_maximum_fusion), channel_id=1, source_target_pairs={{0,16},{4,20},{8,24},{12,28},{16,0},{20,4},{24,8},{28,12},{1,17},{... | collective-permute-start | bytes 122888 | tf_op jit(solution)/shard_map/ppermute | solution.py:16
  133.8 10.4 %collective-permute-start.16 = (f32[40,256]{1,0:T(8,128)S(1)}, f32[40,256]{1,0:T(8,128)S(1)}, u32[]{:S(2)}, u32[]{:S(2)}) collective-permute-start(f32[40,256]{1,0:T(8,128)S(1)} %pad_maximum_fusion), channel_id=1, source_target_pairs={{0,24},{4,28},{8,16},{12,20},{16,8},{20,12},{24,0},{28,4},{1,25},{... | collective-permute-start | bytes 122888 | tf_op jit(solution)/shard_map/ppermute | solution.py:16
  140.3 22.2 %collective-permute-start.26 = (bf16[144,2048]{1,0:T(8,128)(2,1)}, bf16[144,2048]{1,0:T(8,128)(2,1)S(1)}, u32[]{:S(2)}, u32[]{:S(2)}) collective-permute-start(bf16[144,2048]{1,0:T(8,128)(2,1)} %get-tuple-element.49), channel_id=1, source_target_pairs={{0,24},{4,28},{8,16},{12,20},{16,8},{20,12},{24,0},{28,4},{1,25},{... | collective-permute-start | bytes 1769480 | tf_op jit(solution)/shard_map/ppermute | solution.py:16
  144.2 64.4 %collective-permute-start.23 = (bf16[144,2048]{1,0:T(8,128)(2,1)}, bf16[144,2048]{1,0:T(8,128)(2,1)S(1)}, u32[]{:S(2)}, u32[]{:S(2)}) collective-permute-start(bf16[144,2048]{1,0:T(8,128)(2,1)} %shard_map.101), channel_id=1, source_target_pairs={{0,16},{4,20},{8,24},{12,28},{16,0},{20,4},{24,8},{28,12},{1,17},{... | collective-permute-start | bytes 1769480 | tf_op jit(solution)/shard_map/ppermute | solution.py:16
  144.2 64.4 %collective-permute-start.22 = (bf16[144,2048]{1,0:T(8,128)(2,1)}, bf16[144,2048]{1,0:T(8,128)(2,1)S(1)}, u32[]{:S(2)}, u32[]{:S(2)}) collective-permute-start(bf16[144,2048]{1,0:T(8,128)(2,1)} %collective-permute-done.21), channel_id=1, source_target_pairs={{0,8},{4,12},{8,0},{12,4},{16,24},{20,28},{24,16},{28,20},{1,9},{5... | collective-permute-start | bytes 1769480 | tf_op jit(solution)/shard_map/ppermute | solution.py:16
  150.9 76.9 %collective-permute-start.25 = (bf16[80,2048]{1,0:T(8,128)(2,1)}, bf16[80,2048]{1,0:T(8,128)(2,1)S(1)}, u32[]{:S(2)}, u32[]{:S(2)}) collective-permute-start(bf16[80,2048]{1,0:T(8,128)(2,1)} %copy-done.44), channel_id=1, source_target_pairs={{0,16},{4,20},{8,24},{12,28},{16,0},{20,4},{24,8},{28,12},{1,17},{... | collective-permute-start | bytes 983048 | tf_op jit(solution)/shard_map/ppermute | solution.py:16
  158.3 70.6 %collective-permute-start.28 = (bf16[80,2048]{1,0:T(8,128)(2,1)}, bf16[80,2048]{1,0:T(8,128)(2,1)}, u32[]{:S(2)}, u32[]{:S(2)}) collective-permute-start(bf16[80,2048]{1,0:T(8,128)(2,1)} %copy-done.45), channel_id=1, source_target_pairs={{0,24},{4,28},{8,16},{12,20},{16,8},{20,12},{24,0},{28,4},{1,25},{... | collective-permute-start | bytes 983048 | tf_op jit(solution)/shard_map/ppermute | solution.py:16
  214.6 22.9 %collective-permute-start.43 = (bf16[64,2048]{1,0:T(8,128)(2,1)}, bf16[64,2048]{1,0:T(8,128)(2,1)S(1)}, u32[]{:S(2)}, u32[]{:S(2)}) collective-permute-start(bf16[64,2048]{1,0:T(8,128)(2,1)} %get-tuple-element.63), channel_id=1, source_target_pairs={{0,4},{4,0},{8,12},{12,8},{16,20},{20,16},{24,28},{28,24},{1,5},{5... | collective-permute-start | bytes 786440 | tf_op jit(solution)/shard_map/ppermute | solution.py:16
  215.2 23.5 %collective-permute-start.44 = (bf16[64,2048]{1,0:T(8,128)(2,1)}, bf16[64,2048]{1,0:T(8,128)(2,1)S(1)}, u32[]{:S(2)}, u32[]{:S(2)}) collective-permute-start(bf16[64,2048]{1,0:T(8,128)(2,1)} %get-tuple-element.64), channel_id=1, source_target_pairs={{0,8},{4,12},{8,0},{12,4},{16,24},{20,28},{24,16},{28,20},{1,9},{5... | collective-permute-start | bytes 786440 | tf_op jit(solution)/shard_map/ppermute | solution.py:16
  226.4 9.0 %collective-permute-start.55 = (bf16[40,512]{1,0:T(8,128)(2,1)S(1)}, bf16[40,512]{1,0:T(8,128)(2,1)S(1)}, u32[]{:S(2)}, u32[]{:S(2)}) collective-permute-start(bf16[40,512]{1,0:T(8,128)(2,1)S(1)} %pad_maximum_fusion.1), channel_id=1, source_target_pairs={{0,16},{4,20},{8,24},{12,28},{16,0},{20,4},{24,8},{28,12},{1,17},{... | collective-permute-start | bytes 122888 | tf_op jit(solution)/shard_map/ppermute | solution.py:16
  227.8 8.8 %collective-permute-start.56 = (bf16[40,512]{1,0:T(8,128)(2,1)S(1)}, bf16[40,512]{1,0:T(8,128)(2,1)S(1)}, u32[]{:S(2)}, u32[]{:S(2)}) collective-permute-start(bf16[40,512]{1,0:T(8,128)(2,1)S(1)} %pad_maximum_fusion.1), channel_id=1, source_target_pairs={{0,24},{4,28},{8,16},{12,20},{16,8},{20,12},{24,0},{28,4},{1,25},{... | collective-permute-start | bytes 122888 | tf_op jit(solution)/shard_map/ppermute | solution.py:16
  228.9 10.6 %collective-permute-start.47 = (bf16[64,2048]{1,0:T(8,128)(2,1)}, bf16[64,2048]{1,0:T(8,128)(2,1)S(1)}, u32[]{:S(2)}, u32[]{:S(2)}) collective-permute-start(bf16[64,2048]{1,0:T(8,128)(2,1)} %get-tuple-element.68), channel_id=1, source_target_pairs={{0,4},{4,0},{8,12},{12,8},{16,20},{20,16},{24,28},{28,24},{1,5},{5... | collective-permute-start | bytes 786440 | tf_op jit(solution)/shard_map/ppermute | solution.py:16
  235.4 10.9 %collective-permute-start.31 = (bf16[80,2048]{1,0:T(8,128)(2,1)}, bf16[80,2048]{1,0:T(8,128)(2,1)S(1)}, u32[]{:S(2)}, u32[]{:S(2)}) collective-permute-start(bf16[80,2048]{1,0:T(8,128)(2,1)} %get-tuple-element.54), channel_id=1, source_target_pairs={{0,4},{4,0},{8,12},{12,8},{16,20},{20,16},{24,28},{28,24},{1,5},{5... | collective-permute-start | bytes 983048 | tf_op jit(solution)/shard_map/ppermute | solution.py:16
  236.6 16.7 %collective-permute-start.34 = (bf16[80,2048]{1,0:T(8,128)(2,1)}, bf16[80,2048]{1,0:T(8,128)(2,1)S(1)}, u32[]{:S(2)}, u32[]{:S(2)}) collective-permute-start(bf16[80,2048]{1,0:T(8,128)(2,1)} %get-tuple-element.56), channel_id=1, source_target_pairs={{0,4},{4,0},{8,12},{12,8},{16,20},{20,16},{24,28},{28,24},{1,5},{5... | collective-permute-start | bytes 983048 | tf_op jit(solution)/shard_map/ppermute | solution.py:16
  237.5 22.6 %collective-permute-start.37 = (bf16[80,2048]{1,0:T(8,128)(2,1)}, bf16[80,2048]{1,0:T(8,128)(2,1)S(1)}, u32[]{:S(2)}, u32[]{:S(2)}) collective-permute-start(bf16[80,2048]{1,0:T(8,128)(2,1)} %get-tuple-element.58), channel_id=1, source_target_pairs={{0,4},{4,0},{8,12},{12,8},{16,20},{20,16},{24,28},{28,24},{1,5},{5... | collective-permute-start | bytes 983048 | tf_op jit(solution)/shard_map/ppermute | solution.py:16
  238.7 24.9 %collective-permute-start.29 = (bf16[80,2048]{1,0:T(8,128)(2,1)}, bf16[80,2048]{1,0:T(8,128)(2,1)S(1)}, u32[]{:S(2)}, u32[]{:S(2)}) collective-permute-start(bf16[80,2048]{1,0:T(8,128)(2,1)} %get-tuple-element.52), channel_id=1, source_target_pairs={{0,4},{4,0},{8,12},{12,8},{16,20},{20,16},{24,28},{28,24},{1,5},{5... | collective-permute-start | bytes 983048 | tf_op jit(solution)/shard_map/ppermute | solution.py:16
  240.2 25.3 %collective-permute-start.30 = (bf16[80,2048]{1,0:T(8,128)(2,1)}, bf16[80,2048]{1,0:T(8,128)(2,1)S(1)}, u32[]{:S(2)}, u32[]{:S(2)}) collective-permute-start(bf16[80,2048]{1,0:T(8,128)(2,1)} %get-tuple-element.53), channel_id=1, source_target_pairs={{0,8},{4,12},{8,0},{12,4},{16,24},{20,28},{24,16},{28,20},{1,9},{5... | collective-permute-start | bytes 983048 | tf_op jit(solution)/shard_map/ppermute | solution.py:16
  246.3 25.8 %collective-permute-start.33 = (bf16[80,2048]{1,0:T(8,128)(2,1)}, bf16[80,2048]{1,0:T(8,128)(2,1)S(1)}, u32[]{:S(2)}, u32[]{:S(2)}) collective-permute-start(bf16[80,2048]{1,0:T(8,128)(2,1)} %get-tuple-element.55), channel_id=1, source_target_pairs={{0,16},{4,20},{8,24},{12,28},{16,0},{20,4},{24,8},{28,12},{1,17},{... | collective-permute-start | bytes 983048 | tf_op jit(solution)/shard_map/ppermute | solution.py:16
  253.3 32.3 %collective-permute-start.36 = (bf16[80,2048]{1,0:T(8,128)(2,1)}, bf16[80,2048]{1,0:T(8,128)(2,1)S(1)}, u32[]{:S(2)}, u32[]{:S(2)}) collective-permute-start(bf16[80,2048]{1,0:T(8,128)(2,1)} %get-tuple-element.57), channel_id=1, source_target_pairs={{0,24},{4,28},{8,16},{12,20},{16,8},{20,12},{24,0},{28,4},{1,25},{... | collective-permute-start | bytes 983048 | tf_op jit(solution)/shard_map/ppermute | solution.py:16
  260.1 25.6 %collective-permute-start.32 = (bf16[80,2048]{1,0:T(8,128)(2,1)S(1)}, bf16[80,2048]{1,0:T(8,128)(2,1)S(1)}, u32[]{:S(2)}, u32[]{:S(2)}) collective-permute-start(bf16[80,2048]{1,0:T(8,128)(2,1)S(1)} %collective-permute-done.31), channel_id=1, source_target_pairs={{0,8},{4,12},{8,0},{12,4},{16,24},{20,28},{24,16},{28,20},{1,9},{5... | collective-permute-start | bytes 983048 | tf_op jit(solution)/shard_map/ppermute | solution.py:16
  263.6 41.2 %collective-permute-start.35 = (bf16[80,2048]{1,0:T(8,128)(2,1)S(1)}, bf16[80,2048]{1,0:T(8,128)(2,1)S(1)}, u32[]{:S(2)}, u32[]{:S(2)}) collective-permute-start(bf16[80,2048]{1,0:T(8,128)(2,1)S(1)} %collective-permute-done.34), channel_id=1, source_target_pairs={{0,16},{4,20},{8,24},{12,28},{16,0},{20,4},{24,8},{28,12},{1,17},{... | collective-permute-start | bytes 983048 | tf_op jit(solution)/shard_map/ppermute | solution.py:16
  265.5 41.6 %collective-permute-start.38 = (bf16[80,2048]{1,0:T(8,128)(2,1)S(1)}, bf16[80,2048]{1,0:T(8,128)(2,1)S(1)}, u32[]{:S(2)}, u32[]{:S(2)}) collective-permute-start(bf16[80,2048]{1,0:T(8,128)(2,1)S(1)} %collective-permute-done.37), channel_id=1, source_target_pairs={{0,24},{4,28},{8,16},{12,20},{16,8},{20,12},{24,0},{28,4},{1,25},{... | collective-permute-start | bytes 983048 | tf_op jit(solution)/shard_map/ppermute | solution.py:16
  272.0 54.2 %collective-permute-start.49 = (bf16[64,2048]{1,0:T(8,128)(2,1)}, bf16[64,2048]{1,0:T(8,128)(2,1)}, u32[]{:S(2)}, u32[]{:S(2)}) collective-permute-start(bf16[64,2048]{1,0:T(8,128)(2,1)} %get-tuple-element.69), channel_id=1, source_target_pairs={{0,4},{4,0},{8,12},{12,8},{16,20},{20,16},{24,28},{28,24},{1,5},{5... | collective-permute-start | bytes 786440 | tf_op jit(solution)/shard_map/ppermute | solution.py:16
  285.6 40.7 %collective-permute-start.51 = (bf16[64,2048]{1,0:T(8,128)(2,1)}, bf16[64,2048]{1,0:T(8,128)(2,1)}, u32[]{:S(2)}, u32[]{:S(2)}) collective-permute-start(bf16[64,2048]{1,0:T(8,128)(2,1)} %get-tuple-element.70), channel_id=1, source_target_pairs={{0,4},{4,0},{8,12},{12,8},{16,20},{20,16},{24,28},{28,24},{1,5},{5... | collective-permute-start | bytes 786440 | tf_op jit(solution)/shard_map/ppermute | solution.py:16
  285.7 43.0 %collective-permute-start.45 = (bf16[64,2048]{1,0:T(8,128)(2,1)}, bf16[64,2048]{1,0:T(8,128)(2,1)S(1)}, u32[]{:S(2)}, u32[]{:S(2)}) collective-permute-start(bf16[64,2048]{1,0:T(8,128)(2,1)} %get-tuple-element.65), channel_id=1, source_target_pairs={{0,16},{4,20},{8,24},{12,28},{16,0},{20,4},{24,8},{28,12},{1,17},{... | collective-permute-start | bytes 786440 | tf_op jit(solution)/shard_map/ppermute | solution.py:16
  304.8 27.7 %collective-permute-start.46 = (bf16[64,2048]{1,0:T(8,128)(2,1)}, bf16[64,2048]{1,0:T(8,128)(2,1)}, u32[]{:S(2)}, u32[]{:S(2)}) collective-permute-start(bf16[64,2048]{1,0:T(8,128)(2,1)} %get-tuple-element.67), channel_id=1, source_target_pairs={{0,24},{4,28},{8,16},{12,20},{16,8},{20,12},{24,0},{28,4},{1,25},{... | collective-permute-start | bytes 786440 | tf_op jit(solution)/shard_map/ppermute | solution.py:16
  307.1 34.0 %collective-permute-start.48 = (bf16[64,2048]{1,0:T(8,128)(2,1)}, bf16[64,2048]{1,0:T(8,128)(2,1)}, u32[]{:S(2)}, u32[]{:S(2)}) collective-permute-start(bf16[64,2048]{1,0:T(8,128)(2,1)} %copy-done.48), channel_id=1, source_target_pairs={{0,16},{4,20},{8,24},{12,28},{16,0},{20,4},{24,8},{28,12},{1,17},{... | collective-permute-start | bytes 786440 | tf_op jit(solution)/shard_map/ppermute | solution.py:16
  326.2 16.6 %collective-permute-start.50 = (bf16[64,2048]{1,0:T(8,128)(2,1)}, bf16[64,2048]{1,0:T(8,128)(2,1)S(1)}, u32[]{:S(2)}, u32[]{:S(2)}) collective-permute-start(bf16[64,2048]{1,0:T(8,128)(2,1)} %collective-permute-done.49), channel_id=1, source_target_pairs={{0,8},{4,12},{8,0},{12,4},{16,24},{20,28},{24,16},{28,20},{1,9},{5... | collective-permute-start | bytes 786440 | tf_op jit(solution)/shard_map/ppermute | solution.py:16
  326.3 17.2 %collective-permute-start.52 = (bf16[64,2048]{1,0:T(8,128)(2,1)}, bf16[64,2048]{1,0:T(8,128)(2,1)S(1)}, u32[]{:S(2)}, u32[]{:S(2)}) collective-permute-start(bf16[64,2048]{1,0:T(8,128)(2,1)} %collective-permute-done.51), channel_id=1, source_target_pairs={{0,24},{4,28},{8,16},{12,20},{16,8},{20,12},{24,0},{28,4},{1,25},{... | collective-permute-start | bytes 786440 | tf_op jit(solution)/shard_map/ppermute | solution.py:16
  (58 other events, 1378.5 us)

commit v3 on v2

--- a/solution.py
+++ b/solution.py
@@ -7,6 +7,7 @@
 
 
 GROUP = 16
+VMEM_GRANT = 65300 * 1024
 WIDEST = 256
 precise = lax.Precision.HIGHEST
 MEMBER, DP = "member", "dp"
@@ -16,8 +17,10 @@
     return lax.ppermute(value, axis, [(i, i ^ k) for i in range(size)])
 
 
-def launch(kernel, **settings):
-    return pl.pallas_call(kernel, **settings)
+def launch(kernel, grant=None, **settings):
+    return pl.pallas_call(
+        kernel, compiler_params=pltpu.CompilerParams(vmem_limit_bytes=grant), **settings
+    )
 
 
 def bits_of(size):
@@ -226,6 +229,7 @@
 
     return launch(
         kernel,
+        VMEM_GRANT,
         grid=(columns // block,),
         in_specs=[pl.BlockSpec(weights.shape, lambda i: (0, 0))]
         + [pl.BlockSpec((slots * rows, block), lambda i, at=at: (at, i)) for _, at in pieces]
@@ -424,7 +428,7 @@
 
     def kernel(*refs):
         observed_ref, out_ref = refs[count:]
-        parts = [(ref[...], n) for ref, n in zip(refs, counts)]
+        parts = [(ref[...], n) for ref, n in zip(refs[:count], counts)]
         values = jnp.concatenate(
             [
                 jnp.concatenate(
@@ -446,7 +450,9 @@
         )
 
     return launch(
-        kernel, out_shape=jax.ShapeDtypeStruct((side, side), jnp.float32)
+        kernel,
+        in_specs=[pl.BlockSpec(memory_space=pltpu.VMEM)] * (count + 1),
+        out_shape=jax.ShapeDtypeStruct((side, side), jnp.float32),
     )(*every, observed)
 
 
@@ -477,11 +483,28 @@
         out_ref[...] = same + mixing - jnp.sum(mixing, axis=0, keepdims=True) / ensemble
 
     return launch(
-        kernel, out_shape=jax.ShapeDtypeStruct((ensemble, ensemble), jnp.float32)
+        kernel,
+        VMEM_GRANT,
+        in_specs=[pl.BlockSpec(memory_space=pltpu.VMEM)] * 2,
+        out_shape=jax.ShapeDtypeStruct((ensemble, ensemble), jnp.float32),
     )(both, other)
 
 
-def combine(weights, values, classes):
+def doubled(value, size):
+    have, order = [value], [0]
+    for bit in doubling(size):
+        stack = jnp.concatenate(have, axis=0) if len(have) > 1 else have[0]
+        have = have + [swap(stack, MEMBER, size, bit)]
+        order = order + [k ^ bit for k in order]
+    return have, order
+
+
+def doubling(size):
+    bits = bits_of(size)
+    return bits[:1] + bits[:0:-1]
+
+
+def combine(weights, values, order, classes):
     slots = weights.shape[1]
     count = len(values)
     width = values[0].shape[1]
@@ -492,8 +515,9 @@
         for ref in refs[:count]:
             rows = ref[...].astype(jnp.float32)
             for i in range(0, rows.shape[0], classes):
+                at = order[k // slots] * slots + k % slots
                 for s in range(slots):
-                    totals[s] += weights_ref[k, s] * rows[i : i + classes]
+                    totals[s] += weights_ref[at, s] * rows[i : i + classes]
                 k += 1
         for s in range(slots):
             out_ref[s] = totals[s].astype(out_ref.dtype)
@@ -520,12 +544,11 @@
 
 
 def evens(members):
-    half = members // 2
-    return [half] + [k for k in range(2, members, 2) if k != half]
+    return list(range(2, members, 2))
 
 
 def held(members):
-    return evens(members)[:1] + evens(members)[-1:]
+    return [members // 2, members - 2]
 
 
 def on_device(
@@ -567,7 +590,7 @@
 
     each = range(members)
     wait = [k + 1 for k in held(members)]
-    head = evens(members)[0]
+    head = held(members)[0]
     others = [k for k in each if k != head]
     cut = cut_pieces(place, middle_blocks, first_blocks, [(head, 1, 1)])
     cut += cut_pieces(
@@ -604,8 +627,10 @@
         members,
     )
     last_flipped = jnp.transpose(last_weight, (0, 2, 1)).reshape(-1, last_weight.shape[1])
-    last_all = gather_members(last_flipped, members)
-    new_last = jnp.transpose(combine(weights[:, :slots], last_all, classes_total), (0, 2, 1))
+    last_all, order = doubled(last_flipped, members)
+    new_last = jnp.transpose(
+        combine(weights[:, :slots], last_all, order, classes_total), (0, 2, 1)
+    )
 
     new_middle, new_first = join_early(
         place, middle_blocks.shape, first_blocks.shape, early_back

time: 346 us -> 362 us (1.046)
  waiting for transfers between devices: 168 us -> 188 us
  local copies, waits for them, and re-layouts: 20 us -> 13.6 us
    ppermute x57 -> x56, waiting for transfers between devices: 168 us -> 188 us  [swap(): return lax.ppermute(value, axis, [(i, i ^ k) for i in range(size)])]
    ppermute x57 -> x56, starting transfers between devices: 96.6 us -> 99.2 us  [swap(): return lax.ppermute(value, axis, [(i, i ^ k) for i in range(size)])]
    unnamed x101 -> x77, local copies, waits for them, and re-layouts: 7.74 us -> 6.79 us
  transfers between devices with their start and end apart: 57 -> 56, of which waited for: 20 -> 20; matrix products, arithmetic and copies ran while one was open for 5% -> 3% of each run, Pallas kernels for 15% -> 13%
where the time goes in v3:
time: 362 us; the launch traced here: 360 us
  waiting for transfers between devices  188 us (52%)
  starting transfers between devices  99.2 us (27%)
  Pallas kernels  55.4 us (15%)
  local copies, waits for them, and re-layouts  13.6 us (4%)
    ppermute x56, waiting for transfers between devices, swap(): return lax.ppermute(value, axis, [(i, i ^ k) for i in range(size)])  188 us
    ppermute x56, starting transfers between devices, swap(): return lax.ppermute(value, axis, [(i, i ^ k) for i in range(size)])  99.2 us
    pallas_call x5, Pallas kernels, copies(): launch(kernel, in_specs=[pl.BlockSpec(memory_space=pltpu.SMEM)] + [anywhe...  19.7 us
    pallas_call x2, Pallas kernels, update_pieces(): launch(kernel, VMEM_GRANT, grid=(columns // block,), in_specs=[pl.BlockSp...  10.4 us
    pallas_call x1, Pallas kernels, layer_two(): launch(kernel, grid_spec=pltpu.PrefetchScalarGridSpec(num_scalar_prefetch...  8.43 us
  transfers between devices with their start and end apart: 56, of which 20 were waited for; matrix products, arithmetic and copies ran while one was open for 3% of the time, Pallas kernels for 13%

profile of v3, /device:TPU:0, one launch (start us, length us, event | category | flops | bytes accessed | tf_op | source)
XLA Modules:
  0.0 360.5 jit_solution(14334431253252425953)
XLA Ops:
  1.4 4.0 %shard_map.95 = (bf16[512,1024]{1,0:T(8,128)(2,1)}, bf16[512,1024]{1,0:T(8,128)(2,1)}, bf16[512,1024]{1,0:T(8,128)(2,1)}) custom-call(s32[2]{0:T(128)} %pad_add_fusion.place_ref, bf16[2,512,2048]{2,1,0:T(8,128)(2,1)} %refs_4_.1), custom_call_target="tpu_custom_call" | custom-call | tf_op jit(solution)/shard_map/pallas_call | solution.py:75
  5.9 2.6 collective-permute-start.7
  9.8 2.0 collective-permute-start.1
  11.9 45.9 %collective-permute-done.1.refs_2_ = bf16[256,256]{1,0:T(8,128)(2,1)S(1)} collective-permute-done((bf16[256,256]{1,0:T(8,128)(2,1)S(1)}, bf16[256,256]{1,0:T(8,128)(2,1)S(1)}, u32[]{:S(2)}, u32[]{:S(2)}) %collective-permute-start.1) | collective-permute-done | bytes 131104 | tf_op jit(solution)/shard_map/ppermute | solution.py:17
  57.8 1.7 collective-permute-start.4
  59.5 6.3 %collective-permute-done.4.refs_6_ = bf16[256,512]{1,0:T(8,128)(2,1)S(1)} collective-permute-done((bf16[256,512]{1,0:T(8,128)(2,1)S(1)}, bf16[256,512]{1,0:T(8,128)(2,1)S(1)}, u32[]{:S(2)}, u32[]{:S(2)}) %collective-permute-start.4) | collective-permute-done | bytes 262176 | tf_op jit(solution)/shard_map/ppermute | solution.py:17
  71.2 4.9 %shard_map.94.refs_0_.refs_1_.refs_2_.hidden_ref = bf16[4,256,2048]{2,1,0:T(8,128)(2,1)} custom-call(bf16[256,256]{1,0:T(8,128)(2,1)} %copy-done.6, bf16[256,256]{1,0:T(8,128)(2,1)} %copy-done.23, bf16[256,256]{1,0:T(8,128)(2,1)} %copy-done.22, bf16[256,256]{1,0:T(8,128)(2,1)} %copy-done.24, bf16[256,512]{1,0:T(8,128)(2,1)} %copy-done.5, ...), custom_call_target="tpu_custom_call" | custom-call | tf_op jit(solution)/shard_map/pallas_call | solution.py:258
  78.2 8.4 %shard_map.96.total_ref = f32[4,256,1024]{2,1,0:T(8,128)} custom-call(s32[2]{0:T(128)} %pad_add_fusion.place_ref, bf16[4,256,2048]{2,1,0:T(8,128)(2,1)} %shard_map.94.refs_0_.refs_1_.refs_2_.hidden_ref, bf16[4,256,2048]{2,1,0:T(8,128)(2,1)} %shard_map.94.refs_0_.refs_1_.refs_2_.hidden_ref, ...), custom_call_target="tpu_custom_call" | custom-call | tf_op jit(solution)/shard_map/pallas_call | solution.py:291
  87.2 5.6 %shard_map.97 = (f32[10,256]{1,0:T(8,128)}, f32[10,256]{1,0:T(8,128)}, f32[10,256]{1,0:T(8,128)}, f32[10,256]{1,0:T(8,128)}) custom-call(bf16[4,256,2048]{2,1,0:T(8,128)(2,1)} %shard_map.94.refs_0_.refs_1_.refs_2_.hidden_ref, f32[4,256,1024]{2,1,0:T(8,128)} %shard_map.96.total_ref, bf16[512,1024]{1,0:T(8,128)(2,1)} %collective-permute-done.8.array_ref, ...), custom_call_target="tpu_custom_call" | custom-call | tf_op jit(solution)/shard_map/pallas_call | solution.py:331
  94.8 5.5 %shard_map.100 = (bf16[144,2048]{1,0:T(8,128)(2,1)}, bf16[144,2048]{1,0:T(8,128)(2,1)}, bf16[144,2048]{1,0:T(8,128)(2,1)}, bf16[144,2048]{1,0:T(8,128)(2,1)}, bf...) custom-call(s32[2]{0:T(128)} %pad_add_fusion.place_ref, ...), custom_call_target="tpu_custom_call" | custom-call | tf_op jit(solution)/shard_map/pallas_call | solution.py:75
  106.0 16.4 %collective-permute-done.39 = bf16[64,2048]{1,0:T(8,128)(2,1)S(1)} collective-permute-done((bf16[64,2048]{1,0:T(8,128)(2,1)}, bf16[64,2048]{1,0:T(8,128)(2,1)S(1)}, u32[]{:S(2)}, u32[]{:S(2)}) %collective-permute-start.39) | collective-permute-done | bytes 262176 | tf_op jit(solution)/shard_map/ppermute | solution.py:17
  123.9 4.1 %collective-permute-done.41 = bf16[64,2048]{1,0:T(8,128)(2,1)S(1)} collective-permute-done((bf16[64,2048]{1,0:T(8,128)(2,1)}, bf16[64,2048]{1,0:T(8,128)(2,1)S(1)}, u32[]{:S(2)}, u32[]{:S(2)}) %collective-permute-start.41) | collective-permute-done | bytes 262176 | tf_op jit(solution)/shard_map/ppermute | solution.py:17
  128.1 2.6 collective-permute-start.40
  130.7 11.4 %collective-permute-done.13.refs_1_ = f32[20,256]{1,0:T(8,128)S(1)} collective-permute-done((f32[20,256]{1,0:T(8,128)S(1)}, f32[20,256]{1,0:T(8,128)S(1)}, u32[]{:S(2)}, u32[]{:S(2)}) %collective-permute-start.13) | collective-permute-done | bytes 20512 | tf_op jit(solution)/shard_map/ppermute | solution.py:17
  142.0 3.6 %collective-permute-start.42 = (bf16[64,2048]{1,0:T(8,128)(2,1)S(1)}, bf16[64,2048]{1,0:T(8,128)(2,1)}, u32[]{:S(2)}, u32[]{:S(2)}) collective-permute-start(bf16[64,2048]{1,0:T(8,128)(2,1)S(1)} %collective-permute-done.41), channel_id=1, source_target_pairs={{0,24},{4,28},{8,16},{12,20},{16,8},{20,12},{24,0},{28,4},{1,25},{... | collective-permute-start | bytes 786440 | tf_op jit(solution)/shard_map/ppermute | solution.py:17
  146.5 3.6 %collective-permute-start.16 = (f32[40,256]{1,0:T(8,128)S(1)}, f32[40,256]{1,0:T(8,128)S(1)}, u32[]{:S(2)}, u32[]{:S(2)}) collective-permute-start(f32[40,256]{1,0:T(8,128)S(1)} %pad_maximum_fusion.1), channel_id=1, source_target_pairs={{0,24},{4,28},{8,16},{12,20},{16,8},{20,12},{24,0},{28,4},{1,25},{... | collective-permute-start | bytes 122888 | tf_op jit(solution)/shard_map/ppermute | solution.py:17
  150.1 3.0 collective-permute-done.42.refs_7_
  154.6 6.6 %collective-permute-start.20 = (bf16[144,2048]{1,0:T(8,128)(2,1)}, bf16[144,2048]{1,0:T(8,128)(2,1)}, u32[]{:S(2)}, u32[]{:S(2)}) collective-permute-start(bf16[144,2048]{1,0:T(8,128)(2,1)} %get-tuple-element.46), channel_id=1, source_target_pairs={{0,8},{4,12},{8,0},{12,4},{16,24},{20,28},{24,16},{28,20},{1,9},{5... | collective-permute-start | bytes 1769480 | tf_op jit(solution)/shard_map/ppermute | solution.py:17
  161.3 2.8 shard_map.101
  164.1 2.5 collective-permute-start.26
  166.6 1.9 collective-permute-start.22
  168.5 1.9 gather_fusion.1
  171.2 1.9 shard_map.98
  175.7 10.9 %collective-permute-done.20.refs_2_.refs_10_ = bf16[144,2048]{1,0:T(8,128)(2,1)} collective-permute-done((bf16[144,2048]{1,0:T(8,128)(2,1)}, bf16[144,2048]{1,0:T(8,128)(2,1)}, u32[]{:S(2)}, u32[]{:S(2)}) %collective-permute-start.20) | collective-permute-done | bytes 589856 | tf_op jit(solution)/shard_map/ppermute | solution.py:17
  187.1 3.2 collective-permute-done.18.second_ref
  191.6 2.7 shard_map.99.weights_ref
  194.3 3.0 collective-permute-start.28
  197.3 35.2 %collective-permute-done.23.refs_4_.refs_12_ = bf16[144,2048]{1,0:T(8,128)(2,1)} collective-permute-done((bf16[144,2048]{1,0:T(8,128)(2,1)}, bf16[144,2048]{1,0:T(8,128)(2,1)}, u32[]{:S(2)}, u32[]{:S(2)}) %collective-permute-start.23) | collective-permute-done | bytes 589856 | tf_op jit(solution)/shard_map/ppermute | solution.py:17
  232.5 4.9 %shard_map.104 = (bf16[64,2048]{1,0:T(8,128)(2,1)}, bf16[64,2048]{1,0:T(8,128)(2,1)}, bf16[64,2048]{1,0:T(8,128)(2,1)}, bf16[64,2048]{1,0:T(8,128)(2,1)}, bf16[6...) custom-call(f32[16,16]{1,0:T(8,128)} %shard_map.99.weights_ref, ...), custom_call_target="tpu_custom_call" | custom-call | tf_op jit(solution)/shard_map/pallas_call | solution.py:230
  238.1 3.1 collective-permute-start.54
  241.2 3.3 collective-permute-done.54.refs_2_
  245.1 2.5 collective-permute-start.55
  249.1 5.5 %shard_map.102 = (bf16[80,2048]{1,0:T(8,128)(2,1)}, bf16[80,2048]{1,0:T(8,128)(2,1)}, bf16[80,2048]{1,0:T(8,128)(2,1)}, bf16[80,2048]{1,0:T(8,128)(2,1)}, bf16[8...) custom-call(f32[16,16]{1,0:T(8,128)} %shard_map.99.weights_ref, ...), custom_call_target="tpu_custom_call" | custom-call | tf_op jit(solution)/shard_map/pallas_call | solution.py:230
  258.8 6.7 %collective-permute-done.31 = bf16[80,2048]{1,0:T(8,128)(2,1)S(1)} collective-permute-done((bf16[80,2048]{1,0:T(8,128)(2,1)}, bf16[80,2048]{1,0:T(8,128)(2,1)S(1)}, u32[]{:S(2)}, u32[]{:S(2)}) %collective-permute-start.31) | collective-permute-done | bytes 327712 | tf_op jit(solution)/shard_map/ppermute | solution.py:17
  265.5 7.0 %collective-permute-done.34 = bf16[80,2048]{1,0:T(8,128)(2,1)S(1)} collective-permute-done((bf16[80,2048]{1,0:T(8,128)(2,1)}, bf16[80,2048]{1,0:T(8,128)(2,1)S(1)}, u32[]{:S(2)}, u32[]{:S(2)}) %collective-permute-start.34) | collective-permute-done | bytes 327712 | tf_op jit(solution)/shard_map/ppermute | solution.py:17
  273.9 4.1 %collective-permute-done.37 = bf16[80,2048]{1,0:T(8,128)(2,1)S(1)} collective-permute-done((bf16[80,2048]{1,0:T(8,128)(2,1)}, bf16[80,2048]{1,0:T(8,128)(2,1)S(1)}, u32[]{:S(2)}, u32[]{:S(2)}) %collective-permute-start.37) | collective-permute-done | bytes 327712 | tf_op jit(solution)/shard_map/ppermute | solution.py:17
  278.8 2.7 collective-permute-done.29.refs_1_
  282.5 2.2 collective-permute-start.38
  284.7 4.7 %collective-permute-done.33.refs_4_ = bf16[80,2048]{1,0:T(8,128)(2,1)S(1)} collective-permute-done((bf16[80,2048]{1,0:T(8,128)(2,1)}, bf16[80,2048]{1,0:T(8,128)(2,1)S(1)}, u32[]{:S(2)}, u32[]{:S(2)}) %collective-permute-start.33) | collective-permute-done | bytes 327712 | tf_op jit(solution)/shard_map/ppermute | solution.py:17
  291.5 20.7 %collective-permute-start.45 = (bf16[64,2048]{1,0:T(8,128)(2,1)}, bf16[64,2048]{1,0:T(8,128)(2,1)S(1)}, u32[]{:S(2)}, u32[]{:S(2)}) collective-permute-start(bf16[64,2048]{1,0:T(8,128)(2,1)} %get-tuple-element.65), channel_id=1, source_target_pairs={{0,16},{4,20},{8,24},{12,28},{16,0},{20,4},{24,8},{28,12},{1,17},{... | collective-permute-start | bytes 786440 | tf_op jit(solution)/shard_map/ppermute | solution.py:17
  312.1 9.7 %collective-permute-done.35.refs_5_ = bf16[80,2048]{1,0:T(8,128)(2,1)S(1)} collective-permute-done((bf16[80,2048]{1,0:T(8,128)(2,1)S(1)}, bf16[80,2048]{1,0:T(8,128)(2,1)S(1)}, u32[]{:S(2)}, u32[]{:S(2)}) %collective-permute-start.35) | collective-permute-done | bytes 327712 | tf_op jit(solution)/shard_map/ppermute | solution.py:17
  321.8 2.0 collective-permute-start.46
  323.7 8.4 %collective-permute-start.48 = (bf16[64,2048]{1,0:T(8,128)(2,1)}, bf16[64,2048]{1,0:T(8,128)(2,1)S(1)}, u32[]{:S(2)}, u32[]{:S(2)}) collective-permute-start(bf16[64,2048]{1,0:T(8,128)(2,1)} %collective-permute-done.47), channel_id=1, source_target_pairs={{0,8},{4,12},{8,0},{12,4},{16,24},{20,28},{24,16},{28,20},{1,9},{5... | collective-permute-start | bytes 786440 | tf_op jit(solution)/shard_map/ppermute | solution.py:17
  332.2 1.7 shard_map.106
  335.3 4.2 %shard_map.103 = (bf16[2,8,64,2048]{3,2,1,0:T(8,128)(2,1)}, bf16[2,8,32,512]{3,2,1,0:T(8,128)(2,1)}) custom-call(s32[2]{0:T(128)} %pad_add_fusion.place_ref, bf16[80,2048]{1,0:T(8,128)(2,1)} %get-tuple-element.51.refs_0_, bf16[80,2048]{1,0:T(8,128)(2,1)} %copy-done.8, bf16[80,2048]{1,0:T(8,128)(2,1)} %copy-done.9, bf16[80,2048]{1,0:T(8,128)(2,1)} %copy-done.12, ...), custom_call_target="tpu_custom_call" | custom-call | tf_op jit(solution)/shard_map/pallas_call | solution.py:75
  340.3 1.9 collective-permute-start.52
  343.5 3.1 shard_map.105
  348.1 10.9 %collective-permute-done.50 = bf16[64,2048]{1,0:T(8,128)(2,1)S(1)} collective-permute-done((bf16[64,2048]{1,0:T(8,128)(2,1)}, bf16[64,2048]{1,0:T(8,128)(2,1)S(1)}, u32[]{:S(2)}, u32[]{:S(2)}) %collective-permute-start.50) | collective-permute-done | bytes 262176 | tf_op jit(solution)/shard_map/ppermute | solution.py:17
  (176 shorter events, 45.5 us)
Async XLA Ops:
  5.4 70.8 %collective-permute-start.6 = (bf16[512,1024]{1,0:T(8,128)(2,1)}, bf16[512,1024]{1,0:T(8,128)(2,1)S(1)}, u32[]{:S(2)}, u32[]{:S(2)}) collective-permute-start(bf16[512,1024]{1,0:T(8,128)(2,1)} %get-tuple-element.37), channel_id=1, source_target_pairs={{0,1},{1,0},{2,3},{3,2},{4,5},{5,4},{6,7},{7,6},{8,9},{9,8},{10,11... | collective-permute-start | bytes 3145736 | tf_op jit(solution)/shard_map/ppermute | solution.py:17
  5.9 70.2 %collective-permute-start.7 = (bf16[512,1024]{1,0:T(8,128)(2,1)}, bf16[512,1024]{1,0:T(8,128)(2,1)S(1)}, u32[]{:S(2)}, u32[]{:S(2)}) collective-permute-start(bf16[512,1024]{1,0:T(8,128)(2,1)} %get-tuple-element.38), channel_id=1, source_target_pairs={{0,3},{1,2},{2,1},{3,0},{4,7},{5,6},{6,5},{7,4},{8,11},{9,10},{10,... | collective-permute-start | bytes 3145736 | tf_op jit(solution)/shard_map/ppermute | solution.py:17
  8.6 78.1 %collective-permute-start.8 = (bf16[512,1024]{1,0:T(8,128)(2,1)}, bf16[512,1024]{1,0:T(8,128)(2,1)}, u32[]{:S(2)}, u32[]{:S(2)}) collective-permute-start(bf16[512,1024]{1,0:T(8,128)(2,1)} %get-tuple-element.39), channel_id=1, source_target_pairs={{0,2},{1,3},{2,0},{3,1},{4,6},{5,7},{6,4},{7,5},{8,10},{9,11},{10,... | collective-permute-start | bytes 3145736 | tf_op jit(solution)/shard_map/ppermute | solution.py:17
  9.8 48.0 %collective-permute-start.1 = (bf16[256,256]{1,0:T(8,128)(2,1)S(1)}, bf16[256,256]{1,0:T(8,128)(2,1)S(1)}, u32[]{:S(2)}, u32[]{:S(2)}) collective-permute-start(bf16[256,256]{1,0:T(8,128)(2,1)S(1)} %gather_fusion), channel_id=1, source_target_pairs={{0,2},{1,3},{2,0},{3,1},{4,6},{5,7},{6,4},{7,5},{8,10},{9,11},{10,... | collective-permute-start | bytes 393224 | tf_op jit(solution)/shard_map/ppermute | solution.py:17
  11.8 47.6 %collective-permute-start = (bf16[256,256]{1,0:T(8,128)(2,1)S(1)}, bf16[256,256]{1,0:T(8,128)(2,1)S(1)}, u32[]{:S(2)}, u32[]{:S(2)}) collective-permute-start(bf16[256,256]{1,0:T(8,128)(2,1)S(1)} %gather_fusion), channel_id=1, source_target_pairs={{0,1},{1,0},{2,3},{3,2},{4,5},{5,4},{6,7},{7,6},{8,9},{9,8},{10,11... | collective-permute-start | bytes 393224 | tf_op jit(solution)/shard_map/ppermute | solution.py:17
  67.8 18.8 %collective-permute-start.9 = (bf16[10,512]{1,0:T(8,128)(2,1)S(1)}, bf16[10,512]{1,0:T(8,128)(2,1)S(1)}, u32[]{:S(2)}, u32[]{:S(2)}) collective-permute-start(bf16[10,512]{1,0:T(8,128)(2,1)S(1)} %bitcast.42), channel_id=1, source_target_pairs={{0,2},{1,3},{2,0},{3,1},{4,6},{5,7},{6,4},{7,5},{8,10},{9,11},{10,... | collective-permute-start | bytes 30728 | tf_op jit(solution)/shard_map/ppermute | solution.py:17
  93.0 11.0 %collective-permute-start.11 = (f32[10,256]{1,0:T(8,128)}, f32[10,256]{1,0:T(8,128)S(1)}, u32[]{:S(2)}, u32[]{:S(2)}) collective-permute-start(f32[10,256]{1,0:T(8,128)} %get-tuple-element.42), channel_id=1, source_target_pairs={{0,2},{1,3},{2,0},{3,1},{4,6},{5,7},{6,4},{7,5},{8,10},{9,11},{10,... | collective-permute-start | bytes 30728 | tf_op jit(solution)/shard_map/ppermute | solution.py:17
  93.7 10.8 %collective-permute-start.12 = (f32[10,256]{1,0:T(8,128)}, f32[10,256]{1,0:T(8,128)S(1)}, u32[]{:S(2)}, u32[]{:S(2)}) collective-permute-start(f32[10,256]{1,0:T(8,128)} %get-tuple-element.43), channel_id=1, source_target_pairs={{0,3},{1,2},{2,1},{3,0},{4,7},{5,6},{6,5},{7,4},{8,11},{9,10},{10,... | collective-permute-start | bytes 30728 | tf_op jit(solution)/shard_map/ppermute | solution.py:17
  100.3 54.3 %collective-permute-start.21 = (bf16[144,2048]{1,0:T(8,128)(2,1)}, bf16[144,2048]{1,0:T(8,128)(2,1)}, u32[]{:S(2)}, u32[]{:S(2)}) collective-permute-start(bf16[144,2048]{1,0:T(8,128)(2,1)} %get-tuple-element.47), channel_id=1, source_target_pairs={{0,4},{4,0},{8,12},{12,8},{16,20},{20,16},{24,28},{28,24},{1,5},{5... | collective-permute-start | bytes 1769480 | tf_op jit(solution)/shard_map/ppermute | solution.py:17
  101.9 20.5 %collective-permute-start.39 = (bf16[64,2048]{1,0:T(8,128)(2,1)}, bf16[64,2048]{1,0:T(8,128)(2,1)S(1)}, u32[]{:S(2)}, u32[]{:S(2)}) collective-permute-start(bf16[64,2048]{1,0:T(8,128)(2,1)} %get-tuple-element.60), channel_id=1, source_target_pairs={{0,4},{4,0},{8,12},{12,8},{16,20},{20,16},{24,28},{28,24},{1,5},{5... | collective-permute-start | bytes 786440 | tf_op jit(solution)/shard_map/ppermute | solution.py:17
  102.4 25.6 %collective-permute-start.41 = (bf16[64,2048]{1,0:T(8,128)(2,1)}, bf16[64,2048]{1,0:T(8,128)(2,1)S(1)}, u32[]{:S(2)}, u32[]{:S(2)}) collective-permute-start(bf16[64,2048]{1,0:T(8,128)(2,1)} %get-tuple-element.61), channel_id=1, source_target_pairs={{0,4},{4,0},{8,12},{12,8},{16,20},{20,16},{24,28},{28,24},{1,5},{5... | collective-permute-start | bytes 786440 | tf_op jit(solution)/shard_map/ppermute | solution.py:17
  103.9 41.7 %collective-permute-start.24 = (bf16[80,2048]{1,0:T(8,128)(2,1)}, bf16[80,2048]{1,0:T(8,128)(2,1)}, u32[]{:S(2)}, u32[]{:S(2)}) collective-permute-start(bf16[80,2048]{1,0:T(8,128)(2,1)} %get-tuple-element.48), channel_id=1, source_target_pairs={{0,4},{4,0},{8,12},{12,8},{16,20},{20,16},{24,28},{28,24},{1,5},{5... | collective-permute-start | bytes 983048 | tf_op jit(solution)/shard_map/ppermute | solution.py:17
  104.5 41.3 %collective-permute-start.27 = (bf16[80,2048]{1,0:T(8,128)(2,1)}, bf16[80,2048]{1,0:T(8,128)(2,1)}, u32[]{:S(2)}, u32[]{:S(2)}) collective-permute-start(bf16[80,2048]{1,0:T(8,128)(2,1)} %get-tuple-element.50), channel_id=1, source_target_pairs={{0,4},{4,0},{8,12},{12,8},{16,20},{20,16},{24,28},{28,24},{1,5},{5... | collective-permute-start | bytes 983048 | tf_op jit(solution)/shard_map/ppermute | solution.py:17
  122.4 19.6 %collective-permute-start.13 = (f32[20,256]{1,0:T(8,128)S(1)}, f32[20,256]{1,0:T(8,128)S(1)}, u32[]{:S(2)}, u32[]{:S(2)}) collective-permute-start(f32[20,256]{1,0:T(8,128)S(1)} %pad_maximum_fusion.3.refs_0_), channel_id=1, source_target_pairs={{0,4},{4,0},{8,12},{12,8},{16,20},{20,16},{24,28},{28,24},{1,5},{5... | collective-permute-start | bytes 61448 | tf_op jit(solution)/shard_map/ppermute | solution.py:17
  128.1 18.4 %collective-permute-start.40 = (bf16[64,2048]{1,0:T(8,128)(2,1)S(1)}, bf16[64,2048]{1,0:T(8,128)(2,1)}, u32[]{:S(2)}, u32[]{:S(2)}) collective-permute-start(bf16[64,2048]{1,0:T(8,128)(2,1)S(1)} %collective-permute-done.39), channel_id=1, source_target_pairs={{0,16},{4,20},{8,24},{12,28},{16,0},{20,4},{24,8},{28,12},{1,17},{... | collective-permute-start | bytes 786440 | tf_op jit(solution)/shard_map/ppermute | solution.py:17
  142.0 11.1 %collective-permute-start.42 = (bf16[64,2048]{1,0:T(8,128)(2,1)S(1)}, bf16[64,2048]{1,0:T(8,128)(2,1)}, u32[]{:S(2)}, u32[]{:S(2)}) collective-permute-start(bf16[64,2048]{1,0:T(8,128)(2,1)S(1)} %collective-permute-done.41), channel_id=1, source_target_pairs={{0,24},{4,28},{8,16},{12,20},{16,8},{20,12},{24,0},{28,4},{1,25},{... | collective-permute-start | bytes 786440 | tf_op jit(solution)/shard_map/ppermute | solution.py:17
  145.7 18.4 %collective-permute-start.14 = (f32[40,256]{1,0:T(8,128)S(1)}, f32[40,256]{1,0:T(8,128)S(1)}, u32[]{:S(2)}, u32[]{:S(2)}) collective-permute-start(f32[40,256]{1,0:T(8,128)S(1)} %pad_maximum_fusion.1), channel_id=1, source_target_pairs={{0,8},{4,12},{8,0},{12,4},{16,24},{20,28},{24,16},{28,20},{1,9},{5... | collective-permute-start | bytes 122888 | tf_op jit(solution)/shard_map/ppermute | solution.py:17
  145.7 20.9 %collective-permute-start.15 = (f32[40,256]{1,0:T(8,128)S(1)}, f32[40,256]{1,0:T(8,128)S(1)}, u32[]{:S(2)}, u32[]{:S(2)}) collective-permute-start(f32[40,256]{1,0:T(8,128)S(1)} %pad_maximum_fusion.1), channel_id=1, source_target_pairs={{0,16},{4,20},{8,24},{12,28},{16,0},{20,4},{24,8},{28,12},{1,17},{... | collective-permute-start | bytes 122888 | tf_op jit(solution)/shard_map/ppermute | solution.py:17
  146.5 20.1 %collective-permute-start.16 = (f32[40,256]{1,0:T(8,128)S(1)}, f32[40,256]{1,0:T(8,128)S(1)}, u32[]{:S(2)}, u32[]{:S(2)}) collective-permute-start(f32[40,256]{1,0:T(8,128)S(1)} %pad_maximum_fusion.1), channel_id=1, source_target_pairs={{0,24},{4,28},{8,16},{12,20},{16,8},{20,12},{24,0},{28,4},{1,25},{... | collective-permute-start | bytes 122888 | tf_op jit(solution)/shard_map/ppermute | solution.py:17
  153.1 19.9 %collective-permute-start.19 = (bf16[144,2048]{1,0:T(8,128)(2,1)}, bf16[144,2048]{1,0:T(8,128)(2,1)}, u32[]{:S(2)}, u32[]{:S(2)}) collective-permute-start(bf16[144,2048]{1,0:T(8,128)(2,1)} %get-tuple-element.45), channel_id=1, source_target_pairs={{0,4},{4,0},{8,12},{12,8},{16,20},{20,16},{24,28},{28,24},{1,5},{5... | collective-permute-start | bytes 1769480 | tf_op jit(solution)/shard_map/ppermute | solution.py:17
  154.6 32.0 %collective-permute-start.20 = (bf16[144,2048]{1,0:T(8,128)(2,1)}, bf16[144,2048]{1,0:T(8,128)(2,1)}, u32[]{:S(2)}, u32[]{:S(2)}) collective-permute-start(bf16[144,2048]{1,0:T(8,128)(2,1)} %get-tuple-element.46), channel_id=1, source_target_pairs={{0,8},{4,12},{8,0},{12,4},{16,24},{20,28},{24,16},{28,20},{1,9},{5... | collective-permute-start | bytes 1769480 | tf_op jit(solution)/shard_map/ppermute | solution.py:17
  164.1 30.2 %collective-permute-start.26 = (bf16[144,2048]{1,0:T(8,128)(2,1)}, bf16[144,2048]{1,0:T(8,128)(2,1)}, u32[]{:S(2)}, u32[]{:S(2)}) collective-permute-start(bf16[144,2048]{1,0:T(8,128)(2,1)} %get-tuple-element.49), channel_id=1, source_target_pairs={{0,24},{4,28},{8,16},{12,20},{16,8},{20,12},{24,0},{28,4},{1,25},{... | collective-permute-start | bytes 1769480 | tf_op jit(solution)/shard_map/ppermute | solution.py:17
  166.6 65.9 %collective-permute-start.23 = (bf16[144,2048]{1,0:T(8,128)(2,1)}, bf16[144,2048]{1,0:T(8,128)(2,1)}, u32[]{:S(2)}, u32[]{:S(2)}) collective-permute-start(bf16[144,2048]{1,0:T(8,128)(2,1)} %shard_map.101), channel_id=1, source_target_pairs={{0,16},{4,20},{8,24},{12,28},{16,0},{20,4},{24,8},{28,12},{1,17},{... | collective-permute-start | bytes 1769480 | tf_op jit(solution)/shard_map/ppermute | solution.py:17
  166.6 65.9 %collective-permute-start.22 = (bf16[144,2048]{1,0:T(8,128)(2,1)}, bf16[144,2048]{1,0:T(8,128)(2,1)}, u32[]{:S(2)}, u32[]{:S(2)}) collective-permute-start(bf16[144,2048]{1,0:T(8,128)(2,1)} %collective-permute-done.21), channel_id=1, source_target_pairs={{0,8},{4,12},{8,0},{12,4},{16,24},{20,28},{24,16},{28,20},{1,9},{5... | collective-permute-start | bytes 1769480 | tf_op jit(solution)/shard_map/ppermute | solution.py:17
  174.4 63.6 %collective-permute-start.53 = (bf16[20,512]{1,0:T(8,128)(2,1)S(1)}, bf16[20,512]{1,0:T(8,128)(2,1)S(1)}, u32[]{:S(2)}, u32[]{:S(2)}) collective-permute-start(bf16[20,512]{1,0:T(8,128)(2,1)S(1)} %reshape.43.refs_0_), channel_id=1, source_target_pairs={{0,4},{4,0},{8,12},{12,8},{16,20},{20,16},{24,28},{28,24},{1,5},{5... | collective-permute-start | bytes 61448 | tf_op jit(solution)/shard_map/ppermute | solution.py:17
  190.3 57.3 %collective-permute-start.25 = (bf16[80,2048]{1,0:T(8,128)(2,1)}, bf16[80,2048]{1,0:T(8,128)(2,1)}, u32[]{:S(2)}, u32[]{:S(2)}) collective-permute-start(bf16[80,2048]{1,0:T(8,128)(2,1)} %collective-permute-done.24), channel_id=1, source_target_pairs={{0,16},{4,20},{8,24},{12,28},{16,0},{20,4},{24,8},{28,12},{1,17},{... | collective-permute-start | bytes 983048 | tf_op jit(solution)/shard_map/ppermute | solution.py:17
  194.3 54.8 %collective-permute-start.28 = (bf16[80,2048]{1,0:T(8,128)(2,1)}, bf16[80,2048]{1,0:T(8,128)(2,1)}, u32[]{:S(2)}, u32[]{:S(2)}) collective-permute-start(bf16[80,2048]{1,0:T(8,128)(2,1)} %collective-permute-done.27), channel_id=1, source_target_pairs={{0,24},{4,28},{8,16},{12,20},{16,8},{20,12},{24,0},{28,4},{1,25},{... | collective-permute-start | bytes 983048 | tf_op jit(solution)/shard_map/ppermute | solution.py:17
  237.5 19.3 %collective-permute-start.43 = (bf16[64,2048]{1,0:T(8,128)(2,1)}, bf16[64,2048]{1,0:T(8,128)(2,1)}, u32[]{:S(2)}, u32[]{:S(2)}) collective-permute-start(bf16[64,2048]{1,0:T(8,128)(2,1)} %get-tuple-element.63), channel_id=1, source_target_pairs={{0,4},{4,0},{8,12},{12,8},{16,20},{20,16},{24,28},{28,24},{1,5},{5... | collective-permute-start | bytes 786440 | tf_op jit(solution)/shard_map/ppermute | solution.py:17
  238.0 19.3 %collective-permute-start.44 = (bf16[64,2048]{1,0:T(8,128)(2,1)}, bf16[64,2048]{1,0:T(8,128)(2,1)}, u32[]{:S(2)}, u32[]{:S(2)}) collective-permute-start(bf16[64,2048]{1,0:T(8,128)(2,1)} %get-tuple-element.64), channel_id=1, source_target_pairs={{0,8},{4,12},{8,0},{12,4},{16,24},{20,28},{24,16},{28,20},{1,9},{5... | collective-permute-start | bytes 786440 | tf_op jit(solution)/shard_map/ppermute | solution.py:17
  245.1 10.1 %collective-permute-start.55 = (bf16[80,512]{1,0:T(8,128)(2,1)}, bf16[80,512]{1,0:T(8,128)(2,1)S(1)}, u32[]{:S(2)}, u32[]{:S(2)}) collective-permute-start(bf16[80,512]{1,0:T(8,128)(2,1)} %pad_maximum_fusion), channel_id=1, source_target_pairs={{0,8},{4,12},{8,0},{12,4},{16,24},{20,28},{24,16},{28,20},{1,9},{5... | collective-permute-start | bytes 245768 | tf_op jit(solution)/shard_map/ppermute | solution.py:17
  247.6 11.2 %collective-permute-start.47 = (bf16[64,2048]{1,0:T(8,128)(2,1)}, bf16[64,2048]{1,0:T(8,128)(2,1)}, u32[]{:S(2)}, u32[]{:S(2)}) collective-permute-start(bf16[64,2048]{1,0:T(8,128)(2,1)} %get-tuple-element.68), channel_id=1, source_target_pairs={{0,4},{4,0},{8,12},{12,8},{16,20},{20,16},{24,28},{28,24},{1,5},{5... | collective-permute-start | bytes 786440 | tf_op jit(solution)/shard_map/ppermute | solution.py:17
  254.7 10.9 %collective-permute-start.31 = (bf16[80,2048]{1,0:T(8,128)(2,1)}, bf16[80,2048]{1,0:T(8,128)(2,1)S(1)}, u32[]{:S(2)}, u32[]{:S(2)}) collective-permute-start(bf16[80,2048]{1,0:T(8,128)(2,1)} %get-tuple-element.54), channel_id=1, source_target_pairs={{0,4},{4,0},{8,12},{12,8},{16,20},{20,16},{24,28},{28,24},{1,5},{5... | collective-permute-start | bytes 983048 | tf_op jit(solution)/shard_map/ppermute | solution.py:17
  255.3 17.3 %collective-permute-start.34 = (bf16[80,2048]{1,0:T(8,128)(2,1)}, bf16[80,2048]{1,0:T(8,128)(2,1)S(1)}, u32[]{:S(2)}, u32[]{:S(2)}) collective-permute-start(bf16[80,2048]{1,0:T(8,128)(2,1)} %get-tuple-element.56), channel_id=1, source_target_pairs={{0,4},{4,0},{8,12},{12,8},{16,20},{20,16},{24,28},{28,24},{1,5},{5... | collective-permute-start | bytes 983048 | tf_op jit(solution)/shard_map/ppermute | solution.py:17
  256.8 21.2 %collective-permute-start.37 = (bf16[80,2048]{1,0:T(8,128)(2,1)}, bf16[80,2048]{1,0:T(8,128)(2,1)S(1)}, u32[]{:S(2)}, u32[]{:S(2)}) collective-permute-start(bf16[80,2048]{1,0:T(8,128)(2,1)} %get-tuple-element.58), channel_id=1, source_target_pairs={{0,4},{4,0},{8,12},{12,8},{16,20},{20,16},{24,28},{28,24},{1,5},{5... | collective-permute-start | bytes 983048 | tf_op jit(solution)/shard_map/ppermute | solution.py:17
  257.3 24.2 %collective-permute-start.29 = (bf16[80,2048]{1,0:T(8,128)(2,1)}, bf16[80,2048]{1,0:T(8,128)(2,1)S(1)}, u32[]{:S(2)}, u32[]{:S(2)}) collective-permute-start(bf16[80,2048]{1,0:T(8,128)(2,1)} %get-tuple-element.52), channel_id=1, source_target_pairs={{0,4},{4,0},{8,12},{12,8},{16,20},{20,16},{24,28},{28,24},{1,5},{5... | collective-permute-start | bytes 983048 | tf_op jit(solution)/shard_map/ppermute | solution.py:17
  258.8 23.6 %collective-permute-start.30 = (bf16[80,2048]{1,0:T(8,128)(2,1)}, bf16[80,2048]{1,0:T(8,128)(2,1)S(1)}, u32[]{:S(2)}, u32[]{:S(2)}) collective-permute-start(bf16[80,2048]{1,0:T(8,128)(2,1)} %get-tuple-element.53), channel_id=1, source_target_pairs={{0,8},{4,12},{8,0},{12,4},{16,24},{20,28},{24,16},{28,20},{1,9},{5... | collective-permute-start | bytes 983048 | tf_op jit(solution)/shard_map/ppermute | solution.py:17
  265.5 23.9 %collective-permute-start.33 = (bf16[80,2048]{1,0:T(8,128)(2,1)}, bf16[80,2048]{1,0:T(8,128)(2,1)S(1)}, u32[]{:S(2)}, u32[]{:S(2)}) collective-permute-start(bf16[80,2048]{1,0:T(8,128)(2,1)} %get-tuple-element.55), channel_id=1, source_target_pairs={{0,16},{4,20},{8,24},{12,28},{16,0},{20,4},{24,8},{28,12},{1,17},{... | collective-permute-start | bytes 983048 | tf_op jit(solution)/shard_map/ppermute | solution.py:17
  272.6 18.3 %collective-permute-start.36 = (bf16[80,2048]{1,0:T(8,128)(2,1)}, bf16[80,2048]{1,0:T(8,128)(2,1)S(1)}, u32[]{:S(2)}, u32[]{:S(2)}) collective-permute-start(bf16[80,2048]{1,0:T(8,128)(2,1)} %get-tuple-element.57), channel_id=1, source_target_pairs={{0,24},{4,28},{8,16},{12,20},{16,8},{20,12},{24,0},{28,4},{1,25},{... | collective-permute-start | bytes 983048 | tf_op jit(solution)/shard_map/ppermute | solution.py:17
  278.0 13.5 %collective-permute-start.32 = (bf16[80,2048]{1,0:T(8,128)(2,1)S(1)}, bf16[80,2048]{1,0:T(8,128)(2,1)S(1)}, u32[]{:S(2)}, u32[]{:S(2)}) collective-permute-start(bf16[80,2048]{1,0:T(8,128)(2,1)S(1)} %collective-permute-done.31), channel_id=1, source_target_pairs={{0,8},{4,12},{8,0},{12,4},{16,24},{20,28},{24,16},{28,20},{1,9},{5... | collective-permute-start | bytes 983048 | tf_op jit(solution)/shard_map/ppermute | solution.py:17
  281.5 40.3 %collective-permute-start.35 = (bf16[80,2048]{1,0:T(8,128)(2,1)S(1)}, bf16[80,2048]{1,0:T(8,128)(2,1)S(1)}, u32[]{:S(2)}, u32[]{:S(2)}) collective-permute-start(bf16[80,2048]{1,0:T(8,128)(2,1)S(1)} %collective-permute-done.34), channel_id=1, source_target_pairs={{0,16},{4,20},{8,24},{12,28},{16,0},{20,4},{24,8},{28,12},{1,17},{... | collective-permute-start | bytes 983048 | tf_op jit(solution)/shard_map/ppermute | solution.py:17
  282.5 41.3 %collective-permute-start.38 = (bf16[80,2048]{1,0:T(8,128)(2,1)S(1)}, bf16[80,2048]{1,0:T(8,128)(2,1)S(1)}, u32[]{:S(2)}, u32[]{:S(2)}) collective-permute-start(bf16[80,2048]{1,0:T(8,128)(2,1)S(1)} %collective-permute-done.37), channel_id=1, source_target_pairs={{0,24},{4,28},{8,16},{12,20},{16,8},{20,12},{24,0},{28,4},{1,25},{... | collective-permute-start | bytes 983048 | tf_op jit(solution)/shard_map/ppermute | solution.py:17
  289.4 50.1 %collective-permute-start.49 = (bf16[64,2048]{1,0:T(8,128)(2,1)}, bf16[64,2048]{1,0:T(8,128)(2,1)}, u32[]{:S(2)}, u32[]{:S(2)}) collective-permute-start(bf16[64,2048]{1,0:T(8,128)(2,1)} %get-tuple-element.69), channel_id=1, source_target_pairs={{0,4},{4,0},{8,12},{12,8},{16,20},{20,16},{24,28},{28,24},{1,5},{5... | collective-permute-start | bytes 786440 | tf_op jit(solution)/shard_map/ppermute | solution.py:17
  290.9 49.4 %collective-permute-start.51 = (bf16[64,2048]{1,0:T(8,128)(2,1)}, bf16[64,2048]{1,0:T(8,128)(2,1)}, u32[]{:S(2)}, u32[]{:S(2)}) collective-permute-start(bf16[64,2048]{1,0:T(8,128)(2,1)} %get-tuple-element.70), channel_id=1, source_target_pairs={{0,4},{4,0},{8,12},{12,8},{16,20},{20,16},{24,28},{28,24},{1,5},{5... | collective-permute-start | bytes 786440 | tf_op jit(solution)/shard_map/ppermute | solution.py:17
  291.5 51.4 %collective-permute-start.45 = (bf16[64,2048]{1,0:T(8,128)(2,1)}, bf16[64,2048]{1,0:T(8,128)(2,1)S(1)}, u32[]{:S(2)}, u32[]{:S(2)}) collective-permute-start(bf16[64,2048]{1,0:T(8,128)(2,1)} %get-tuple-element.65), channel_id=1, source_target_pairs={{0,16},{4,20},{8,24},{12,28},{16,0},{20,4},{24,8},{28,12},{1,17},{... | collective-permute-start | bytes 786440 | tf_op jit(solution)/shard_map/ppermute | solution.py:17
  321.8 24.9 %collective-permute-start.46 = (bf16[64,2048]{1,0:T(8,128)(2,1)}, bf16[64,2048]{1,0:T(8,128)(2,1)S(1)}, u32[]{:S(2)}, u32[]{:S(2)}) collective-permute-start(bf16[64,2048]{1,0:T(8,128)(2,1)} %get-tuple-element.67), channel_id=1, source_target_pairs={{0,24},{4,28},{8,16},{12,20},{16,8},{20,12},{24,0},{28,4},{1,25},{... | collective-permute-start | bytes 786440 | tf_op jit(solution)/shard_map/ppermute | solution.py:17
  323.7 23.7 %collective-permute-start.48 = (bf16[64,2048]{1,0:T(8,128)(2,1)}, bf16[64,2048]{1,0:T(8,128)(2,1)S(1)}, u32[]{:S(2)}, u32[]{:S(2)}) collective-permute-start(bf16[64,2048]{1,0:T(8,128)(2,1)} %collective-permute-done.47), channel_id=1, source_target_pairs={{0,8},{4,12},{8,0},{12,4},{16,24},{20,28},{24,16},{28,20},{1,9},{5... | collective-permute-start | bytes 786440 | tf_op jit(solution)/shard_map/ppermute | solution.py:17
  339.6 19.5 %collective-permute-start.50 = (bf16[64,2048]{1,0:T(8,128)(2,1)}, bf16[64,2048]{1,0:T(8,128)(2,1)S(1)}, u32[]{:S(2)}, u32[]{:S(2)}) collective-permute-start(bf16[64,2048]{1,0:T(8,128)(2,1)} %collective-permute-done.49), channel_id=1, source_target_pairs={{0,16},{4,20},{8,24},{12,28},{16,0},{20,4},{24,8},{28,12},{1,17},{... | collective-permute-start | bytes 786440 | tf_op jit(solution)/shard_map/ppermute | solution.py:17
  340.3 19.5 %collective-permute-start.52 = (bf16[64,2048]{1,0:T(8,128)(2,1)}, bf16[64,2048]{1,0:T(8,128)(2,1)S(1)}, u32[]{:S(2)}, u32[]{:S(2)}) collective-permute-start(bf16[64,2048]{1,0:T(8,128)(2,1)} %collective-permute-done.51), channel_id=1, source_target_pairs={{0,24},{4,28},{8,16},{12,20},{16,8},{20,12},{24,0},{28,4},{1,25},{... | collective-permute-start | bytes 786440 | tf_op jit(solution)/shard_map/ppermute | solution.py:17
  (45 other events, 1115.0 us)
